TPU v7x, 128 devices: a whole 4x4x4 slice. The times are simulated.
128 devices in a mesh: ep: 32 (over z, y, core), sp: 4 (over x).
Axes of the slice: x: 4, y: 4, z: 4, core: 2. Of those that a mesh axis runs over, the one named last changes fastest.
Arguments:
- hidden_in: bfloat16 [16384, 6656], P(('ep', 'sp')), may hold values from -6 to 6
- grad_out: bfloat16 [16384, 6656], P(('ep', 'sp')), may hold values from -6 to 6
- route_ids: int32 [16384, 8], P(('ep', 'sp')), may hold values from 0 to 255, all different within a row; in each aligned block of 128 rows (0 to 127, 128 to 255, ...) at most 6 rows name the same one
- route_probs: float32 [16384, 8], P(('ep', 'sp')), may hold values from 0.05 to 0.6
- w_gate: bfloat16 [32, 6656, 1024], P('ep', 'sp'), may hold values from -0.078125 to 0.078125
- w_up: bfloat16 [32, 6656, 1024], P('ep', 'sp'), may hold values from -0.078125 to 0.078125
- w_down: bfloat16 [32, 1024, 6656], P('ep', None, 'sp'), may hold values from -0.1875 to 0.1875
Outputs:
- grad_in: bfloat16 [16384, 6656], P(('ep', 'sp'))
- grad_w_gate: bfloat16 [32, 6656, 1024], P('ep', 'sp')
- grad_w_up: bfloat16 [32, 6656, 1024], P('ep', 'sp')
- grad_w_down: bfloat16 [32, 1024, 6656], P('ep', None, 'sp')
- grad_probs: bfloat16 [16384, 8], P(('ep', 'sp'))
Inputs may be any that keep to these rules, and one draw needn't show every extreme that they name: `route_ids`: each row names 8 different routed experts; only those below 32 belong to the window. In each aligned block of 128 rows (the rows of one device) no routed expert is named by more than 6 rows, a bound that some block reaches.
All inputs are finite; a program needn't handle non-finite values.
Results may differ from a plain program's by a relative error of at most 0.03.
Values may be sent and summed in bfloat16 or wider, within the bound.
No kernel may reach another device: no remote copies, remote signals or barrier semaphores. Data moves between devices by JAX's collectives and lax.ppermute only.
A program may use at most 128 MiB of HBM per device.

v0:
```python
import jax
import jax.numpy as jnp
from jax import lax
from jax.sharding import PartitionSpec as P

CAP = 6


def activate_rows(summed, slot_weights):
    hidden_width = summed.shape[1] // 3
    gate_sum = summed[:, :hidden_width]
    up_sum = summed[:, hidden_width : 2 * hidden_width]
    back_sum = summed[:, 2 * hidden_width :]
    weight = slot_weights[:, None]
    sigmoid_gate = jax.nn.sigmoid(gate_sum)
    activation = gate_sum * sigmoid_gate * up_sum
    grad_act = weight * back_sum
    grad_gate = (grad_act * up_sum * sigmoid_gate * (1.0 + gate_sum * (1.0 - sigmoid_gate))).astype(
        jnp.bfloat16
    )
    grad_up = (grad_act * gate_sum * sigmoid_gate).astype(jnp.bfloat16)
    weighted = (weight * activation).astype(jnp.bfloat16)
    slot_prob = jnp.sum(back_sum * activation, axis=1).astype(jnp.bfloat16)
    return (weighted, grad_gate, grad_up, slot_prob)


def on_device(hidden_in, grad_out, route_ids, route_probs, w_gate, w_up, w_down):
    ep_count = lax.axis_size("ep")
    sp_count = lax.axis_size("sp")
    tok_rows = hidden_in.shape[0]
    model_width = hidden_in.shape[1]
    route_count = route_ids.shape[1]
    quarter = model_width // sp_count
    experts = ep_count * w_gate.shape[0]
    flat_ids = route_ids.reshape(-1)
    inside = flat_ids < experts
    onehot = (flat_ids[:, None] == jnp.arange(experts, dtype=jnp.int32)[None, :]).astype(jnp.int32)
    slot_rank = jnp.sum((jnp.cumsum(onehot, axis=0) - onehot) * onehot, axis=1)
    slot_index = jnp.where(inside, flat_ids * CAP + slot_rank, experts * CAP)
    token_ids = jnp.arange(tok_rows * route_count, dtype=jnp.int32) // route_count
    source_rows = (
        jnp.full((experts * CAP + 1,), tok_rows, jnp.int32).at[slot_index].set(token_ids)[:-1]
    )
    source_rows = source_rows.reshape(experts, 1, CAP)
    slot_probs = (
        jnp.zeros((experts * CAP + 1,), jnp.float32)
        .at[slot_index]
        .set(route_probs.reshape(-1))[:-1]
    )
    slot_probs = slot_probs.astype(jnp.bfloat16).reshape(experts, 1, CAP)
    lane_ids = jnp.arange(sp_count, dtype=jnp.int32)[None, :, None]
    spread_index = (source_rows * sp_count + lane_ids).reshape(-1)

    def spread(matrix):
        padded = jnp.concatenate([matrix, jnp.zeros((1, model_width), matrix.dtype)], axis=0)
        flat_rows = padded.reshape((tok_rows + 1) * sp_count, quarter)
        return jnp.take(flat_rows, spread_index, axis=0).reshape(experts, sp_count, CAP, quarter)

    x_send = spread(hidden_in)
    dy_send = spread(grad_out)
    p_send = jnp.broadcast_to(slot_probs, (experts, sp_count, CAP))
    x_recv, dy_recv, p_recv = (
        lax.all_to_all(
            x_send.reshape(experts * sp_count, CAP, quarter),
            ("ep", "sp"),
            split_axis=0,
            concat_axis=0,
            tiled=True,
        ),
        lax.all_to_all(
            dy_send.reshape(experts * sp_count, CAP, quarter),
            ("ep", "sp"),
            split_axis=0,
            concat_axis=0,
            tiled=True,
        ),
        lax.all_to_all(
            p_send.reshape(experts * sp_count, CAP),
            ("ep", "sp"),
            split_axis=0,
            concat_axis=0,
            tiled=True,
        ),
    )
    row_count = ep_count * sp_count * CAP
    x_rows = x_recv.reshape(row_count, quarter)
    dy_rows = dy_recv.reshape(row_count, quarter)
    p_rows = p_recv.reshape(row_count).astype(jnp.float32)
    gate_weight = w_gate[0]
    up_weight = w_up[0]
    down_weight = w_down[0]
    gate_part = jnp.dot(x_rows, gate_weight, preferred_element_type=jnp.float32)
    up_part = jnp.dot(x_rows, up_weight, preferred_element_type=jnp.float32)
    back_part = lax.dot_general(
        dy_rows, down_weight, (((1,), (1,)), ((), ())), preferred_element_type=jnp.float32
    )
    summed = lax.psum(
        jnp.concatenate([gate_part, up_part, back_part], axis=1).astype(jnp.bfloat16), "sp"
    ).astype(jnp.float32)
    weighted, grad_gate, grad_up, slot_prob = activate_rows(summed, p_rows)
    contract_rows = (((0,), (0,)), ((), ()))
    grad_gate_weight = lax.dot_general(
        x_rows, grad_gate, contract_rows, preferred_element_type=jnp.float32
    ).astype(jnp.bfloat16)
    grad_up_weight = lax.dot_general(
        x_rows, grad_up, contract_rows, preferred_element_type=jnp.float32
    ).astype(jnp.bfloat16)
    grad_down_weight = lax.dot_general(
        weighted, dy_rows, contract_rows, preferred_element_type=jnp.float32
    ).astype(jnp.bfloat16)
    contract_hidden = (((1,), (1,)), ((), ()))
    row_grad = lax.dot_general(
        grad_gate, gate_weight, contract_hidden, preferred_element_type=jnp.float32
    )
    row_grad = row_grad + lax.dot_general(
        grad_up, up_weight, contract_hidden, preferred_element_type=jnp.float32
    )
    row_grad = row_grad.astype(jnp.bfloat16)
    back_rows, back_probs = (
        lax.all_to_all(
            row_grad.reshape(ep_count * sp_count, CAP, quarter),
            ("ep", "sp"),
            split_axis=0,
            concat_axis=0,
            tiled=True,
        ),
        lax.all_to_all(
            slot_prob.reshape(ep_count * sp_count, CAP),
            ("ep", "sp"),
            split_axis=0,
            concat_axis=0,
            tiled=True,
        ),
    )
    back_rows = back_rows.reshape(ep_count, sp_count, CAP, quarter)
    back_probs = back_probs.reshape(ep_count, sp_count, CAP)
    keep_mask = inside.reshape(tok_rows, route_count)
    expert_of = jnp.where(inside, flat_ids, 0).reshape(tok_rows, route_count)
    rank_of = jnp.where(inside, slot_rank, 0).reshape(tok_rows, route_count)
    slot_of = jnp.where(keep_mask, expert_of * CAP + rank_of, -1)
    slot_iota = jnp.arange(ep_count * CAP, dtype=jnp.int32)[None, None, :]
    combine = jnp.sum((slot_of[:, :, None] == slot_iota).astype(jnp.float32), axis=1).astype(
        jnp.bfloat16
    )
    combine = combine.reshape(tok_rows, ep_count, CAP)
    grad_in = jnp.einsum("tec,escq->tsq", combine, back_rows, preferred_element_type=jnp.float32)
    grad_in = grad_in.reshape(tok_rows, model_width).astype(jnp.bfloat16)
    prob_index = (expert_of * (sp_count * CAP) + rank_of).reshape(-1)
    picked = jnp.take(back_probs.reshape(-1), prob_index, axis=0).reshape(tok_rows, route_count)
    grad_probs = jnp.where(keep_mask, picked, jnp.zeros_like(picked))
    return (
        grad_in,
        grad_gate_weight[None],
        grad_up_weight[None],
        grad_down_weight[None],
        grad_probs,
    )


def solution(mesh):
    placed = (
        P(("ep", "sp"), None),
        P(("ep", "sp"), None),
        P(("ep", "sp"), None),
        P(("ep", "sp"), None),
        P("ep", "sp", None),
        P("ep", "sp", None),
        P("ep", None, "sp"),
    )
    return jax.shard_map(
        on_device,
        mesh=mesh,
        in_specs=placed,
        out_specs=(
            P(("ep", "sp"), None),
            P("ep", "sp", None),
            P("ep", "sp", None),
            P("ep", None, "sp"),
            P(("ep", "sp"), None),
        ),
        check_vma=False,
    )
```

profile of v0, /device:TPU:1, one launch (start us, length us, event | category | flops | bytes accessed | tf_op | source)
XLA Modules:
  0.0 399.6 jit_solution(3451705955774551207)
XLA Ops:
  9.7 17.5 %reduce-window.6 = s32[32,8,128]{2,1,0:T(8,128)} reduce-window(s32[32,8,128]{2,1,0:T(8,128)} %fusion.26, s32[]{:T(128)} %constant.27.clone.1), window={size=1x1x128 pad=0_0x0_0x127_0}, to_apply=%region_0.0 | reduce-window | flops 4161536 | bytes 262148 | tf_op jit(solution)/shard_map/reduce-window
  34.8 4.5 %scatter_custom_fusion.1 = s32[193]{0:T(256)S(1)} fusion(s32[1024]{0:T(1024)S(1)} %bitcast.79, s32[1024]{0:T(1024)} %add_select_fusion.1, s32[]{:T(128)} %constant.40.clone.1), kind=kCustom, calls=%fused_computation.72 | custom fusion | bytes 1284 | tf_op jit(solution)/shard_map/scatter | solution.py:42
  42.4 3.9 reshape.197
  53.1 7.8 %gather_fusion.1 = bf16[768,1664]{1,0:T(8,128)(2,1)} fusion(bf16[516,1664]{1,0:T(8,128)(2,1)} %reshape.197, s32[1024]{0:T(1024)S(1)} %pad_clamp_fusion), kind=kCustom, calls=%fused_computation.clone | custom fusion | bytes 5114880 | tf_op jit(solution)/shard_map/jit(_take)/gather | solution.py:57
  60.9 7.8 %gather_fusion.2 = bf16[768,1664]{1,0:T(8,128)(2,1)} fusion(bf16[516,1664]{1,0:T(8,128)(2,1)} %reshape.199, s32[1024]{0:T(1024)S(1)} %pad_clamp_fusion), kind=kCustom, calls=%fused_computation.1.clone | custom fusion | bytes 5114880 | tf_op jit(solution)/shard_map/jit(_take)/gather | solution.py:57
  68.7 5.4 %broadcast_select_fusion.1 = (bf16[768,1664]{1,0:T(8,128)(2,1)}, bf16[768,1664]{1,0:T(8,128)(2,1)}) fusion(bf16[768,1664]{1,0:T(8,128)(2,1)} %gather_fusion.1, pred[768]{0:T(1024)(128)(4,1)S(1)} %compare_and_fusion, bf16[768,1664]{1,0:T(8,128)(2,1)} %gather_fusion.2), kind=kLoop, calls=%fused_computation.33 | loop fusion | flops 2555904 | bytes 10224384 | tf_op jit(solution)/shard_map/jit(_take)/select_n | solution.py:57
  74.1 5.3 %reshape_reshape.9 = bf16[128,6,1664]{2,1,0:T(8,128)(2,1)} reshape(bf16[768,1664]{1,0:T(8,128)(2,1)} %get-tuple-element.33) | data formatting | bytes 5111808 | tf_op jit(solution)/shard_map/reshape;reshape | solution.py:64
  79.4 11.9 %all-to-all-start.1 = ((bf16[128,6,1664]{2,1,0:T(8,128)(2,1)}), bf16[128,6,1664]{2,1,0:T(8,128)(2,1)}, u32[]{:S(2)}, u32[]{:S(2)}) async-start(bf16[128,6,1664]{2,1,0:T(8,128)(2,1)} %reshape_reshape.9), calls=%async_computation.1 | async-start | bytes 6815744 | tf_op jit(solution)/shard_map/all_to_all | solution.py:63
  91.3 5.3 %reshape_reshape.10 = bf16[128,6,1664]{2,1,0:T(8,128)(2,1)} reshape(bf16[768,1664]{1,0:T(8,128)(2,1)} %get-tuple-element.34) | data formatting | bytes 5111808 | tf_op jit(solution)/shard_map/reshape;reshape | solution.py:71
  96.6 39.3 %all-to-all-done.1 = bf16[128,6,1664]{2,1,0:T(8,128)(2,1)} async-done(((bf16[128,6,1664]{2,1,0:T(8,128)(2,1)}), bf16[128,6,1664]{2,1,0:T(8,128)(2,1)}, u32[]{:S(2)}, u32[]{:S(2)}) %all-to-all-start.1) | async-done | bytes 2555936 | tf_op jit(solution)/shard_map/all_to_all | solution.py:63
  135.9 4.9 %all-to-all-start.2 = ((bf16[128,6,1664]{2,1,0:T(8,128)(2,1)}), bf16[128,6,1664]{2,1,0:T(8,128)(2,1)}, u32[]{:S(2)}, u32[]{:S(2)}) async-start(bf16[128,6,1664]{2,1,0:T(8,128)(2,1)} %reshape_reshape.10), calls=%async_computation.2 | async-start | bytes 6815744 | tf_op jit(solution)/shard_map/all_to_all | solution.py:70
  141.0 5.3 %reshape.198 = bf16[768,1664]{1,0:T(8,128)(2,1)} reshape(bf16[128,6,1664]{2,1,0:T(8,128)(2,1)} %all-to-all-done.1) | data formatting | bytes 5111808 | tf_op jit(solution)/shard_map/reshape | solution.py:86
  146.4 7.0 %fusion.16 = bf16[768,1024]{1,0:T(8,128)(2,1)} fusion(bf16[768,1664]{1,0:T(8,128)(2,1)} %reshape.198, bf16[1,1664,1024]{2,1,0:T(8,128)(2,1)} %param.14), kind=kOutput, calls=%fused_computation.35 | convolution fusion | flops 2618032128 | bytes 7536640 | tf_op jit(solution)/shard_map/dot_general | solution.py:93
  153.4 4.1 %fusion.13 = bf16[768,1024]{1,0:T(8,128)(2,1)} fusion(bf16[768,1664]{1,0:T(8,128)(2,1)S(1)} %copy-done.3, bf16[1,1664,1024]{2,1,0:T(8,128)(2,1)S(1)} %copy-done), kind=kOutput, calls=%fused_computation.34 | convolution fusion | flops 2618032128 | bytes 7536640 | tf_op jit(solution)/shard_map/dot_general | solution.py:92
  157.5 28.0 %all-to-all-done.2 = bf16[128,6,1664]{2,1,0:T(8,128)(2,1)} async-done(((bf16[128,6,1664]{2,1,0:T(8,128)(2,1)}), bf16[128,6,1664]{2,1,0:T(8,128)(2,1)}, u32[]{:S(2)}, u32[]{:S(2)}) %all-to-all-start.2) | async-done | bytes 2555936 | tf_op jit(solution)/shard_map/all_to_all | solution.py:70
  185.5 5.3 %reshape.200 = bf16[768,1664]{1,0:T(8,128)(2,1)} reshape(bf16[128,6,1664]{2,1,0:T(8,128)(2,1)} %all-to-all-done.2) | data formatting | bytes 5111808 | tf_op jit(solution)/shard_map/reshape | solution.py:87
  190.8 5.9 %fusion.19 = bf16[768,1024]{1,0:T(8,128)(2,1)S(1)} fusion(bf16[768,1664]{1,0:T(8,128)(2,1)} %reshape.200, bf16[1,1024,1664]{2,1,0:T(8,128)(2,1)} %param.15), kind=kOutput, calls=%fused_computation.36 | convolution fusion | flops 2618032128 | bytes 7536640 | tf_op jit(solution)/shard_map/dot_general | solution.py:94
  202.1 5.0 %scatter_custom_fusion = f32[193]{0:T(256)} fusion(s32[1024]{0:T(1024)} %bitcast.80, f32[1024]{0:T(1024)} %reshape.233, f32[]{:T(128)} %constant.36.clone.1), kind=kCustom, calls=%fused_computation.74 | custom fusion | bytes 1284 | tf_op jit(solution)/shard_map/scatter | solution.py:48
  215.4 4.8 %all-to-all-start = ((bf16[128,1,6]{2,1,0:T(2,128)(2,1)}), bf16[128,1,6]{2,1,0:T(2,128)(2,1)}, u32[]{:S(2)}, u32[]{:S(2)}) async-start(bf16[128,1,6]{2,1,0:T(2,128)(2,1)} %copy.61), calls=%async_computation | async-start | bytes 131072 | tf_op jit(solution)/shard_map/all_to_all | solution.py:77
  223.0 7.0 %all-to-all-done = bf16[128,1,6]{2,1,0:T(2,128)(2,1)} async-done(((bf16[128,1,6]{2,1,0:T(2,128)(2,1)}), bf16[128,1,6]{2,1,0:T(2,128)(2,1)}, u32[]{:S(2)}, u32[]{:S(2)}) %all-to-all-start) | async-done | bytes 1568 | tf_op jit(solution)/shard_map/all_to_all | solution.py:77
  231.8 64.7 %all-reduce.4.cloned.1.call-done = bf16[768,3072]{1,0:T(8,128)(2,1)} async-done(((bf16[768,3072]{1,0:T(8,128)(2,1)}), bf16[768,3072]{1,0:T(8,128)(2,1)}) %all-reduce.4.cloned.1.call-update) | async-done | bytes 4718608 | tf_op jit(solution)/shard_map/psum | solution.py:97
  300.1 4.2 %multiply_convert_fusion.1 = (bf16[768,1024]{1,0:T(8,128)(2,1)}, bf16[768,1024]{1,0:T(8,128)(2,1)}, bf16[768]{0:T(1024)(128)(2,1)S(1)}) fusion(f32[768,3072]{1,0:T(8,128)S(1)} %convert_element_type.85, f32[768]{0:T(1024)S(1)} %copy-done.14), kind=kLoop, calls=%fused_computation.27 | loop fusion | flops 14155008 | bytes 12587520 | tf_op jit(solution)/shard_map/convert_element_type | solution.py:21
  305.6 8.2 %all-to-all-start.4 = ((bf16[128,1,6]{2,1,0:T(2,128)(2,1)}), bf16[128,1,6]{2,1,0:T(2,128)(2,1)S(1)}, u32[]{:S(2)}, u32[]{:S(2)}) async-start(bf16[128,1,6]{2,1,0:T(2,128)(2,1)} %convert_element_type.97), calls=%async_computation.4 | async-start | bytes 131072 | tf_op jit(solution)/shard_map/all_to_all | solution.py:127
  313.8 4.6 %fusion.6 = f32[768,1664]{1,0:T(8,128)S(1)} fusion(bf16[768,1024]{1,0:T(8,128)(2,1)} %get-tuple-element.29, bf16[1,1664,1024]{2,1,0:T(8,128)(2,1)S(1)} %copy-done), kind=kOutput, calls=%fused_computation.17 | convolution fusion | flops 2617245696 | bytes 10092544 | tf_op jit(solution)/shard_map/dot_general | solution.py:112
  324.4 10.2 %all-to-all-start.3 = ((bf16[128,6,1664]{2,1,0:T(8,128)(2,1)}), bf16[128,6,1664]{2,1,0:T(8,128)(2,1)}, u32[]{:S(2)}, u32[]{:S(2)}) async-start(bf16[128,6,1664]{2,1,0:T(8,128)(2,1)} %reshape.201), calls=%async_computation.3 | async-start | bytes 6815744 | tf_op jit(solution)/shard_map/all_to_all | solution.py:120
  334.6 6.1 %fusion.11 = bf16[1,1664,1024]{2,1,0:T(8,128)(2,1)} fusion(bf16[768,1664]{1,0:T(8,128)(2,1)S(1)} %copy-done.4, bf16[768,1024]{1,0:T(8,128)(2,1)} %get-tuple-element.28), kind=kOutput, calls=%fused_computation.22 | convolution fusion | flops 2618949632 | bytes 7536640 | tf_op jit(solution)/shard_map/dot_general | solution.py:105
  340.7 4.3 %fusion.10 = bf16[1,1664,1024]{2,1,0:T(8,128)(2,1)} fusion(bf16[768,1664]{1,0:T(8,128)(2,1)S(1)} %copy-done.4, bf16[768,1024]{1,0:T(8,128)(2,1)S(1)} %copy-done.6), kind=kOutput, calls=%fused_computation.21 | convolution fusion | flops 2618949632 | bytes 7536640 | tf_op jit(solution)/shard_map/dot_general | solution.py:102
  345.0 8.1 %fusion.12 = bf16[1,1024,1664]{2,1,0:T(8,128)(2,1)} fusion(bf16[768,1664]{1,0:T(8,128)(2,1)S(1)} %copy-done.5, f32[768]{0:T(1024)S(1)} %copy-done.15, f32[768,3072]{1,0:T(8,128)} %copy-done.2), kind=kOutput, calls=%fused_computation.23 | convolution fusion | flops 2624454656 | bytes 12258304 | tf_op jit(solution)/shard_map/dot_general | solution.py:108
  353.4 6.8 %gather_fusion = bf16[1024]{0:T(1024)(128)(2,1)S(1)} fusion(bf16[768]{0:T(1024)(128)(2,1)S(1)} %reshape_reshape.11, s32[1024]{0:T(1024)S(1)} %broadcast_clamp_fusion), kind=kCustom, calls=%fused_computation.2 | custom fusion | bytes 8192 | tf_op jit(solution)/shard_map/jit(_take)/gather | solution.py:149
  361.0 18.1 %all-to-all-done.3 = bf16[128,6,1664]{2,1,0:T(8,128)(2,1)} async-done(((bf16[128,6,1664]{2,1,0:T(8,128)(2,1)}), bf16[128,6,1664]{2,1,0:T(8,128)(2,1)}, u32[]{:S(2)}, u32[]{:S(2)}) %all-to-all-start.3) | async-done | bytes 2555936 | tf_op jit(solution)/shard_map/all_to_all | solution.py:120
  379.1 4.4 %copy.71 = bf16[32,4,6,1664]{3,1,0,2:T(4,128)(2,1)} copy(bf16[32,4,6,1664]{3,2,1,0:T(8,128)(2,1)} %bitcast.7) | data formatting | bytes 5111808 | tf_op jit(solution)/shard_map/reshape | solution.py:135
  383.5 5.7 %dot_general.37 = bf16[6656,6,32]{0,2,1:T(8,128)(2,1)} reshape(bf16[4,1664,6,32]{1,0,3,2:T(4,128)(2,1)} %bitcast.74) | data formatting | bytes 5111808 | tf_op jit(solution)/shard_map/tec,escq->tsq/dot_general | solution.py:146
  (96 shorter events, 53.7 us)
Async XLA Ops:
  7.2 146.2 %copy-start = (bf16[1,1664,1024]{2,1,0:T(8,128)(2,1)S(1)}, bf16[1,1664,1024]{2,1,0:T(8,128)(2,1)}, u32[]{:S(2)}) copy-start(bf16[1,1664,1024]{2,1,0:T(8,128)(2,1)} %param.13) | copy-start | bytes 10223620
  31.1 0.6 copy-start.13
  34.8 4.5 %copy-start.17 = (s32[1024,1]{0,1:T(1,128)}, s32[1024,1]{0,1:T(1,128)S(1)}, u32[]{:S(2)}) copy-start(s32[1024,1]{0,1:T(1,128)S(1)} %compare_select_fusion.2) | copy-start | bytes 12292
  79.4 56.5 %all-to-all-start.1 = ((bf16[128,6,1664]{2,1,0:T(8,128)(2,1)}), bf16[128,6,1664]{2,1,0:T(8,128)(2,1)}, u32[]{:S(2)}, u32[]{:S(2)}) async-start(bf16[128,6,1664]{2,1,0:T(8,128)(2,1)} %reshape_reshape.9), calls=%async_computation.1 | async-start | bytes 6815744 | tf_op jit(solution)/shard_map/all_to_all | solution.py:63
  135.9 49.6 %all-to-all-start.2 = ((bf16[128,6,1664]{2,1,0:T(8,128)(2,1)}), bf16[128,6,1664]{2,1,0:T(8,128)(2,1)}, u32[]{:S(2)}, u32[]{:S(2)}) async-start(bf16[128,6,1664]{2,1,0:T(8,128)(2,1)} %reshape_reshape.10), calls=%async_computation.2 | async-start | bytes 6815744 | tf_op jit(solution)/shard_map/all_to_all | solution.py:70
  140.8 155.7 %all-reduce.4.cloned.1.call-start = ((), (), s32[]{:S(2)}) async-start(), calls=%async_computation.5 | async-start | bytes 9437184 | tf_op jit(solution)/shard_map/psum | solution.py:97
  146.4 7.0 %copy-start.3 = (bf16[768,1664]{1,0:T(8,128)(2,1)S(1)}, bf16[768,1664]{1,0:T(8,128)(2,1)}, u32[]{:S(2)}) copy-start(bf16[768,1664]{1,0:T(8,128)(2,1)} %reshape.198) | copy-start | bytes 7667716
  190.8 5.9 %copy-start.8 = (bf16[768,1024]{1,0:T(8,128)(2,1)S(1)}, bf16[768,1024]{1,0:T(8,128)(2,1)}, u32[]{:S(2)}) copy-start(bf16[768,1024]{1,0:T(8,128)(2,1)} %fusion.16) | copy-start | bytes 4718596
  190.8 5.9 %copy-start.9 = (bf16[768,1024]{1,0:T(8,128)(2,1)S(1)}, bf16[768,1024]{1,0:T(8,128)(2,1)}, u32[]{:S(2)}) copy-start(bf16[768,1024]{1,0:T(8,128)(2,1)} %fusion.13) | copy-start | bytes 4718596
  199.1 21.1 %copy-start.11 = (s32[128,8]{1,0:T(8,128)S(1)}, s32[128,8]{1,0:T(8,128)}, u32[]{:S(2)}) copy-start(s32[128,8]{1,0:T(8,128)} %get-tuple-element.31) | copy-start | bytes 12292
  199.1 21.7 %copy-start.10 = (s32[128,8]{1,0:T(8,128)S(1)}, s32[128,8]{1,0:T(8,128)}, u32[]{:S(2)}) copy-start(s32[128,8]{1,0:T(8,128)} %get-tuple-element.26) | copy-start | bytes 12292
  215.4 14.6 %all-to-all-start = ((bf16[128,1,6]{2,1,0:T(2,128)(2,1)}), bf16[128,1,6]{2,1,0:T(2,128)(2,1)}, u32[]{:S(2)}, u32[]{:S(2)}) async-start(bf16[128,1,6]{2,1,0:T(2,128)(2,1)} %copy.61), calls=%async_computation | async-start | bytes 131072 | tf_op jit(solution)/shard_map/all_to_all | solution.py:77
  231.8 68.3 %copy-start.14 = (f32[768]{0:T(1024)S(1)}, f32[768]{0:T(1024)}, u32[]{:S(2)}) copy-start(f32[768]{0:T(1024)} %reshape.204) | copy-start | bytes 9220
  300.1 4.7 %copy-start.2 = (f32[768,3072]{1,0:T(8,128)}, f32[768,3072]{1,0:T(8,128)S(1)}, u32[]{:S(2)}) copy-start(f32[768,3072]{1,0:T(8,128)S(1)} %convert_element_type.85) | copy-start | bytes 28311556
  305.6 18.8 %all-to-all-start.4 = ((bf16[128,1,6]{2,1,0:T(2,128)(2,1)}), bf16[128,1,6]{2,1,0:T(2,128)(2,1)S(1)}, u32[]{:S(2)}, u32[]{:S(2)}) async-start(bf16[128,1,6]{2,1,0:T(2,128)(2,1)} %convert_element_type.97), calls=%async_computation.4 | async-start | bytes 131072 | tf_op jit(solution)/shard_map/all_to_all | solution.py:127
  313.8 4.6 %copy-start.7 = (bf16[768,1024]{1,0:T(8,128)(2,1)S(1)}, bf16[768,1024]{1,0:T(8,128)(2,1)}, u32[]{:S(2)}) copy-start(bf16[768,1024]{1,0:T(8,128)(2,1)} %get-tuple-element.28) | copy-start | bytes 4718596
  313.8 4.6 %copy-start.18 = (bf16[1,1664,1024]{2,1,0:T(8,128)(2,1)S(1)}, bf16[1,1664,1024]{2,1,0:T(8,128)(2,1)}, u32[]{:S(2)}) copy-start(bf16[1,1664,1024]{2,1,0:T(8,128)(2,1)} %param.14) | copy-start | bytes 10223620
  324.4 10.2 %copy-start.16 = (s32[1024,1]{0,1:T(1,128)S(1)}, s32[1024,1]{0,1:T(1,128)}, u32[]{:S(2)}) copy-start(s32[1024,1]{0,1:T(1,128)} %compare_select_fusion.1) | copy-start | bytes 12292
  324.4 10.2 %copy-start.4 = (bf16[768,1664]{1,0:T(8,128)(2,1)S(1)}, bf16[768,1664]{1,0:T(8,128)(2,1)}, u32[]{:S(2)}) copy-start(bf16[768,1664]{1,0:T(8,128)(2,1)} %reshape.198) | copy-start | bytes 7667716
  324.4 54.8 %all-to-all-start.3 = ((bf16[128,6,1664]{2,1,0:T(8,128)(2,1)}), bf16[128,6,1664]{2,1,0:T(8,128)(2,1)}, u32[]{:S(2)}, u32[]{:S(2)}) async-start(bf16[128,6,1664]{2,1,0:T(8,128)(2,1)} %reshape.201), calls=%async_computation.3 | async-start | bytes 6815744 | tf_op jit(solution)/shard_map/all_to_all | solution.py:120
  334.6 6.1 %copy-start.6 = (bf16[768,1024]{1,0:T(8,128)(2,1)S(1)}, bf16[768,1024]{1,0:T(8,128)(2,1)}, u32[]{:S(2)}) copy-start(bf16[768,1024]{1,0:T(8,128)(2,1)} %get-tuple-element.29) | copy-start | bytes 4718596
  340.7 4.3 %copy-start.5 = (bf16[768,1664]{1,0:T(8,128)(2,1)S(1)}, bf16[768,1664]{1,0:T(8,128)(2,1)}, u32[]{:S(2)}) copy-start(bf16[768,1664]{1,0:T(8,128)(2,1)} %reshape.200) | copy-start | bytes 7667716
  340.7 4.3 %copy-start.15 = (f32[768]{0:T(1024)S(1)}, f32[768]{0:T(1024)}, u32[]{:S(2)}) copy-start(f32[768]{0:T(1024)} %reshape.204) | copy-start | bytes 9220
  383.5 5.7 %copy-start.12 = (bf16[128,32,6]{0,2,1:T(8,128)(2,1)S(1)}, bf16[128,32,6]{0,2,1:T(8,128)(2,1)}, u32[]{:S(2)}) copy-start(bf16[128,32,6]{0,2,1:T(8,128)(2,1)} %convert_element_type.81) | copy-start | bytes 147460
  383.5 9.2 %copy-start.1 = (bf16[1,1664,1024]{2,1,0:T(8,128)(2,1)S(1)}, bf16[1,1664,1024]{2,1,0:T(8,128)(2,1)}, u32[]{:S(2)}) copy-start(bf16[1,1664,1024]{2,1,0:T(8,128)(2,1)} %param.13) | copy-start | bytes 10223620
Sparse Core Ops, SparseCore 0:
  199.3 97.1 all-reduce.3
where the time goes:
time: 402 us; the launch traced here: 400 us
  waiting for transfers between devices  157 us (39%)
  local copies, waits for them, and re-layouts  99.7 us (25%)
  matrix products  47 us (12%)
  other arithmetic  41.2 us (10%)
  starting transfers between devices  40.2 us (10%)
  between operations  14.4 us (4%)
    psum x1, waiting for transfers between devices, on_device(): lax.psum(jnp.concatenate([gate_part, up_part, back_part], axis=1).astype(...  64.7 us
    all_to_all x1, waiting for transfers between devices, on_device(): lax.all_to_all(x_send.reshape(experts * sp_count, CAP, quarter), ('ep', '...  39.3 us
    all_to_all x1, waiting for transfers between devices, on_device(): lax.all_to_all(dy_send.reshape(experts * sp_count, CAP, quarter), ('ep',...  28 us
    another operation x4, other arithmetic  19.7 us
    all_to_all x1, waiting for transfers between devices, on_device(): lax.all_to_all(row_grad.reshape(ep_count * sp_count, CAP, quarter), ('ep'...  18.1 us
    gather x2, local copies, waits for them, and re-layouts, spread(): jnp.take(flat_rows, spread_index, axis=0)  15.7 us
    all_to_all x1, starting transfers between devices, on_device(): lax.all_to_all(x_send.reshape(experts * sp_count, CAP, quarter), ('ep', '...  11.9 us
    all_to_all x1, starting transfers between devices, on_device(): lax.all_to_all(row_grad.reshape(ep_count * sp_count, CAP, quarter), ('ep'...  10.2 us
  transfers between devices with their start and end apart: 6, of which 5 were waited for; matrix products, arithmetic and copies ran while one was open for 19% of the time, Pallas kernels for 0%

commit v1 on v0

v1 whole, which is shorter than its diff:
```python
import functools

import jax
import jax.numpy as jnp
from jax import lax
from jax.experimental import pallas as pl
from jax.experimental.pallas import tpu as pltpu
from jax.sharding import PartitionSpec as P

CAP = 6
EXPERTS = 32
TOK = 128
TOP = 8
WIDE = 1280
TAIL = 384
QUARTER = WIDE + TAIL
PACKED = 8
BLOCK = 32
SLOTS = BLOCK * CAP
ROWS8 = BLOCK * PACKED
MIB = 1 << 20
BF16 = jnp.bfloat16
F32 = jnp.float32


def iota(shape, dim):
    return lax.broadcasted_iota(jnp.int32, shape, dim)


def product(a, b):
    return jnp.dot(a, b, preferred_element_type=F32)


def product_t(a, b):
    return lax.dot_general(a, b, (((1,), (1,)), ((), ())), preferred_element_type=F32)


def one_hot(mask):
    return jnp.where(mask, 1.0, 0.0)


def tables(ids, probs, left_ref, combine_ref, spare_ref):
    lane = iota((TOK, 128), 1)
    member = jnp.zeros((TOK, 128), F32)
    weight = jnp.zeros((TOK, 128), F32)
    for k in range(TOP):
        hit = ids[:, k : k + 1] == lane
        member = member + jnp.where(hit, 1.0, 0.0)
        weight = weight + jnp.where(hit, probs[:, k : k + 1], 0.0)
    member = member.astype(BF16)
    before = one_hot(iota((TOK, TOK), 1) < iota((TOK, TOK), 0)).astype(BF16)
    rank = product(before, member).astype(BF16)
    widen = one_hot(iota((128, ROWS8), 0) == iota((128, ROWS8), 1) // PACKED).astype(BF16)
    member8 = product(member, widen)
    rank8 = product(rank, widen)
    weight8 = product(weight.astype(BF16), widen)
    place = iota((TOK, ROWS8), 1) % PACKED
    rank8 = jnp.where(member8 > 0.5, rank8, -1.0)
    own = one_hot((rank8 == place.astype(F32)) & (place < CAP))
    combine_ref[0] = own.astype(BF16)
    own_t = own.T
    for g in range(3):
        goal = (place - CAP) * 3 + g
        tail = one_hot((rank8 == goal.astype(F32)) & (place >= CAP))
        combine_ref[g + 1] = tail.astype(BF16)
        left_ref[g] = jnp.concatenate([own_t, tail.T], axis=1).astype(BF16)
    prob = jnp.sum(own_t * weight8.T, axis=1, keepdims=True)
    row = iota((ROWS8, 128), 0)
    diagonal = jnp.where(row % PACKED == iota((ROWS8, 128), 1), prob, 0.0).astype(BF16)
    r = iota((ROWS8, ROWS8), 0)
    c = iota((ROWS8, ROWS8), 1)
    lift = one_hot((r // PACKED == c // PACKED) & (r % PACKED == CAP)).astype(BF16)
    spare_ref[...] = product(lift, diagonal).astype(BF16)


def spread(left_ref, x_ref, out_ref):
    rest = x_ref[:, WIDE:]
    for g in range(3):
        cols = pl.ds(g * TAIL, TAIL)
        right = jnp.concatenate([x_ref[:, cols], rest], axis=0)
        out_ref[:, cols] = product(left_ref[g], right).astype(BF16)
    return product(left_ref[0][:, :TOK], x_ref[:, 3 * TAIL : WIDE])


def spread_x_kernel(ids_ref, probs_ref, x_ref, out_ref, left_ref, combine_ref, spare_ref):
    @pl.when(pl.program_id(0) == 0)
    def _():
        tables(ids_ref[...], probs_ref[...], left_ref, combine_ref, spare_ref)

    out_ref[:, 3 * TAIL :] = spread(left_ref, x_ref, out_ref).astype(BF16)


def spread_dy_kernel(left_ref, spare_ref, x_ref, out_ref):
    last = spread(left_ref, x_ref, out_ref)
    out_ref[:, 3 * TAIL :] = last.astype(BF16) + spare_ref[...]


def unpack_masks(main_ref, tail_ref):
    r = iota((SLOTS, ROWS8), 0)
    c = iota((SLOTS, ROWS8), 1)
    same = r // CAP == c // PACKED
    slot = r % CAP
    place = c % PACKED
    main_ref[...] = one_hot(same & (slot == place)).astype(BF16)
    for g in range(3):
        tail = one_hot(same & (place >= CAP) & (slot == (place - CAP) * 3 + g))
        tail_ref[:, g * ROWS8 : (g + 1) * ROWS8] = tail.astype(BF16)


def stacked(packed):
    return jnp.concatenate([packed[:, g * TAIL : (g + 1) * TAIL] for g in range(3)], axis=0)


def unpack(main_ref, tail_ref, packed, rows_ref):
    rows_ref[:, :WIDE] = product(main_ref[...], packed).astype(BF16)
    rows_ref[:, WIDE:] = product(tail_ref[...], stacked(packed)).astype(BF16)


def gate_up_kernel(packed_ref, gate_ref, up_ref, rows_ref, parts_ref, main_ref, tail_ref):
    @pl.when(pl.program_id(0) == 0)
    def _():
        unpack_masks(main_ref, tail_ref)

    unpack(main_ref, tail_ref, packed_ref[...], rows_ref)
    rows = rows_ref[...]
    hidden = gate_ref.shape[1]
    parts_ref[:, :hidden] = product(rows, gate_ref[...]).astype(BF16)
    parts_ref[:, hidden:] = product(rows, up_ref[...]).astype(BF16)


def back_kernel(packed_ref, down_ref, rows_ref, part_ref, prob_ref, main_ref, tail_ref):
    @pl.when(pl.program_id(0) == 0)
    def _():
        unpack_masks(main_ref, tail_ref)

    packed = packed_ref[...]
    unpack(main_ref, tail_ref, packed, rows_ref)
    part_ref[...] = product_t(rows_ref[...], down_ref[...]).astype(BF16)
    r = iota((SLOTS, ROWS8), 0)
    c = iota((SLOTS, ROWS8), 1)
    pick = one_hot((r // CAP == c // PACKED) & (c % PACKED == CAP)).astype(BF16)
    probs = product(pick, packed[:, 3 * TAIL :])
    mine = iota((SLOTS, 128), 0) % CAP == iota((SLOTS, 128), 1)
    prob = jnp.sum(jnp.where(mine, probs, 0.0), axis=1, keepdims=True)
    prob_ref[...] = jnp.broadcast_to(prob, (SLOTS, 128)).astype(BF16)


def activate_kernel(gate_up_ref, back_ref, prob_ref, grads_ref, weighted_ref, slot_ref):
    hidden = back_ref.shape[1]
    gate = gate_up_ref[:, :hidden].astype(F32)
    up = gate_up_ref[:, hidden:].astype(F32)
    back = back_ref[...].astype(F32)
    weight = prob_ref[:, :1].astype(F32)
    sigmoid = 1.0 / (1.0 + jnp.exp(-gate))
    swish = gate * sigmoid
    act = swish * up
    grad_act = weight * back
    grads_ref[:, :hidden] = (grad_act * up * sigmoid * (1.0 + gate * (1.0 - sigmoid))).astype(BF16)
    grads_ref[:, hidden:] = (grad_act * swish).astype(BF16)
    weighted_ref[...] = (weight * act).astype(BF16)
    slot = jnp.sum(back * act, axis=1, keepdims=True)
    shape = slot_ref.shape
    mine = iota(shape, 0) % CAP == iota(shape, 1)
    slot_ref[...] = jnp.where(mine, slot, 0.0).astype(BF16)


def row_grad_kernel(own_ref, grads_ref, gate_ref, up_ref, slot_ref, out_ref, pack_ref, lift_ref):
    @pl.when(pl.program_id(0) == 0)
    def _():
        r = iota((ROWS8, SLOTS), 0)
        c = iota((ROWS8, SLOTS), 1)
        same = r // PACKED == c // CAP
        place = r % PACKED
        slot = c % CAP
        for g in range(3):
            pack_ref[g, :, :SLOTS] = one_hot(same & (slot == place)).astype(BF16)
            tail = one_hot(same & (place >= CAP) & (slot == (place - CAP) * 3 + g))
            pack_ref[g, :, SLOTS:] = tail.astype(BF16)
        lift_ref[...] = one_hot(same & (place == CAP)).astype(BF16)

    hidden = gate_ref.shape[1]
    rows = product_t(grads_ref[:, :hidden], gate_ref[...])
    rows = (rows + product_t(grads_ref[:, hidden:], up_ref[...])).astype(BF16)
    rest = rows[:, WIDE:]
    for g in range(3):
        right = jnp.concatenate([rows[:, g * TAIL : (g + 1) * TAIL], rest], axis=0)
        out_ref[:, g * TAIL : (g + 1) * TAIL] = product(pack_ref[g], right).astype(BF16)
    last = product(pack_ref[0, :, :SLOTS], rows[:, 3 * TAIL : WIDE])
    held = jnp.where(own_ref[0] == pl.program_id(0), 1.0, 0.0)
    last = last + held * product(lift_ref[...], slot_ref[...])
    out_ref[:, 3 * TAIL :] = last.astype(BF16)


def combine_kernel(ids_ref, combine_ref, packed_ref, out_ref, probs_ref, slot_ref):
    step = pl.program_id(0)
    packed = packed_ref[...]
    out_ref[:, :WIDE] = product(combine_ref[0], packed).astype(BF16)
    tails = jnp.concatenate([combine_ref[g + 1] for g in range(3)], axis=1)
    out_ref[:, WIDE:] = product(tails, stacked(packed)).astype(BF16)
    spare = packed[:, 3 * TAIL :].astype(F32)

    @pl.when(step == 0)
    def _():
        slot_ref[...] = spare

    @pl.when(step > 0)
    def _():
        slot_ref[...] += spare

    @pl.when(step == pl.num_programs(0) - 1)
    def _():
        row = iota((ROWS8, 128), 0)
        slots = jnp.where(row % PACKED == CAP, slot_ref[...], 0.0).astype(BF16)
        r = iota((ROWS8, ROWS8), 0)
        c = iota((ROWS8, ROWS8), 1)
        group = one_hot(r // PACKED == c // PACKED).astype(BF16)
        wide = lax.dot_general(slots, group, (((0,), (0,)), ((), ())), preferred_element_type=F32)
        mine = iota((128, ROWS8), 0) == iota((128, ROWS8), 1) % PACKED
        flat = jnp.sum(jnp.where(mine, wide, 0.0), axis=0, keepdims=True)
        value = (combine_ref[0].astype(F32) * flat).astype(BF16)
        gather = one_hot(iota((ROWS8, 128), 0) // PACKED == iota((ROWS8, 128), 1)).astype(BF16)
        table = product(value, gather)
        lane = iota((TOK, 128), 1)
        for k in range(TOP):
            hit = (ids_ref[:, k : k + 1] == lane) & (lane < EXPERTS)
            found = jnp.sum(jnp.where(hit, table, 0.0), axis=1, keepdims=True)
            probs_ref[:, k : k + 1] = found.astype(BF16)


def call(kernel, grid, ins, outs, scratch=(), flops=0, moved=0):
    return pl.pallas_call(
        kernel,
        grid=(grid,),
        in_specs=ins,
        out_specs=[s for s, _ in outs],
        out_shape=[jax.ShapeDtypeStruct(shape, kind) for _, (shape, kind) in outs],
        scratch_shapes=list(scratch),
        compiler_params=pltpu.CompilerParams(
            dimension_semantics=("arbitrary",), vmem_limit_bytes=48 * MIB
        ),
        cost_estimate=pl.CostEstimate(flops=flops, bytes_accessed=moved, transcendentals=0),
    )


def whole(*shape):
    return pl.BlockSpec(shape, lambda i: (0,) * len(shape))


def once(*shape):
    return pl.BlockSpec(shape, lambda i: (0,) * len(shape), pipeline_mode=pl.Buffered(1))


def rows_of(rows, cols):
    return pl.BlockSpec((rows, cols), lambda i: (i, 0))


def cols_of(rows, cols):
    return pl.BlockSpec((rows, cols), lambda i: (0, i))


def on_device(hidden_in, grad_out, route_ids, route_probs, w_gate, w_up, w_down):
    sp_count = lax.axis_size("sp")
    pieces = lax.axis_size("ep") * sp_count
    hidden = w_gate.shape[2]
    model = hidden_in.shape[1]
    all_rows = pieces * CAP
    packed8 = pieces * PACKED
    gate_weight, up_weight, down_weight = w_gate[0], w_up[0], w_down[0]
    packet = (rows_of(ROWS8, WIDE), ((packed8, WIDE), BF16))
    x_send, left, combine, spare = call(
        spread_x_kernel,
        sp_count,
        [whole(TOK, TOP), whole(TOK, TOP), cols_of(TOK, QUARTER)],
        [
            packet,
            (whole(3, ROWS8, ROWS8), ((3, ROWS8, ROWS8), BF16)),
            (whole(4, TOK, ROWS8), ((4, TOK, ROWS8), BF16)),
            (whole(ROWS8, 128), ((ROWS8, 128), BF16)),
        ],
        flops=2 * packed8 * WIDE * 256,
        moved=2 * (packed8 * WIDE + TOK * model),
    )(route_ids, route_probs, hidden_in)
    (dy_send,) = call(
        spread_dy_kernel,
        sp_count,
        [whole(3, ROWS8, ROWS8), whole(ROWS8, 128), cols_of(TOK, QUARTER)],
        [packet],
        flops=2 * packed8 * WIDE * 256,
        moved=2 * (packed8 * WIDE + TOK * model),
    )(left, spare, grad_out)

    def exchange(packed):
        pieced = packed.reshape(pieces, PACKED, WIDE)
        moved = lax.all_to_all(pieced, ("sp", "ep"), split_axis=0, concat_axis=0, tiled=True)
        return moved.reshape(packed8, WIDE)

    x_packed = exchange(x_send)
    dy_packed = exchange(dy_send)
    masks = (pltpu.VMEM((SLOTS, ROWS8), BF16), pltpu.VMEM((SLOTS, 3 * ROWS8), BF16))
    rows_out = (rows_of(SLOTS, QUARTER), ((all_rows, QUARTER), BF16))
    x_rows, gate_up_part = call(
        gate_up_kernel,
        sp_count,
        [rows_of(ROWS8, WIDE), once(QUARTER, hidden), once(QUARTER, hidden)],
        [rows_out, (rows_of(SLOTS, 2 * hidden), ((all_rows, 2 * hidden), BF16))],
        masks,
        flops=4 * all_rows * QUARTER * hidden,
        moved=2 * (packed8 * WIDE + 2 * QUARTER * hidden + all_rows * (QUARTER + 2 * hidden)),
    )(x_packed, gate_weight, up_weight)
    gate_up = lax.psum_scatter(gate_up_part, "sp", scatter_dimension=0, tiled=True)
    dy_rows, back_part, prob_rows = call(
        back_kernel,
        sp_count,
        [rows_of(ROWS8, WIDE), once(hidden, QUARTER)],
        [
            rows_out,
            (rows_of(SLOTS, hidden), ((all_rows, hidden), BF16)),
            (rows_of(SLOTS, 128), ((all_rows, 128), BF16)),
        ],
        masks,
        flops=2 * all_rows * QUARTER * hidden,
        moved=2 * (packed8 * WIDE + QUARTER * hidden + all_rows * (QUARTER + hidden)),
    )(dy_packed, down_weight)
    back = lax.psum_scatter(back_part, "sp", scatter_dimension=0, tiled=True)
    own = lax.axis_index("sp").astype(jnp.int32)
    own_rows = all_rows // sp_count
    prob_own = lax.dynamic_slice_in_dim(prob_rows, own * own_rows, own_rows, axis=0)
    parts = 4
    step_rows = own_rows // parts
    grads_own, weighted_own, slot_own = call(
        activate_kernel,
        parts,
        [rows_of(step_rows, 2 * hidden), rows_of(step_rows, hidden), rows_of(step_rows, 128)],
        [
            (rows_of(step_rows, 2 * hidden), ((own_rows, 2 * hidden), BF16)),
            (rows_of(step_rows, hidden), ((own_rows, hidden), BF16)),
            (rows_of(step_rows, 128), ((own_rows, 128), BF16)),
        ],
        flops=20 * own_rows * hidden,
        moved=12 * own_rows * hidden,
    )(gate_up, back, prob_own)
    grads = lax.all_gather(grads_own, "sp", axis=0, tiled=True)
    weighted = lax.all_gather(weighted_own, "sp", axis=0, tiled=True)
    (back_send,) = call(
        row_grad_kernel,
        sp_count,
        [
            pl.BlockSpec(memory_space=pltpu.SMEM),
            rows_of(SLOTS, 2 * hidden),
            once(QUARTER, hidden),
            once(QUARTER, hidden),
            whole(SLOTS, 128),
        ],
        [packet],
        (pltpu.VMEM((3, ROWS8, 2 * SLOTS), BF16), pltpu.VMEM((ROWS8, SLOTS), BF16)),
        flops=4 * all_rows * QUARTER * hidden,
        moved=2 * (packed8 * WIDE + 2 * QUARTER * hidden + all_rows * 2 * hidden),
    )(own.reshape(1), grads, gate_weight, up_weight, slot_own)
    back_packed = exchange(back_send)
    contract_rows = (((0,), (0,)), ((), ()))

    def over_rows(a, b):
        return lax.dot_general(a, b, contract_rows, preferred_element_type=F32).astype(BF16)

    grad_gate_weight = over_rows(x_rows, grads[:, :hidden])
    grad_up_weight = over_rows(x_rows, grads[:, hidden:])
    grad_down_weight = over_rows(weighted, dy_rows)
    grad_in, grad_probs = call(
        combine_kernel,
        sp_count,
        [whole(TOK, TOP), whole(4, TOK, ROWS8), rows_of(ROWS8, WIDE)],
        [
            (cols_of(TOK, QUARTER), ((TOK, model), BF16)),
            (whole(TOK, TOP), ((TOK, TOP), BF16)),
        ],
        (pltpu.VMEM((ROWS8, 128), F32),),
        flops=2 * packed8 * WIDE * TOK * 2,
        moved=2 * (packed8 * WIDE + TOK * model),
    )(route_ids, combine, back_packed)
    return (
        grad_in,
        grad_gate_weight[None],
        grad_up_weight[None],
        grad_down_weight[None],
        grad_probs,
    )


def solution(mesh):
    placed = (
        P(("ep", "sp"), None),
        P(("ep", "sp"), None),
        P(("ep", "sp"), None),
        P(("ep", "sp"), None),
        P("ep", "sp", None),
        P("ep", "sp", None),
        P("ep", None, "sp"),
    )
    return jax.shard_map(
        on_device,
        mesh=mesh,
        in_specs=placed,
        out_specs=(
            P(("ep", "sp"), None),
            P("ep", "sp", None),
            P("ep", "sp", None),
            P("ep", None, "sp"),
            P(("ep", "sp"), None),
        ),
        check_vma=False,
    )
```

time: 402 us -> 292 us (0.73)
  blocking collectives: 0 us -> 101 us
  local copies, waits for them, and re-layouts: 99.7 us -> 13.3 us
  waiting for transfers between devices: 157 us -> 93.6 us
  Pallas kernels: 0 us -> 45.9 us
  other arithmetic: 41.2 us -> 0 us
  starting transfers between devices: 40.2 us -> 8.65 us
  matrix products: 47 us -> 15.7 us
    all_to_all x0 -> x2, blocking collectives: none -> 101 us  [exchange(): lax.all_to_all(pieced, ('sp', 'ep'), split_axis=0, concat_axis=0, tiled=T...]
    all_to_all x5 -> x1, waiting for transfers between devices: 92.4 us -> 19.6 us  [exchange(): lax.all_to_all(pieced, ('sp', 'ep'), split_axis=0, concat_axis=0, tiled=T...]
    psum x1 -> x0, waiting for transfers between devices: 64.7 us -> none  [on_device(): lax.psum(jnp.concatenate([gate_part, up_part, back_part], axis=1).astype(...]
    pallas_call x0 -> x7, Pallas kernels: none -> 45.9 us  [the longest x1 16.1 us: on_device(): call(row_grad_kernel, sp_count, [pl.BlockSpec(memory_space=pltpu.SMEM), r...]
    all_gather x0 -> x2, waiting for transfers between devices: none -> 39.6 us  [the longest x1 38.8 us: on_device(): grads = lax.all_gather(grads_own, 'sp', axis=0, tiled=True)]
    reduce_scatter x0 -> x2, waiting for transfers between devices: none -> 33.8 us  [the longest x1 33.8 us: on_device(): lax.psum_scatter(gate_up_part, 'sp', scatter_dimension=0, tiled=True)]
    all_to_all x5 -> x1, starting transfers between devices: 40 us -> 8.49 us  [exchange(): lax.all_to_all(pieced, ('sp', 'ep'), split_axis=0, concat_axis=0, tiled=T...]
    dot_general x9 -> x3, matrix products: 47 us -> 15.7 us  [over_rows(): lax.dot_general(a, b, contract_rows, preferred_element_type=F32)]
  transfers between devices with their start and end apart: 6 -> 5, of which waited for: 5 -> 4; matrix products, arithmetic and copies ran while one was open for 19% -> 5% of each run, Pallas kernels for 0% -> 10%
where the time goes in v1:
time: 292 us
  blocking collectives  101 us (35%)
  waiting for transfers between devices  93.6 us (32%)
  Pallas kernels  45.9 us (16%)
  matrix products  15.7 us (5%)
  between operations  13.9 us (5%)
  local copies, waits for them, and re-layouts  13.3 us (5%)
  starting transfers between devices  8.65 us (3%)
    all_to_all x2, blocking collectives, exchange(): lax.all_to_all(pieced, ('sp', 'ep'), split_axis=0, concat_axis=0, tiled=T...  101 us
    all_gather x1, waiting for transfers between devices, on_device(): grads = lax.all_gather(grads_own, 'sp', axis=0, tiled=True)  38.8 us
    reduce_scatter x1, waiting for transfers between devices, on_device(): lax.psum_scatter(gate_up_part, 'sp', scatter_dimension=0, tiled=True)  33.8 us
    all_to_all x1, waiting for transfers between devices, exchange(): lax.all_to_all(pieced, ('sp', 'ep'), split_axis=0, concat_axis=0, tiled=T...  19.6 us
    pallas_call x1, Pallas kernels, on_device(): call(row_grad_kernel, sp_count, [pl.BlockSpec(memory_space=pltpu.SMEM), r...  16.1 us
    dot_general x3, matrix products, over_rows(): lax.dot_general(a, b, contract_rows, preferred_element_type=F32)  15.7 us
    unnamed x25, local copies, waits for them, and re-layouts  13.3 us
    pallas_call x1, Pallas kernels, on_device(): call(gate_up_kernel, sp_count, [rows_of(ROWS8, WIDE), once(QUARTER, hidde...  11.6 us
  transfers between devices with their start and end apart: 5, of which 4 were waited for; matrix products, arithmetic and copies ran while one was open for 5% of the time, Pallas kernels for 10%

profile of v1, /device:TPU:1, one launch (start us, length us, event | category | flops | bytes accessed | tf_op | source)
XLA Modules:
  0.0 291.5 jit_solution(2072818957567729715)
XLA Ops:
  7.2 0.8 copy.14.ids_ref
  8.0 0.8 copy.13.probs_ref
  8.8 1.4 copy-done.7
  10.2 2.6 shard_map.110
  12.9 1.7 shard_map.112
  14.6 47.5 %all_to_all.15 = bf16[128,8,1280]{2,1,0:T(8,128)(2,1)} all-to-all(bf16[128,8,1280]{2,1,0:T(8,128)(2,1)S(1)} %bitcast.21), channel_id=1, replica_groups=mesh['ep'=32,'sp'=4] {'sp','ep'}, dimensions={0} | all-to-all | bytes 5242880 | tf_op jit(solution)/shard_map/all_to_all | solution.py:294
  62.1 8.5 %shard_map.113 = (bf16[768,1664]{1,0:T(8,128)(2,1)S(1)}, bf16[768,1024]{1,0:T(8,128)(2,1)S(1)}, bf16[768,128]{1,0:T(8,128)(2,1)S(1)}) custom-call(bf16[1024,1280]{1,0:T(8,128)(2,1)} %bitcast.25, bf16[1024,1664]{1,0:T(8,128)(2,1)} %bitcast.26), custom_call_target="tpu_custom_call" | custom-call | flops 2617245696 | bytes 10158080 | tf_op jit(solution)/shard_map/pallas_call | solution.py:311
  70.6 1.1 copy-done.2
  71.7 1.5 copy-done.8
  73.2 0.0 reduce-scatter.3.cloned.1.call-start
  73.2 53.0 %all_to_all.16 = bf16[128,8,1280]{2,1,0:T(8,128)(2,1)S(1)} all-to-all(bf16[128,8,1280]{2,1,0:T(8,128)(2,1)S(1)} %bitcast.22), channel_id=1, replica_groups=mesh['ep'=32,'sp'=4] {'sp','ep'}, dimensions={0} | all-to-all | bytes 5242880 | tf_op jit(solution)/shard_map/all_to_all | solution.py:294
  126.3 11.6 %shard_map.111 = (bf16[768,1664]{1,0:T(8,128)(2,1)S(1)}, bf16[768,2048]{1,0:T(8,128)(2,1)}) custom-call(bf16[1024,1280]{1,0:T(8,128)(2,1)S(1)} %bitcast.24, bf16[1664,1024]{1,0:T(8,128)(2,1)} %bitcast.27, bf16[1664,1024]{1,0:T(8,128)(2,1)} %bitcast.29), custom_call_target="tpu_custom_call" | custom-call | flops 5234491392 | bytes 15138816 | tf_op jit(solution)/shard_map/pallas_call | solution.py:301
  137.9 1.5 copy-done.9
  139.4 0.0 all-gather.3.cloned.1.call-start
  139.5 33.8 %reduce-scatter.3.cloned.1.call-done.gate_up_ref = bf16[192,2048]{1,0:T(8,128)(2,1)} async-done(((bf16[768,2048]{1,0:T(8,128)(2,1)}), bf16[192,2048]{1,0:T(8,128)(2,1)}) %reduce-scatter.3.cloned.1.call-update) | async-done | bytes 786448 | tf_op jit(solution)/shard_map/reduce_scatter | solution.py:310
  173.3 1.1 copy-done.3
  174.4 1.0 copy-done.4
  175.4 1.9 shard_map.114
  177.4 0.0 all-gather.5.cloned.1.call-start
  177.4 0.5 all-gather.5.cloned.1.call-update
  178.0 38.8 %all-gather.3.cloned.1.call-done.grads_ref = bf16[768,2048]{1,0:T(8,128)(2,1)} async-done(((bf16[192,2048]{1,0:T(8,128)(2,1)}), bf16[768,2048]{1,0:T(8,128)(2,1)}) %all-gather.3.cloned.1.call-update) | async-done | bytes 3145744 | tf_op jit(solution)/shard_map/all_gather | solution.py:342
  216.8 1.9 copy-done.5
  218.6 16.1 %shard_map.115 = bf16[1024,1280]{1,0:T(8,128)(2,1)S(1)} custom-call(s32[1]{0:T(128)} %bitcast.own_ref, bf16[768,2048]{1,0:T(8,128)(2,1)S(1)} %copy-done.5, bf16[1664,1024]{1,0:T(8,128)(2,1)} %bitcast.28, bf16[1664,1024]{1,0:T(8,128)(2,1)} %bitcast.30, bf16[192,128]{1,0:T(8,128)(2,1)S(1)} %get-tuple-element.27.slot_ref), custom_call_target="tpu_custom_call" | custom-call | flops 5234491392 | bytes 12582912 | tf_op jit(solution)/shard_map/pallas_call | solution.py:344
  234.8 1.5 copy-done
  236.3 8.5 %all-to-all-start.2 = ((bf16[128,8,1280]{2,1,0:T(8,128)(2,1)}), bf16[128,8,1280]{2,1,0:T(8,128)(2,1)S(1)}, u32[]{:S(2)}, u32[]{:S(2)}) async-start(bf16[128,8,1280]{2,1,0:T(8,128)(2,1)} %bitcast.23), calls=%async_computation.4 | async-start | bytes 5242880 | tf_op jit(solution)/shard_map/all_to_all | solution.py:294
  244.8 0.8 all-gather.5.cloned.1.call-done
  245.6 7.2 %fusion.2 = bf16[1,1024,1664]{2,1,0:T(8,128)(2,1)} fusion(bf16[768,1024]{1,0:T(8,128)(2,1)} %all-gather.5.cloned.1.call-done, bf16[768,1664]{1,0:T(8,128)(2,1)} %copy-done.8), kind=kOutput, calls=%fused_computation.5 | convolution fusion | flops 2618949632 | bytes 7536640 | tf_op jit(solution)/shard_map/dot_general | solution.py:363
  252.7 4.2 %fusion = bf16[1,1664,1024]{2,1,0:T(8,128)(2,1)} fusion(bf16[768,1664]{1,0:T(8,128)(2,1)S(1)} %copy-done.10, bf16[768,2048]{1,0:T(8,128)(2,1)S(1)} %copy-done.6), kind=kOutput, calls=%fused_computation.3 | convolution fusion | flops 2618949632 | bytes 7536640 | tf_op jit(solution)/shard_map/dot_general | solution.py:363
  257.0 4.3 %fusion.1 = bf16[1,1664,1024]{2,1,0:T(8,128)(2,1)} fusion(bf16[768,1664]{1,0:T(8,128)(2,1)S(1)} %copy-done.10, bf16[768,2048]{1,0:T(8,128)(2,1)S(1)} %copy-done.6), kind=kOutput, calls=%fused_computation.4 | convolution fusion | flops 2618949632 | bytes 7536640 | tf_op jit(solution)/shard_map/dot_general | solution.py:363
  261.2 19.6 %all-to-all-done.2 = bf16[128,8,1280]{2,1,0:T(8,128)(2,1)S(1)} async-done(((bf16[128,8,1280]{2,1,0:T(8,128)(2,1)}), bf16[128,8,1280]{2,1,0:T(8,128)(2,1)S(1)}, u32[]{:S(2)}, u32[]{:S(2)}) %all-to-all-start.2) | async-done | bytes 2621472 | tf_op jit(solution)/shard_map/all_to_all | solution.py:294
  280.8 3.5 %shard_map.116 = (bf16[128,6656]{1,0:T(8,128)(2,1)}, bf16[128,8]{1,0:T(8,128)(2,1)S(1)}) custom-call(s32[128,8]{1,0:T(8,128)S(1)} %copy.14.ids_ref, bf16[4,128,256]{2,1,0:T(8,128)(2,1)S(1)} %get-tuple-element.19.combine_ref, bf16[1024,1280]{1,0:T(8,128)(2,1)S(1)} %bitcast.20), custom_call_target="tpu_custom_call" | custom-call | flops 671088640 | bytes 4325376 | tf_op jit(solution)/shard_map/pallas_call | solution.py:368
  284.3 0.7 copy.15
  (20 shorter events, 0.1 us)
Async XLA Ops:
  7.2 132.3 %reduce-scatter.5.cloned.1.call-start = ((), (), s32[]{:S(2)}) async-start(), calls=%async_computation.6 | async-start | bytes 1966080 | tf_op jit(solution)/shard_map/reduce_scatter | solution.py:324
  8.8 1.5 copy-start.7
  10.2 2.6 copy-start.1
  70.6 1.1 copy-start.2
  71.7 1.5 copy-start.8
  73.2 100.1 %reduce-scatter.3.cloned.1.call-start = ((), (), s32[]{:S(2)}) async-start(), calls=%async_computation.5 | async-start | bytes 3932160 | tf_op jit(solution)/shard_map/reduce_scatter | solution.py:310
  137.9 1.5 copy-start.9
  139.4 77.4 %all-gather.3.cloned.1.call-start = ((), (), s32[]{:S(2)}) async-start(), calls=%async_computation.7 | async-start | bytes 3932160 | tf_op jit(solution)/shard_map/all_gather | solution.py:342
  173.3 1.1 copy-start.3
  174.4 1.0 copy-start.4
  177.4 68.2 %all-gather.5.cloned.1.call-start = ((), (), s32[]{:S(2)}) async-start(), calls=%async_computation.8 | async-start | bytes 1966080 | tf_op jit(solution)/shard_map/all_gather | solution.py:343
  216.8 1.9 copy-start.5
  234.7 1.5 copy-start
  236.3 44.6 %all-to-all-start.2 = ((bf16[128,8,1280]{2,1,0:T(8,128)(2,1)}), bf16[128,8,1280]{2,1,0:T(8,128)(2,1)S(1)}, u32[]{:S(2)}, u32[]{:S(2)}) async-start(bf16[128,8,1280]{2,1,0:T(8,128)(2,1)} %bitcast.23), calls=%async_computation.4 | async-start | bytes 5242880 | tf_op jit(solution)/shard_map/all_to_all | solution.py:294
  245.6 7.2 %copy-start.6 = (bf16[768,2048]{1,0:T(8,128)(2,1)S(1)}, bf16[768,2048]{1,0:T(8,128)(2,1)}, u32[]{:S(2)}) copy-start(bf16[768,2048]{1,0:T(8,128)(2,1)} %all-gather.3.cloned.1.call-done.grads_ref) | copy-start | bytes 9437188
  245.6 7.2 %copy-start.10 = (bf16[768,1664]{1,0:T(8,128)(2,1)S(1)}, bf16[768,1664]{1,0:T(8,128)(2,1)}, u32[]{:S(2)}) copy-start(bf16[768,1664]{1,0:T(8,128)(2,1)} %copy-done.9) | copy-start | bytes 7667716
Sparse Core Ops, SparseCore 0:
  73.3 46.3 reduce-scatter.4
  139.5 33.7 reduce-scatter.2
  177.5 39.1 all-gather.2
  218.8 26.6 all-gather.4

commit v2 on v1

v2 whole, which is shorter than its diff:
```python
import jax
import jax.numpy as jnp
from jax import lax
from jax.experimental import pallas as pl
from jax.experimental.pallas import tpu as pltpu
from jax.sharding import PartitionSpec as P

CAP = 6
EXPERTS = 32
TOK = 128
TOP = 8
WIDE = 1280
TAIL = 384
QUARTER = WIDE + TAIL
PACKED = 8
BLOCK = 32
SLOTS = BLOCK * CAP
ROWS8 = BLOCK * PACKED
MIB = 1 << 20
BF16 = jnp.bfloat16
F32 = jnp.float32


def iota(shape, dim):
    return lax.broadcasted_iota(jnp.int32, shape, dim)


def product(a, b):
    return jnp.dot(a, b, preferred_element_type=F32)


def product_t(a, b):
    return lax.dot_general(a, b, (((1,), (1,)), ((), ())), preferred_element_type=F32)


def one_hot(mask):
    return jnp.where(mask, 1.0, 0.0)


def tables(ids, probs, left_ref, combine_ref, spare_ref):
    expert = iota((EXPERTS, TOK), 0)
    member = jnp.zeros((EXPERTS, TOK), F32)
    weight = jnp.zeros((EXPERTS, TOK), F32)
    for k in range(TOP):
        hit = ids[k : k + 1, :] == expert
        member = member + jnp.where(hit, 1.0, 0.0)
        weight = weight + jnp.where(hit, probs[k : k + 1, :], 0.0)
    member = member.astype(BF16)
    before = one_hot(iota((TOK, TOK), 0) < iota((TOK, TOK), 1)).astype(BF16)
    rank = product(member, before).astype(BF16)
    widen = one_hot(iota((ROWS8, EXPERTS), 0) // PACKED == iota((ROWS8, EXPERTS), 1)).astype(BF16)
    member8 = product(widen, member)
    rank8 = jnp.where(member8 > 0.5, product(widen, rank), -1.0)
    weight8 = product(widen, weight.astype(BF16))
    place = iota((ROWS8, TOK), 0) % PACKED
    own = one_hot((rank8 == place.astype(F32)) & (place < CAP))
    combine_ref[0] = own.T.astype(BF16)
    for g in range(3):
        goal = (place - CAP) * 3 + g
        tail = one_hot((rank8 == goal.astype(F32)) & (place >= CAP))
        combine_ref[g + 1] = tail.T.astype(BF16)
        left_ref[g] = jnp.concatenate([own, tail], axis=1).astype(BF16)
    prob = jnp.sum(own * weight8, axis=1, keepdims=True)
    row = iota((ROWS8, 128), 0)
    diagonal = jnp.where(row % PACKED == iota((ROWS8, 128), 1), prob, 0.0).astype(BF16)
    r = iota((ROWS8, ROWS8), 0)
    c = iota((ROWS8, ROWS8), 1)
    lift = one_hot((r // PACKED == c // PACKED) & (r % PACKED == CAP)).astype(BF16)
    spare_ref[...] = product(lift, diagonal).astype(BF16)


def spread(left_ref, x_ref, out_ref):
    rest = x_ref[:, WIDE:]
    for g in range(3):
        cols = pl.ds(g * TAIL, TAIL)
        right = jnp.concatenate([x_ref[:, cols], rest], axis=0)
        out_ref[:, cols] = product(left_ref[g], right).astype(BF16)
    return product(left_ref[0][:, :TOK], x_ref[:, 3 * TAIL : WIDE])


def spread_x_kernel(ids_ref, probs_ref, x_ref, out_ref, left_ref, combine_ref, spare_ref):
    @pl.when(pl.program_id(0) == 0)
    def _():
        tables(ids_ref[...], probs_ref[...], left_ref, combine_ref, spare_ref)

    out_ref[:, 3 * TAIL :] = spread(left_ref, x_ref, out_ref).astype(BF16)


def spread_dy_kernel(left_ref, spare_ref, x_ref, out_ref):
    last = spread(left_ref, x_ref, out_ref)
    out_ref[:, 3 * TAIL :] = last.astype(BF16) + spare_ref[...]


def unpack_masks(main_ref, tail_ref):
    r = iota((SLOTS, ROWS8), 0)
    c = iota((SLOTS, ROWS8), 1)
    same = r // CAP == c // PACKED
    slot = r % CAP
    place = c % PACKED
    main_ref[...] = one_hot(same & (slot == place)).astype(BF16)
    for g in range(3):
        tail = one_hot(same & (place >= CAP) & (slot == (place - CAP) * 3 + g))
        tail_ref[:, g * ROWS8 : (g + 1) * ROWS8] = tail.astype(BF16)


def stacked(packed):
    return jnp.concatenate([packed[:, g * TAIL : (g + 1) * TAIL] for g in range(3)], axis=0)


def unpack(main_ref, tail_ref, packed, rows_ref):
    rows_ref[:, :WIDE] = product(main_ref[...], packed).astype(BF16)
    rows_ref[:, WIDE:] = product(tail_ref[...], stacked(packed)).astype(BF16)


def unpack_all(packed_ref, rows_ref, main_ref, tail_ref):
    unpack_masks(main_ref, tail_ref)
    for j in range(packed_ref.shape[0] // ROWS8):
        rows = rows_ref.at[pl.ds(j * SLOTS, SLOTS)]
        unpack(main_ref, tail_ref, packed_ref[pl.ds(j * ROWS8, ROWS8), :], rows)


def gate_up_kernel(packed_ref, gate_ref, up_ref, rows_ref, parts_ref, main_ref, tail_ref):
    unpack_all(packed_ref, rows_ref, main_ref, tail_ref)
    hidden = gate_ref.shape[1]

    @pl.loop(0, hidden, step=256)
    def _(c):
        rows = rows_ref[...]
        c = pl.multiple_of(c, 256)
        cols = pl.ds(c, 256)
        parts_ref[:, cols] = product(rows, gate_ref[:, cols]).astype(BF16)
        later = pl.ds(pl.multiple_of(hidden + c, 256), 256)
        parts_ref[:, later] = product(rows, up_ref[:, cols]).astype(BF16)


def back_kernel(packed_ref, down_ref, rows_ref, part_ref, prob_ref, main_ref, tail_ref):
    unpack_all(packed_ref, rows_ref, main_ref, tail_ref)
    r = iota((SLOTS, ROWS8), 0)
    c = iota((SLOTS, ROWS8), 1)
    pick = one_hot((r // CAP == c // PACKED) & (c % PACKED == CAP)).astype(BF16)
    mine = iota((SLOTS, 128), 0) % CAP == iota((SLOTS, 128), 1)
    for j in range(packed_ref.shape[0] // ROWS8):
        probs = product(pick, packed_ref[pl.ds(j * ROWS8, ROWS8), 3 * TAIL :])
        prob = jnp.sum(jnp.where(mine, probs, 0.0), axis=1, keepdims=True)
        prob_ref[pl.ds(j * SLOTS, SLOTS), :] = jnp.broadcast_to(prob, (SLOTS, 128)).astype(BF16)

    @pl.loop(0, down_ref.shape[1], step=256)
    def _(c):
        cols = pl.ds(pl.multiple_of(c, 256), 256)
        part_ref[:, cols] = product(rows_ref[...], down_ref[:, cols]).astype(BF16)


def activate_kernel(
    gate_up_ref, back_ref, prob_ref, first_ref, second_ref, weighted_ref, slot_ref
):
    hidden = back_ref.shape[1]
    half = first_ref.shape[0]
    step = 32
    for start in range(0, back_ref.shape[0], step):
        rows = pl.ds(start, step)
        grads_ref = first_ref if start < half else second_ref
        at = pl.ds(start % half, step)
        gate = gate_up_ref[rows, :hidden].astype(F32)
        up = gate_up_ref[rows, hidden:].astype(F32)
        back = back_ref[rows, :].astype(F32)
        weight = prob_ref[rows, :1].astype(F32)
        sigmoid = 1.0 / (1.0 + jnp.exp(-gate))
        swish = gate * sigmoid
        act = swish * up
        grad_act = weight * back
        grad_gate = grad_act * up * sigmoid * (1.0 + gate * (1.0 - sigmoid))
        grads_ref[at, :hidden] = grad_gate.astype(BF16)
        grads_ref[at, hidden:] = (grad_act * swish).astype(BF16)
        weighted_ref[rows, :] = (weight * act).astype(BF16)
        slot = jnp.sum(back * act, axis=1, keepdims=True)
        mine = (start + iota((step, 128), 0)) % CAP == iota((step, 128), 1)
        slot_ref[rows, :] = jnp.where(mine, slot, 0.0).astype(BF16)


def pack(rows_t, out_ref):
    r = iota((ROWS8, SLOTS), 0)
    c = iota((ROWS8, SLOTS), 1)
    same = r // PACKED == c // CAP
    place = r % PACKED
    slot = c % CAP
    main = one_hot(same & (slot == place)).astype(BF16)
    rest = rows_t[WIDE:]
    for g in range(3):
        tail = one_hot(same & (place >= CAP) & (slot == (place - CAP) * 3 + g)).astype(BF16)
        left = jnp.concatenate([main, tail], axis=1)
        right = jnp.concatenate([rows_t[g * TAIL : (g + 1) * TAIL], rest], axis=1)
        out_ref[:, g * TAIL : (g + 1) * TAIL] = product_t(left, right).astype(BF16)
    return product_t(main, rows_t[3 * TAIL : WIDE])


def row_grads(first_ref, second_ref, gate_ref, up_ref):
    hidden = gate_ref.shape[1]
    grads = jnp.concatenate([first_ref[...], second_ref[...]], axis=0)
    rows = product_t(gate_ref[...], grads[:, :hidden])
    return (rows + product_t(up_ref[...], grads[:, hidden:])).astype(BF16)


def row_grad_own_kernel(where_ref, first_ref, second_ref, gate_ref, up_ref, slot_ref, out_ref):
    last = pack(row_grads(first_ref, second_ref, gate_ref, up_ref), out_ref)
    r = iota((ROWS8, SLOTS), 0)
    c = iota((ROWS8, SLOTS), 1)
    lift = one_hot((r // PACKED == c // CAP) & (r % PACKED == CAP)).astype(BF16)
    out_ref[:, 3 * TAIL :] = (last + product(lift, slot_ref[...])).astype(BF16)


def row_grad_kernel(where_ref, first_ref, second_ref, gate_ref, up_ref, before_ref, out_ref):
    last = pack(row_grads(first_ref, second_ref, gate_ref, up_ref), out_ref)
    out_ref[:, 3 * TAIL :] = last.astype(BF16)


def combine_kernel(ids_ref, left_ref, combine_ref, packed_ref, out_ref, probs_ref, slot_ref):
    step = pl.program_id(0)
    packed = packed_ref[...]
    out_ref[:, :WIDE] = product(combine_ref[0], packed).astype(BF16)
    tails = jnp.concatenate([combine_ref[g + 1] for g in range(3)], axis=1)
    out_ref[:, WIDE:] = product(tails, stacked(packed)).astype(BF16)
    spare = packed[:, 3 * TAIL :].astype(F32)

    @pl.when(step == 0)
    def _():
        slot_ref[...] = spare

    @pl.when(step > 0)
    def _():
        slot_ref[...] += spare

    @pl.when(step == pl.num_programs(0) - 1)
    def _():
        row = iota((ROWS8, 128), 0)
        slots = jnp.where(row % PACKED == CAP, slot_ref[...], 0.0).astype(BF16)
        r = iota((ROWS8, ROWS8), 0)
        c = iota((ROWS8, ROWS8), 1)
        group = one_hot(r // PACKED == c // PACKED).astype(BF16)
        wide = product(group, slots)
        mine = iota((ROWS8, 128), 1) == row % PACKED
        column = jnp.sum(jnp.where(mine, wide, 0.0), axis=1, keepdims=True)
        value = (left_ref[0, :, :TOK].astype(F32) * column).astype(BF16)
        gather = one_hot(iota((EXPERTS, ROWS8), 1) // PACKED == iota((EXPERTS, ROWS8), 0))
        table = product(gather.astype(BF16), value)
        expert = iota((EXPERTS, TOK), 0)
        for k in range(TOP):
            hit = ids_ref[k : k + 1, :] == expert
            found = jnp.sum(jnp.where(hit, table, 0.0), axis=0, keepdims=True)
            probs_ref[k : k + 1, :] = found


def call(kernel, grid, ins, outs, scratch=(), flops=0, moved=0, prefetch=0, aliases=None):
    return pl.pallas_call(
        kernel,
        grid_spec=pltpu.PrefetchScalarGridSpec(
            num_scalar_prefetch=prefetch,
            grid=(grid,),
            in_specs=ins,
            out_specs=[s for s, _, _ in outs],
            scratch_shapes=list(scratch),
        ),
        out_shape=[place(shape, kind) for _, (shape, kind), place in outs],
        compiler_params=pltpu.CompilerParams(
            dimension_semantics=("arbitrary",), vmem_limit_bytes=24 * MIB
        ),
        input_output_aliases=aliases or {},
        cost_estimate=pl.CostEstimate(flops=flops, bytes_accessed=moved, transcendentals=0),
    )


def whole(*shape):
    return pl.BlockSpec(shape, lambda *i: (0,) * len(shape))


def rows_of(rows, cols):
    return pl.BlockSpec((rows, cols), lambda i, *_: (i, 0))


def cols_of(rows, cols):
    return pl.BlockSpec((rows, cols), lambda i, *_: (0, i))


NEAR = pl.BlockSpec(memory_space=pltpu.VMEM)


def on_device(hidden_in, grad_out, route_ids, route_probs, w_gate, w_up, w_down):
    sp_count = lax.axis_size("sp")
    pieces = lax.axis_size("ep") * sp_count
    hidden = w_gate.shape[2]
    model = hidden_in.shape[1]
    all_rows = pieces * CAP
    packed8 = pieces * PACKED
    gate_weight, up_weight, down_weight = w_gate[0], w_up[0], w_down[0]
    ids, probs = route_ids.T, route_probs.T
    far, near = pltpu.HBM, jax.ShapeDtypeStruct
    tie = lax.optimization_barrier
    packet = (rows_of(ROWS8, WIDE), ((packed8, WIDE), BF16), far)
    x_send, left, combine, spare = call(
        spread_x_kernel,
        sp_count,
        [whole(TOP, TOK), whole(TOP, TOK), cols_of(TOK, QUARTER)],
        [
            packet,
            (whole(3, ROWS8, ROWS8), ((3, ROWS8, ROWS8), BF16), far),
            (whole(4, TOK, ROWS8), ((4, TOK, ROWS8), BF16), far),
            (whole(ROWS8, 128), ((ROWS8, 128), BF16), far),
        ],
        flops=2 * packed8 * WIDE * 256,
        moved=2 * (packed8 * WIDE + TOK * model),
    )(ids, probs, hidden_in)
    (dy_send,) = call(
        spread_dy_kernel,
        sp_count,
        [whole(3, ROWS8, ROWS8), whole(ROWS8, 128), cols_of(TOK, QUARTER)],
        [packet],
        flops=2 * packed8 * WIDE * 256,
        moved=2 * (packed8 * WIDE + TOK * model),
    )(left, spare, grad_out)

    def exchange(packed):
        pieced = packed.reshape(pieces, PACKED, WIDE)
        moved = lax.all_to_all(pieced, ("sp", "ep"), split_axis=0, concat_axis=0, tiled=True)
        return moved.reshape(packed8, WIDE)

    x_packed = exchange(x_send)
    x_packed, dy_send, down_turned = tie((x_packed, dy_send, tie(down_weight.T)))
    dy_packed = exchange(dy_send)
    masks = (pltpu.VMEM((SLOTS, ROWS8), BF16), pltpu.VMEM((SLOTS, 3 * ROWS8), BF16))
    rows_out = (whole(all_rows, QUARTER), ((all_rows, QUARTER), BF16), far)
    x_rows, gate_up_part = call(
        gate_up_kernel,
        1,
        [NEAR, NEAR, NEAR],
        [rows_out, (whole(all_rows, 2 * hidden), ((all_rows, 2 * hidden), BF16), far)],
        masks,
        flops=4 * all_rows * QUARTER * hidden,
        moved=2 * (packed8 * WIDE + 2 * QUARTER * hidden + all_rows * (QUARTER + 2 * hidden)),
    )(x_packed, gate_weight, up_weight)
    gate_up = lax.psum_scatter(gate_up_part, "sp", scatter_dimension=0, tiled=True)
    dy_packed, _ = tie((dy_packed, gate_up_part))
    dy_rows, back_part, prob_rows = call(
        back_kernel,
        1,
        [NEAR, NEAR],
        [
            rows_out,
            (whole(all_rows, hidden), ((all_rows, hidden), BF16), far),
            (whole(all_rows, 128), ((all_rows, 128), BF16), far),
        ],
        masks,
        flops=32 * 2 * all_rows * QUARTER * hidden,
        moved=2 * (packed8 * WIDE + QUARTER * hidden + all_rows * (QUARTER + hidden)),
    )(dy_packed, down_turned)
    back_part, gate_up = tie((back_part, gate_up))
    back = lax.psum_scatter(back_part, "sp", scatter_dimension=0, tiled=True)
    own = lax.axis_index("sp").astype(jnp.int32)
    own_rows = all_rows // sp_count
    half = own_rows // 2
    prob_own = lax.dynamic_slice_in_dim(prob_rows, own * own_rows, own_rows, axis=0)
    first, second, weighted_own, slot_own = call(
        activate_kernel,
        1,
        [NEAR, NEAR, NEAR],
        [
            (whole(half, 2 * hidden), ((half, 2 * hidden), BF16), far),
            (whole(half, 2 * hidden), ((half, 2 * hidden), BF16), far),
            (whole(own_rows, hidden), ((own_rows, hidden), BF16), far),
            (whole(own_rows, 128), ((own_rows, 128), BF16), near),
        ],
        flops=20 * own_rows * hidden,
        moved=12 * own_rows * hidden,
    )(gate_up, back, prob_own)
    upward = [(i, (i + 1) % sp_count) for i in range(sp_count)]
    downward = [(i, (i - 1) % sp_count) for i in range(sp_count)]
    below_first = lax.ppermute(first, "sp", upward)
    above_second = lax.ppermute(second, "sp", downward)
    below_second = lax.ppermute(second, "sp", upward)
    above_first = lax.ppermute(first, "sp", downward)
    landing = (
        pl.BlockSpec((ROWS8, WIDE), lambda i, at: (at[0], 0)),
        ((packed8, WIDE), BF16),
        far,
    )
    row_cost = dict(
        flops=4 * own_rows * QUARTER * hidden,
        moved=2 * (ROWS8 * WIDE + 2 * QUARTER * hidden + own_rows * 2 * hidden),
        prefetch=1,
    )
    (back_send,) = call(
        row_grad_own_kernel, 1, [NEAR, NEAR, NEAR, NEAR, NEAR], [landing], **row_cost
    )(own.reshape(1), first, second, gate_weight, up_weight, slot_own)

    def row_grad(at, halves, back_send):
        return call(
            row_grad_kernel,
            1,
            [NEAR, NEAR, NEAR, NEAR, pl.BlockSpec(memory_space=pl.ANY)],
            [landing],
            aliases={5: 0},
            **row_cost,
        )(at.reshape(1), *halves, gate_weight, up_weight, back_send)[0]

    below_first, above_second, back_send = tie((below_first, above_second, back_send))
    across_first = lax.ppermute(below_first, "sp", upward)
    across_second = lax.ppermute(above_second, "sp", downward)
    below, above, across = ((own + n) % sp_count for n in (sp_count - 1, 1, 2))
    back_send = row_grad(below, (below_first, below_second), back_send)
    back_send = row_grad(above, (above_first, above_second), back_send)
    across_first, across_second, back_send = tie((across_first, across_second, back_send))
    weighted_own, _, _ = tie((weighted_own, across_first, across_second))
    weighted = lax.all_gather(weighted_own, "sp", axis=0, tiled=True)
    back_send = row_grad(across, (across_first, across_second), back_send)
    back_packed = exchange(back_send)
    pieces_of = (
        (own, 0, first),
        (own, half, second),
        (below, 0, below_first),
        (below, half, below_second),
        (above, 0, above_first),
        (above, half, above_second),
        (across, 0, across_first),
        (across, half, across_second),
    )
    grads_all = jnp.zeros((all_rows, 2 * hidden), BF16)
    grads_all, _ = tie((grads_all, back_send))
    for at, shift, grads in pieces_of:
        grads_all = lax.dynamic_update_slice_in_dim(
            grads_all, grads, at * own_rows + shift, axis=0
        )
    contract_rows = (((0,), (0,)), ((), ()))

    def over_rows(a, b):
        return lax.dot_general(a, b, contract_rows, preferred_element_type=F32).astype(BF16)

    grad_gate_weight = over_rows(x_rows, grads_all[:, :hidden])
    grad_up_weight = over_rows(x_rows, grads_all[:, hidden:])
    grad_down_weight = over_rows(weighted, dy_rows)
    grad_in, grad_probs = call(
        combine_kernel,
        sp_count,
        [whole(TOP, TOK), whole(3, ROWS8, ROWS8), whole(4, TOK, ROWS8), rows_of(ROWS8, WIDE)],
        [
            (cols_of(TOK, QUARTER), ((TOK, model), BF16), near),
            (whole(TOP, TOK), ((TOP, TOK), F32), near),
        ],
        (pltpu.VMEM((ROWS8, 128), F32),),
        flops=2 * packed8 * WIDE * TOK * 2,
        moved=2 * (packed8 * WIDE + TOK * model),
    )(ids, left, combine, back_packed)
    return (
        grad_in,
        grad_gate_weight[None],
        grad_up_weight[None],
        grad_down_weight[None],
        grad_probs.astype(BF16).T,
    )


def solution(mesh):
    placed = (
        P(("ep", "sp"), None),
        P(("ep", "sp"), None),
        P(("ep", "sp"), None),
        P(("ep", "sp"), None),
        P("ep", "sp", None),
        P("ep", "sp", None),
        P("ep", None, "sp"),
    )
    return jax.shard_map(
        on_device,
        mesh=mesh,
        in_specs=placed,
        out_specs=(
            P(("ep", "sp"), None),
            P("ep", "sp", None),
            P("ep", "sp", None),
            P("ep", None, "sp"),
            P(("ep", "sp"), None),
        ),
        check_vma=False,
    )
```

time: 292 us -> 266 us (0.911)
  blocking collectives: 101 us -> 0 us
  starting transfers between devices: 8.65 us -> 36.8 us
  local copies, waits for them, and re-layouts: 13.3 us -> 35 us
  waiting for transfers between devices: 93.6 us -> 110 us
  Pallas kernels: 45.9 us -> 51.3 us
    all_to_all x2 -> x0, blocking collectives: 101 us -> none  [exchange(): lax.all_to_all(pieced, ('sp', 'ep'), split_axis=0, concat_axis=0, tiled=T...]
    all_gather x1 -> x0, waiting for transfers between devices: 38.8 us -> none  [on_device(): grads = lax.all_gather(grads_own, 'sp', axis=0, tiled=True)]
    all_to_all x1 -> x3, waiting for transfers between devices: 19.6 us -> 53 us  [exchange(): lax.all_to_all(pieced, ('sp', 'ep'), split_axis=0, concat_axis=0, tiled=T...]
    reduce_scatter x1, waiting for transfers between devices: 0.02 us -> 26.7 us  [on_device(): back = lax.psum_scatter(back_part, 'sp', scatter_dimension=0, tiled=True)]
    reduce_scatter x1, waiting for transfers between devices: 33.8 us -> 7.95 us  [on_device(): lax.psum_scatter(gate_up_part, 'sp', scatter_dimension=0, tiled=True)]
    all_to_all x1 -> x3, starting transfers between devices: 8.49 us -> 28.7 us  [exchange(): lax.all_to_all(pieced, ('sp', 'ep'), split_axis=0, concat_axis=0, tiled=T...]
    all_gather x1, waiting for transfers between devices: 0.81 us -> 19.7 us  [on_device(): weighted = lax.all_gather(weighted_own, 'sp', axis=0, tiled=True)]
    dynamic_update_slice x0 -> x8, local copies, waits for them, and re-layouts: none -> 11.6 us  [on_device(): lax.dynamic_update_slice_in_dim(grads_all, grads, at * own_rows + shift,...]
  transfers between devices with their start and end apart: 5 -> 12, of which waited for: 4 -> 6; matrix products, arithmetic and copies ran while one was open for 5% -> 14% of each run, Pallas kernels for 10% -> 14%
where the time goes in v2:
time: 266 us; the launch traced here: 265 us
  waiting for transfers between devices  110 us (41%)
  Pallas kernels  51.3 us (19%)
  starting transfers between devices  36.8 us (14%)
  local copies, waits for them, and re-layouts  35 us (13%)
  matrix products  17.6 us (7%)
  between operations  13.9 us (5%)
    all_to_all x3, waiting for transfers between devices, exchange(): lax.all_to_all(pieced, ('sp', 'ep'), split_axis=0, concat_axis=0, tiled=T...  53 us
    all_to_all x3, starting transfers between devices, exchange(): lax.all_to_all(pieced, ('sp', 'ep'), split_axis=0, concat_axis=0, tiled=T...  28.7 us
    reduce_scatter x1, waiting for transfers between devices, on_device(): back = lax.psum_scatter(back_part, 'sp', scatter_dimension=0, tiled=True)  26.7 us
    unnamed x47, local copies, waits for them, and re-layouts  22.3 us
    all_gather x1, waiting for transfers between devices, on_device(): weighted = lax.all_gather(weighted_own, 'sp', axis=0, tiled=True)  19.7 us
    dot_general x3, matrix products, over_rows(): lax.dot_general(a, b, contract_rows, preferred_element_type=F32)  17.6 us
    pallas_call x3, Pallas kernels, row_grad(): call(row_grad_kernel, 1, [NEAR, NEAR, NEAR, NEAR, pl.BlockSpec(memory_spa...  16.3 us
    dynamic_update_slice x8, local copies, waits for them, and re-layouts, on_device(): lax.dynamic_update_slice_in_dim(grads_all, grads, at * own_rows + shift,...  11.6 us
  transfers between devices with their start and end apart: 12, of which 6 were waited for; matrix products, arithmetic and copies ran while one was open for 14% of the time, Pallas kernels for 14%

profile of v2, /device:TPU:1, one launch (start us, length us, event | category | flops | bytes accessed | tf_op | source)
XLA Modules:
  0.0 265.2 jit_solution(6387066211603638928)
XLA Ops:
  10.0 3.6 %shard_map.110 = (bf16[1024,1280]{1,0:T(8,128)(2,1)}, bf16[3,256,256]{2,1,0:T(8,128)(2,1)}, bf16[4,128,256]{2,1,0:T(8,128)(2,1)}, bf16[256,128]{1,0:T(8,128)(2,1)}) custom-call(s32[8,128]{1,0:T(8,128)S(1)} %bitcast.41, f32[8,128]{1,0:T(8,128)S(1)} %bitcast.43, bf16[128,6656]{1,0:T(8,128)(2,1)S(1)} %copy-done.18), custom_call_target="tpu_custom_call" | custom-call | flops 671088640 | bytes 4325376 | tf_op jit(solution)/shard_map/pallas_call | solution.py:298
  13.6 11.9 %all-to-all-start = ((bf16[128,8,1280]{2,1,0:T(8,128)(2,1)}), bf16[128,8,1280]{2,1,0:T(8,128)(2,1)}, u32[]{:S(2)}, u32[]{:S(2)}) async-start(bf16[128,8,1280]{2,1,0:T(8,128)(2,1)} %bitcast.46), calls=%async_computation | async-start | bytes 5242880 | tf_op jit(solution)/shard_map/all_to_all | solution.py:322
  25.5 5.7 %copy.15 = bf16[1,1024,1664]{1,2,0:T(8,128)(2,1)} copy(bf16[1,1024,1664]{2,1,0:T(8,128)(2,1)} %param.13) | data formatting | bytes 6815744 | tf_op args[6]
  31.2 2.9 %shard_map.111 = bf16[1024,1280]{1,0:T(8,128)(2,1)} custom-call(bf16[3,256,256]{2,1,0:T(8,128)(2,1)S(1)} %copy-done.10, bf16[256,128]{1,0:T(8,128)(2,1)S(1)} %copy-done.15, bf16[128,6656]{1,0:T(8,128)(2,1)S(1)} %copy-done.5), custom_call_target="tpu_custom_call" | custom-call | flops 671088640 | bytes 4325376 | tf_op jit(solution)/shard_map/pallas_call | solution.py:311
  34.2 27.1 %all-to-all-done = bf16[128,8,1280]{2,1,0:T(8,128)(2,1)} async-done(((bf16[128,8,1280]{2,1,0:T(8,128)(2,1)}), bf16[128,8,1280]{2,1,0:T(8,128)(2,1)}, u32[]{:S(2)}, u32[]{:S(2)}) %all-to-all-start) | async-done | bytes 2621472 | tf_op jit(solution)/shard_map/all_to_all | solution.py:322
  61.3 5.5 %all-to-all-start.1 = ((bf16[128,8,1280]{2,1,0:T(8,128)(2,1)}), bf16[128,8,1280]{2,1,0:T(8,128)(2,1)}, u32[]{:S(2)}, u32[]{:S(2)}) async-start(bf16[128,8,1280]{2,1,0:T(8,128)(2,1)} %bitcast.45), calls=%async_computation.1 | async-start | bytes 5242880 | tf_op jit(solution)/shard_map/all_to_all | solution.py:322
  66.8 2.0 copy-done.1
  68.8 11.4 %shard_map.112 = (bf16[768,1664]{1,0:T(8,128)(2,1)}, bf16[768,2048]{1,0:T(8,128)(2,1)}) custom-call(bf16[1024,1280]{1,0:T(8,128)(2,1)} %bitcast.4.packed_ref, bf16[1664,1024]{1,0:T(8,128)(2,1)S(1)} %bitcast.29, bf16[1664,1024]{1,0:T(8,128)(2,1)S(1)} %bitcast.34), custom_call_target="tpu_custom_call" | custom-call | flops 5234491392 | bytes 15138816 | tf_op jit(solution)/shard_map/pallas_call | solution.py:330
  80.2 25.9 %all-to-all-done.1 = bf16[128,8,1280]{2,1,0:T(8,128)(2,1)} async-done(((bf16[128,8,1280]{2,1,0:T(8,128)(2,1)}), bf16[128,8,1280]{2,1,0:T(8,128)(2,1)}, u32[]{:S(2)}, u32[]{:S(2)}) %all-to-all-start.1) | async-done | bytes 2621472 | tf_op jit(solution)/shard_map/all_to_all | solution.py:322
  106.2 2.0 copy-done.4
  108.2 8.0 %shard_map.113 = (bf16[768,1664]{1,0:T(8,128)(2,1)}, bf16[768,1024]{1,0:T(8,128)(2,1)}, bf16[768,128]{1,0:T(8,128)(2,1)}) custom-call(bf16[1024,1280]{1,0:T(8,128)(2,1)} %bitcast.8.packed_ref, bf16[1664,1024]{1,0:T(8,128)(2,1)S(1)} %bitcast.40), custom_call_target="tpu_custom_call" | custom-call | flops 83751862272 | bytes 10158080 | tf_op jit(solution)/shard_map/pallas_call | solution.py:341
  116.2 8.0 %reduce-scatter.3.cloned.1.call-done.gate_up_ref = bf16[192,2048]{1,0:T(8,128)(2,1)} async-done(((bf16[768,2048]{1,0:T(8,128)(2,1)}), bf16[192,2048]{1,0:T(8,128)(2,1)}) %reduce-scatter.3.cloned.1.call-update) | async-done | bytes 786448 | tf_op jit(solution)/shard_map/reduce_scatter | solution.py:339
  125.0 26.7 %reduce-scatter.5.cloned.1.call-done.back_ref = bf16[192,1024]{1,0:T(8,128)(2,1)} async-done(((bf16[768,1024]{1,0:T(8,128)(2,1)}), bf16[192,1024]{1,0:T(8,128)(2,1)}) %reduce-scatter.5.cloned.1.call-update) | async-done | bytes 393232 | tf_op jit(solution)/shard_map/reduce_scatter | solution.py:355
  156.3 1.9 collective-permute-start.1
  158.2 2.7 %collective-permute-start.4 = (bf16[96,2048]{1,0:T(8,128)(2,1)}, bf16[96,2048]{1,0:T(8,128)(2,1)}, u32[]{:S(2)}, u32[]{:S(2)}) collective-permute-start(bf16[96,2048]{1,0:T(8,128)(2,1)} %get-tuple-element.47.first_ref), channel_id=1, source_target_pairs={{0,3},{1,0},{2,1},{3,2},{4,7},{5,4},{6,5},{7,6},{8,11},{9,8},{10,9... | collective-permute-start | bytes 1179656 | tf_op jit(solution)/shard_map/ppermute | solution.py:378
  160.9 2.0 copy-done.2
  164.8 4.4 %shard_map.115.before_ref = bf16[1024,1280]{1,0:T(8,128)(2,1)} custom-call(s32[1]{0:T(128)} %bitcast.11.where_ref, bf16[96,2048]{1,0:T(8,128)(2,1)S(1)} %copy-done.8, bf16[96,2048]{1,0:T(8,128)(2,1)S(1)} %copy-done.6, bf16[1664,1024]{1,0:T(8,128)(2,1)S(1)} %bitcast.30, bf16[1664,1024]{1,0:T(8,128)(2,1)S(1)} %bitcast.35, ...), custom_call_target="tpu_custom_call" | custom-call | flops 1308622848 | bytes 8257536 | tf_op jit(solution)/shard_map/pallas_call | solution.py:389
  169.2 2.7 %collective-permute-start.3 = (bf16[96,2048]{1,0:T(8,128)(2,1)}, bf16[96,2048]{1,0:T(8,128)(2,1)}, u32[]{:S(2)}, u32[]{:S(2)}) collective-permute-start(bf16[96,2048]{1,0:T(8,128)(2,1)} %collective-permute-done.1.second_ref), channel_id=1, source_target_pairs={{0,3},{1,0},{2,1},{3,2},{4,7},{5,4},{6,5},{7,6},{8,11},{9,8},{10,9... | collective-permute-start | bytes 1179656 | tf_op jit(solution)/shard_map/ppermute | solution.py:405
  171.9 2.5 collective-permute-done.5.second_ref
  174.4 2.0 copy-done.3
  176.3 5.5 %shard_map.116.before_ref = bf16[1024,1280]{1,0:T(8,128)(2,1)} custom-call(s32[1]{0:T(128)} %bitcast.13.where_ref, bf16[96,2048]{1,0:T(8,128)(2,1)} %collective-permute-done.first_ref, bf16[96,2048]{1,0:T(8,128)(2,1)} %collective-permute-done.5.second_ref, bf16[1664,1024]{1,0:T(8,128)(2,1)S(1)} %bitcast.31, ...), custom_call_target="tpu_custom_call", output_to_operand_aliasing={{}: (5, {})} | custom-call | flops 1308622848 | bytes 8257536 | tf_op jit(solution)/shard_map/pallas_call | solution.py:394
  181.8 5.4 %shard_map.117.before_ref = bf16[1024,1280]{1,0:T(8,128)(2,1)} custom-call(s32[1]{0:T(128)} %bitcast.12.where_ref, bf16[96,2048]{1,0:T(8,128)(2,1)} %collective-permute-done.4.first_ref, bf16[96,2048]{1,0:T(8,128)(2,1)} %collective-permute-done.1.second_ref, bf16[1664,1024]{1,0:T(8,128)(2,1)S(1)} %bitcast.32, ...), custom_call_target="tpu_custom_call", output_to_operand_aliasing={{}: (5, {})} | custom-call | flops 1308622848 | bytes 8257536 | tf_op jit(solution)/shard_map/pallas_call | solution.py:394
  187.2 5.4 %shard_map.118 = bf16[1024,1280]{1,0:T(8,128)(2,1)} custom-call(s32[1]{0:T(128)} %bitcast.2.where_ref, bf16[96,2048]{1,0:T(8,128)(2,1)} %collective-permute-done.2.first_ref, bf16[96,2048]{1,0:T(8,128)(2,1)} %collective-permute-done.3.second_ref, bf16[1664,1024]{1,0:T(8,128)(2,1)S(1)} %bitcast.33, ...), custom_call_target="tpu_custom_call", output_to_operand_aliasing={{}: (5, {})} | custom-call | flops 1308622848 | bytes 8257536 | tf_op jit(solution)/shard_map/pallas_call | solution.py:394
  192.7 11.3 %all-to-all-start.2 = ((bf16[128,8,1280]{2,1,0:T(8,128)(2,1)}), bf16[128,8,1280]{2,1,0:T(8,128)(2,1)S(1)}, u32[]{:S(2)}, u32[]{:S(2)}) async-start(bf16[128,8,1280]{2,1,0:T(8,128)(2,1)} %bitcast.44), calls=%async_computation.4 | async-start | bytes 5242880 | tf_op jit(solution)/shard_map/all_to_all | solution.py:322
  207.0 1.9 constant_dynamic-update-slice_fusion.5
  212.4 1.8 constant_dynamic-update-slice_fusion.2
  215.9 1.8 constant_dynamic-update-slice_fusion
  217.7 6.3 %fusion = bf16[1,1664,1024]{2,1,0:T(8,128)(2,1)} fusion(bf16[768,1664]{1,0:T(8,128)(2,1)S(1)} %copy-done.22, bf16[768,2048]{1,0:T(8,128)(2,1)} %constant_dynamic-update-slice_fusion), kind=kOutput, calls=%fused_computation.3 | convolution fusion | flops 2618949632 | bytes 7536640 | tf_op jit(solution)/shard_map/dot_general | solution.py:433
  224.0 4.2 %fusion.1 = bf16[1,1664,1024]{2,1,0:T(8,128)(2,1)} fusion(bf16[768,1664]{1,0:T(8,128)(2,1)S(1)} %copy-done.22, bf16[768,2048]{1,0:T(8,128)(2,1)S(1)} %copy-done.21), kind=kOutput, calls=%fused_computation.4 | convolution fusion | flops 2618949632 | bytes 7536640 | tf_op jit(solution)/shard_map/dot_general | solution.py:433
  228.2 19.7 %all-gather.2.cloned.1.call-done = bf16[768,1024]{1,0:T(8,128)(2,1)} async-done(((bf16[192,1024]{1,0:T(8,128)(2,1)}), bf16[768,1024]{1,0:T(8,128)(2,1)}) %all-gather.2.cloned.1.call-update) | async-done | bytes 1572880 | tf_op jit(solution)/shard_map/all_gather | solution.py:411
  247.9 7.1 %fusion.2 = bf16[1,1024,1664]{2,1,0:T(8,128)(2,1)} fusion(bf16[768,1024]{1,0:T(8,128)(2,1)} %all-gather.2.cloned.1.call-done, bf16[768,1664]{1,0:T(8,128)(2,1)} %get-tuple-element.61), kind=kOutput, calls=%fused_computation.5 | convolution fusion | flops 2618949632 | bytes 7536640 | tf_op jit(solution)/shard_map/dot_general | solution.py:433
  255.0 3.1 %shard_map.119 = (bf16[128,6656]{1,0:T(8,128)(2,1)}, f32[8,128]{1,0:T(8,128)S(1)}) custom-call(s32[8,128]{1,0:T(8,128)S(1)} %bitcast.42, bf16[3,256,256]{2,1,0:T(8,128)(2,1)S(1)} %copy-done.11, bf16[4,128,256]{2,1,0:T(8,128)(2,1)S(1)} %copy-done.14, bf16[1024,1280]{1,0:T(8,128)(2,1)S(1)} %bitcast.39), custom_call_target="tpu_custom_call" | custom-call | flops 671088640 | bytes 4325376 | tf_op jit(solution)/shard_map/pallas_call | solution.py:438
  (66 shorter events, 19.1 us)
Async XLA Ops:
  7.9 1.5 copy-start.18
  13.6 47.7 %all-to-all-start = ((bf16[128,8,1280]{2,1,0:T(8,128)(2,1)}), bf16[128,8,1280]{2,1,0:T(8,128)(2,1)}, u32[]{:S(2)}, u32[]{:S(2)}) async-start(bf16[128,8,1280]{2,1,0:T(8,128)(2,1)} %bitcast.46), calls=%async_computation | async-start | bytes 5242880 | tf_op jit(solution)/shard_map/all_to_all | solution.py:322
  25.5 5.8 %copy-start.5 = (bf16[128,6656]{1,0:T(8,128)(2,1)S(1)}, bf16[128,6656]{1,0:T(8,128)(2,1)}, u32[]{:S(2)}) copy-start(bf16[128,6656]{1,0:T(8,128)(2,1)} %x_ref.3) | copy-start | bytes 5111812
  25.5 5.7 %copy-start.10 = (bf16[3,256,256]{2,1,0:T(8,128)(2,1)S(1)}, bf16[3,256,256]{2,1,0:T(8,128)(2,1)}, u32[]{:S(2)}) copy-start(bf16[3,256,256]{2,1,0:T(8,128)(2,1)} %get-tuple-element.34.left_ref) | copy-start | bytes 1179652
  25.5 5.7 %copy-start.15 = (bf16[256,128]{1,0:T(8,128)(2,1)S(1)}, bf16[256,128]{1,0:T(8,128)(2,1)}, u32[]{:S(2)}) copy-start(bf16[256,128]{1,0:T(8,128)(2,1)} %get-tuple-element.37.spare_ref) | copy-start | bytes 196612
  34.2 32.7 %copy-start = (bf16[1,1664,1024]{2,1,0:T(8,128)(2,1)S(1)}, bf16[1,1664,1024]{2,1,0:T(8,128)(2,1)}, u32[]{:S(2)}) copy-start(bf16[1,1664,1024]{2,1,0:T(8,128)(2,1)} %param.11) | copy-start | bytes 10223620
  61.3 44.9 %all-to-all-start.1 = ((bf16[128,8,1280]{2,1,0:T(8,128)(2,1)}), bf16[128,8,1280]{2,1,0:T(8,128)(2,1)}, u32[]{:S(2)}, u32[]{:S(2)}) async-start(bf16[128,8,1280]{2,1,0:T(8,128)(2,1)} %bitcast.45), calls=%async_computation.1 | async-start | bytes 5242880 | tf_op jit(solution)/shard_map/all_to_all | solution.py:322
  66.8 57.4 %reduce-scatter.3.cloned.1.call-start = ((), (), s32[]{:S(2)}) async-start(), calls=%async_computation.5 | async-start | bytes 3932160 | tf_op jit(solution)/shard_map/reduce_scatter | solution.py:339
  66.8 2.0 copy-start.1
  80.2 71.6 %reduce-scatter.5.cloned.1.call-start = ((), (), s32[]{:S(2)}) async-start(), calls=%async_computation.6 | async-start | bytes 1966080 | tf_op jit(solution)/shard_map/reduce_scatter | solution.py:355
  106.2 2.0 copy-start.4
  151.8 1.1 copy-start.12
  152.9 1.0 copy-start.13
  155.5 13.7 %collective-permute-start = (bf16[96,2048]{1,0:T(8,128)(2,1)}, bf16[96,2048]{1,0:T(8,128)(2,1)}, u32[]{:S(2)}, u32[]{:S(2)}) collective-permute-start(bf16[96,2048]{1,0:T(8,128)(2,1)} %get-tuple-element.47.first_ref), channel_id=1, source_target_pairs={{0,1},{1,2},{2,3},{3,0},{4,5},{5,6},{6,7},{7,4},{8,9},{9,10},{10,1... | collective-permute-start | bytes 1179656 | tf_op jit(solution)/shard_map/ppermute | solution.py:375
  156.3 12.9 %collective-permute-start.1 = (bf16[96,2048]{1,0:T(8,128)(2,1)}, bf16[96,2048]{1,0:T(8,128)(2,1)}, u32[]{:S(2)}, u32[]{:S(2)}) collective-permute-start(bf16[96,2048]{1,0:T(8,128)(2,1)} %get-tuple-element.48.second_ref), channel_id=1, source_target_pairs={{0,3},{1,0},{2,1},{3,2},{4,7},{5,4},{6,5},{7,6},{8,11},{9,8},{10,9... | collective-permute-start | bytes 1179656 | tf_op jit(solution)/shard_map/ppermute | solution.py:376
  158.2 16.2 %collective-permute-start.5 = (bf16[96,2048]{1,0:T(8,128)(2,1)}, bf16[96,2048]{1,0:T(8,128)(2,1)}, u32[]{:S(2)}, u32[]{:S(2)}) collective-permute-start(bf16[96,2048]{1,0:T(8,128)(2,1)} %get-tuple-element.48.second_ref), channel_id=1, source_target_pairs={{0,1},{1,2},{2,3},{3,0},{4,5},{5,6},{6,7},{7,4},{8,9},{9,10},{10,1... | collective-permute-start | bytes 1179656 | tf_op jit(solution)/shard_map/ppermute | solution.py:377
  158.2 23.6 %collective-permute-start.4 = (bf16[96,2048]{1,0:T(8,128)(2,1)}, bf16[96,2048]{1,0:T(8,128)(2,1)}, u32[]{:S(2)}, u32[]{:S(2)}) collective-permute-start(bf16[96,2048]{1,0:T(8,128)(2,1)} %get-tuple-element.47.first_ref), channel_id=1, source_target_pairs={{0,3},{1,0},{2,1},{3,2},{4,7},{5,4},{6,5},{7,6},{8,11},{9,8},{10,9... | collective-permute-start | bytes 1179656 | tf_op jit(solution)/shard_map/ppermute | solution.py:378
  160.9 2.0 copy-start.2
  162.8 1.0 copy-start.6
  169.2 18.0 %collective-permute-start.2 = (bf16[96,2048]{1,0:T(8,128)(2,1)}, bf16[96,2048]{1,0:T(8,128)(2,1)}, u32[]{:S(2)}, u32[]{:S(2)}) collective-permute-start(bf16[96,2048]{1,0:T(8,128)(2,1)} %collective-permute-done.first_ref), channel_id=1, source_target_pairs={{0,1},{1,2},{2,3},{3,0},{4,5},{5,6},{6,7},{7,4},{8,9},{9,10},{10,1... | collective-permute-start | bytes 1179656 | tf_op jit(solution)/shard_map/ppermute | solution.py:404
  169.2 18.0 %collective-permute-start.3 = (bf16[96,2048]{1,0:T(8,128)(2,1)}, bf16[96,2048]{1,0:T(8,128)(2,1)}, u32[]{:S(2)}, u32[]{:S(2)}) collective-permute-start(bf16[96,2048]{1,0:T(8,128)(2,1)} %collective-permute-done.1.second_ref), channel_id=1, source_target_pairs={{0,3},{1,0},{2,1},{3,2},{4,7},{5,4},{6,5},{7,6},{8,11},{9,8},{10,9... | collective-permute-start | bytes 1179656 | tf_op jit(solution)/shard_map/ppermute | solution.py:405
  174.4 2.0 copy-start.3
  192.7 11.8 %copy-start.9 = (bf16[96,2048]{1,0:T(8,128)(2,1)S(1)}, bf16[96,2048]{1,0:T(8,128)(2,1)}, u32[]{:S(2)}) copy-start(bf16[96,2048]{1,0:T(8,128)(2,1)} %get-tuple-element.47.first_ref) | copy-start | bytes 1179652
  192.7 62.3 %all-to-all-start.2 = ((bf16[128,8,1280]{2,1,0:T(8,128)(2,1)}), bf16[128,8,1280]{2,1,0:T(8,128)(2,1)S(1)}, u32[]{:S(2)}, u32[]{:S(2)}) async-start(bf16[128,8,1280]{2,1,0:T(8,128)(2,1)} %bitcast.44), calls=%async_computation.4 | async-start | bytes 5242880 | tf_op jit(solution)/shard_map/all_to_all | solution.py:322
  204.0 2.2 copy-start.7
  204.0 43.9 %all-gather.2.cloned.1.call-start = ((), (), s32[]{:S(2)}) async-start(), calls=%async_computation.7 | async-start | bytes 1966080 | tf_op jit(solution)/shard_map/all_gather | solution.py:411
  204.5 1.7 copy-start.20
  206.2 11.5 %copy-start.22 = (bf16[768,1664]{1,0:T(8,128)(2,1)S(1)}, bf16[768,1664]{1,0:T(8,128)(2,1)}, u32[]{:S(2)}) copy-start(bf16[768,1664]{1,0:T(8,128)(2,1)} %get-tuple-element.57) | copy-start | bytes 7667716
  217.7 6.3 %copy-start.21 = (bf16[768,2048]{1,0:T(8,128)(2,1)S(1)}, bf16[768,2048]{1,0:T(8,128)(2,1)}, u32[]{:S(2)}) copy-start(bf16[768,2048]{1,0:T(8,128)(2,1)} %constant_dynamic-update-slice_fusion) | copy-start | bytes 9437188
  247.9 7.1 %copy-start.11 = (bf16[3,256,256]{2,1,0:T(8,128)(2,1)S(1)}, bf16[3,256,256]{2,1,0:T(8,128)(2,1)}, u32[]{:S(2)}) copy-start(bf16[3,256,256]{2,1,0:T(8,128)(2,1)} %get-tuple-element.34.left_ref) | copy-start | bytes 1179652
  247.9 7.1 %copy-start.14 = (bf16[4,128,256]{2,1,0:T(8,128)(2,1)S(1)}, bf16[4,128,256]{2,1,0:T(8,128)(2,1)}, u32[]{:S(2)}) copy-start(bf16[4,128,256]{2,1,0:T(8,128)(2,1)} %get-tuple-element.35.combine_ref) | copy-start | bytes 786436
  247.9 7.1 %copy-start.17 = (s32[128,8]{0,1:T(8,128)S(1)}, s32[128,8]{0,1:T(8,128)}, u32[]{:S(2)}) copy-start(s32[128,8]{0,1:T(8,128)} %param.9) | copy-start | bytes 12292
  (3 other events, 2.4 us)
Sparse Core Ops, SparseCore 0:
  80.3 43.8 reduce-scatter.2
  127.2 24.5 reduce-scatter.4
  206.5 41.3 all-gather.1

commit v3 on v2

--- a/solution.py
+++ b/solution.py
@@ -1,3 +1,5 @@
+import functools
+
 import jax
 import jax.numpy as jnp
 from jax import lax
@@ -113,104 +115,173 @@
 
 
 def unpack_all(packed_ref, rows_ref, main_ref, tail_ref):
-    unpack_masks(main_ref, tail_ref)
     for j in range(packed_ref.shape[0] // ROWS8):
         rows = rows_ref.at[pl.ds(j * SLOTS, SLOTS)]
         unpack(main_ref, tail_ref, packed_ref[pl.ds(j * ROWS8, ROWS8), :], rows)
 
 
-def gate_up_kernel(packed_ref, gate_ref, up_ref, rows_ref, parts_ref, main_ref, tail_ref):
-    unpack_all(packed_ref, rows_ref, main_ref, tail_ref)
+def shares(source, held, sems):
+    count = sems.shape[0]
+    rows = held.shape[0] // count
+    parts = [pl.ds(i * rows, rows) for i in range(count)]
+    return [
+        pltpu.make_async_copy(source.at[part], held.at[part], sems.at[i])
+        for i, part in enumerate(parts)
+    ]
+
+
+def start(copies):
+    for copy in copies:
+        copy.start()
+
+
+def finish(copies):
+    for copy in copies:
+        copy.wait()
+
+
+def gate_up_kernel(
+    packed_ref, gate_hbm, up_hbm, rows_ref, parts_ref, gate_ref, up_ref, gate_sem, up_sem, *masks
+):
+    first = pl.program_id(0) == 0
+    weights = ((gate_hbm, gate_ref, gate_sem), (up_hbm, up_ref, up_sem))
+
+    @pl.when(first)
+    def _():
+        for weight in weights:
+            start(shares(*weight))
+        unpack_masks(*masks)
+
+    unpack_all(packed_ref, rows_ref, *masks)
     hidden = gate_ref.shape[1]
-
-    @pl.loop(0, hidden, step=256)
-    def _(c):
-        rows = rows_ref[...]
-        c = pl.multiple_of(c, 256)
-        cols = pl.ds(c, 256)
-        parts_ref[:, cols] = product(rows, gate_ref[:, cols]).astype(BF16)
-        later = pl.ds(pl.multiple_of(hidden + c, 256), 256)
-        parts_ref[:, later] = product(rows, up_ref[:, cols]).astype(BF16)
-
-
-def back_kernel(packed_ref, down_ref, rows_ref, part_ref, prob_ref, main_ref, tail_ref):
-    unpack_all(packed_ref, rows_ref, main_ref, tail_ref)
+    for j, weight in enumerate(weights):
+
+        @pl.when(first)
+        def _(weight=weight):
+            finish(shares(*weight))
+
+        cols = pl.ds(j * hidden, hidden)
+        parts_ref[:, cols] = product(rows_ref[...], weight[1][...]).astype(BF16)
+
+
+def block_of(rows_ref, at, count=SLOTS):
+    return rows_ref[pl.ds(pl.multiple_of(at * SLOTS, SLOTS), count), :]
+
+
+def back_far_kernel(
+    at_ref, packed_ref, down_hbm, rows_ref, first_ref, second_ref, prob_ref, down_ref, sem, *masks
+):
+    copies = shares(down_hbm, down_ref, sem)
+    start(copies)
+    unpack_masks(*masks)
+    unpack_all(packed_ref, rows_ref, *masks)
+    finish(copies)
+    part = product_t(block_of(rows_ref, at_ref[3]), down_ref[...]).astype(BF16)
+    half = first_ref.shape[0]
+    first_ref[...] = part[:half]
+    second_ref[...] = part[half:]
     r = iota((SLOTS, ROWS8), 0)
     c = iota((SLOTS, ROWS8), 1)
     pick = one_hot((r // CAP == c // PACKED) & (c % PACKED == CAP)).astype(BF16)
     mine = iota((SLOTS, 128), 0) % CAP == iota((SLOTS, 128), 1)
-    for j in range(packed_ref.shape[0] // ROWS8):
-        probs = product(pick, packed_ref[pl.ds(j * ROWS8, ROWS8), 3 * TAIL :])
-        prob = jnp.sum(jnp.where(mine, probs, 0.0), axis=1, keepdims=True)
-        prob_ref[pl.ds(j * SLOTS, SLOTS), :] = jnp.broadcast_to(prob, (SLOTS, 128)).astype(BF16)
-
-    @pl.loop(0, down_ref.shape[1], step=256)
-    def _(c):
-        cols = pl.ds(pl.multiple_of(c, 256), 256)
-        part_ref[:, cols] = product(rows_ref[...], down_ref[:, cols]).astype(BF16)
+    own8 = pl.ds(pl.multiple_of(at_ref[0] * ROWS8, ROWS8), ROWS8)
+    probs = product(pick, packed_ref[own8, 3 * TAIL :])
+    prob = jnp.sum(jnp.where(mine, probs, 0.0), axis=1, keepdims=True)
+    prob_ref[...] = jnp.broadcast_to(prob, (SLOTS, 128)).astype(BF16)
+
+
+def back_near_kernel(at_ref, rows_ref, down_hbm, own_ref, below_ref, above_ref, down_ref, sem):
+    copies = shares(down_hbm, down_ref, sem)
+    start(copies)
+    finish(copies)
+    blocks = [block_of(rows_ref, at_ref[j]) for j in range(3)]
+    part = product_t(jnp.concatenate(blocks, axis=0), down_ref[...]).astype(BF16)
+    own_ref[...] = part[:SLOTS]
+    below_ref[...] = part[SLOTS : 2 * SLOTS]
+    above_ref[...] = part[2 * SLOTS :]
+
+
+def join_kernel(below_ref, above_ref, first_ref, second_ref, below_out, above_out):
+    half = first_ref.shape[0]
+    below_out[:half] = below_ref[:half]
+    below_out[half:] = (below_ref[half:].astype(F32) + second_ref[...].astype(F32)).astype(BF16)
+    above_out[:half] = (above_ref[:half].astype(F32) + first_ref[...].astype(F32)).astype(BF16)
+    above_out[half:] = above_ref[half:]
 
 
 def activate_kernel(
-    gate_up_ref, back_ref, prob_ref, first_ref, second_ref, weighted_ref, slot_ref
+    gate_up_ref, own_ref, left_ref, right_ref, prob_ref, first_ref, second_ref, weighted_ref, slot_ref
 ):
-    hidden = back_ref.shape[1]
+    rows, hidden = own_ref.shape
     half = first_ref.shape[0]
     step = 32
-    for start in range(0, back_ref.shape[0], step):
-        rows = pl.ds(start, step)
+    for start in range(0, rows, step):
+        at = pl.ds(start, step)
         grads_ref = first_ref if start < half else second_ref
-        at = pl.ds(start % half, step)
-        gate = gate_up_ref[rows, :hidden].astype(F32)
-        up = gate_up_ref[rows, hidden:].astype(F32)
-        back = back_ref[rows, :].astype(F32)
-        weight = prob_ref[rows, :1].astype(F32)
+        to = pl.ds(start % half, step)
+        gate = gate_up_ref[at, :hidden].astype(F32)
+        up = gate_up_ref[at, hidden:].astype(F32)
+        back = own_ref[at, :].astype(F32) + left_ref[at, :].astype(F32)
+        back = back + right_ref[at, :].astype(F32)
+        weight = prob_ref[at, :1].astype(F32)
         sigmoid = 1.0 / (1.0 + jnp.exp(-gate))
         swish = gate * sigmoid
         act = swish * up
         grad_act = weight * back
         grad_gate = grad_act * up * sigmoid * (1.0 + gate * (1.0 - sigmoid))
-        grads_ref[at, :hidden] = grad_gate.astype(BF16)
-        grads_ref[at, hidden:] = (grad_act * swish).astype(BF16)
-        weighted_ref[rows, :] = (weight * act).astype(BF16)
+        grads_ref[to, :hidden] = grad_gate.astype(BF16)
+        grads_ref[to, hidden:] = (grad_act * swish).astype(BF16)
+        weighted_ref[at, :] = (weight * act).astype(BF16)
         slot = jnp.sum(back * act, axis=1, keepdims=True)
         mine = (start + iota((step, 128), 0)) % CAP == iota((step, 128), 1)
-        slot_ref[rows, :] = jnp.where(mine, slot, 0.0).astype(BF16)
-
-
-def pack(rows_t, out_ref):
+        slot_ref[at, :] = jnp.where(mine, slot, 0.0).astype(BF16)
+
+
+def pack(rows, out_ref):
     r = iota((ROWS8, SLOTS), 0)
     c = iota((ROWS8, SLOTS), 1)
     same = r // PACKED == c // CAP
     place = r % PACKED
     slot = c % CAP
     main = one_hot(same & (slot == place)).astype(BF16)
-    rest = rows_t[WIDE:]
+    rest = rows[:, WIDE:]
     for g in range(3):
         tail = one_hot(same & (place >= CAP) & (slot == (place - CAP) * 3 + g)).astype(BF16)
         left = jnp.concatenate([main, tail], axis=1)
-        right = jnp.concatenate([rows_t[g * TAIL : (g + 1) * TAIL], rest], axis=1)
-        out_ref[:, g * TAIL : (g + 1) * TAIL] = product_t(left, right).astype(BF16)
-    return product_t(main, rows_t[3 * TAIL : WIDE])
-
-
-def row_grads(first_ref, second_ref, gate_ref, up_ref):
+        right = jnp.concatenate([rows[:, g * TAIL : (g + 1) * TAIL], rest], axis=0)
+        out_ref[:, g * TAIL : (g + 1) * TAIL] = product(left, right).astype(BF16)
+    return product(main, rows[:, 3 * TAIL : WIDE])
+
+
+def row_grad_kernel(blocks, own, at_ref, *refs):
+    grads_refs, rest = refs[:-9], refs[-9:]
+    gate_hbm, up_hbm, extra_ref, out_ref, rows_ref, gate_ref, up_ref, gate_sem, up_sem = rest
     hidden = gate_ref.shape[1]
-    grads = jnp.concatenate([first_ref[...], second_ref[...]], axis=0)
-    rows = product_t(gate_ref[...], grads[:, :hidden])
-    return (rows + product_t(up_ref[...], grads[:, hidden:])).astype(BF16)
-
-
-def row_grad_own_kernel(where_ref, first_ref, second_ref, gate_ref, up_ref, slot_ref, out_ref):
-    last = pack(row_grads(first_ref, second_ref, gate_ref, up_ref), out_ref)
-    r = iota((ROWS8, SLOTS), 0)
-    c = iota((ROWS8, SLOTS), 1)
-    lift = one_hot((r // PACKED == c // CAP) & (r % PACKED == CAP)).astype(BF16)
-    out_ref[:, 3 * TAIL :] = (last + product(lift, slot_ref[...])).astype(BF16)
-
-
-def row_grad_kernel(where_ref, first_ref, second_ref, gate_ref, up_ref, before_ref, out_ref):
-    last = pack(row_grads(first_ref, second_ref, gate_ref, up_ref), out_ref)
-    out_ref[:, 3 * TAIL :] = last.astype(BF16)
+    step = pl.program_id(0)
+
+    @pl.when(step == 0)
+    def _():
+        gate_copies = shares(gate_hbm, gate_ref, gate_sem)
+        up_copies = shares(up_hbm, up_ref, up_sem)
+        start(gate_copies)
+        start(up_copies)
+        grads = jnp.concatenate([r[...] for r in grads_refs], axis=0)
+        finish(gate_copies)
+        rows = product_t(grads[:, :hidden], gate_ref[...])
+        finish(up_copies)
+        rows_ref[...] = (rows + product_t(grads[:, hidden:], up_ref[...])).astype(BF16)
+
+    for j in range(blocks):
+
+        @pl.when(step == j)
+        def _(j=j):
+            spare = pack(rows_ref[j * SLOTS : (j + 1) * SLOTS, :], out_ref)
+            if own:
+                r = iota((ROWS8, SLOTS), 0)
+                c = iota((ROWS8, SLOTS), 1)
+                lift = one_hot((r // PACKED == c // CAP) & (r % PACKED == CAP)).astype(BF16)
+                spare = spare + product(lift, extra_ref[...])
+            out_ref[:, 3 * TAIL :] = spare.astype(BF16)
 
 
 def combine_kernel(ids_ref, left_ref, combine_ref, packed_ref, out_ref, probs_ref, slot_ref):
@@ -249,7 +320,9 @@
             probs_ref[k : k + 1, :] = found
 
 
-def call(kernel, grid, ins, outs, scratch=(), flops=0, moved=0, prefetch=0, aliases=None):
+def call(
+    kernel, grid, ins, outs, scratch=(), flops=0, moved=0, prefetch=0, aliases=None, limit=24
+):
     return pl.pallas_call(
         kernel,
         grid_spec=pltpu.PrefetchScalarGridSpec(
@@ -261,7 +334,7 @@
         ),
         out_shape=[place(shape, kind) for _, (shape, kind), place in outs],
         compiler_params=pltpu.CompilerParams(
-            dimension_semantics=("arbitrary",), vmem_limit_bytes=24 * MIB
+            dimension_semantics=("arbitrary",), vmem_limit_bytes=limit * MIB
         ),
         input_output_aliases=aliases or {},
         cost_estimate=pl.CostEstimate(flops=flops, bytes_accessed=moved, transcendentals=0),
@@ -280,7 +353,7 @@
     return pl.BlockSpec((rows, cols), lambda i, *_: (0, i))
 
 
-NEAR = pl.BlockSpec(memory_space=pltpu.VMEM)
+ANY = pl.BlockSpec(memory_space=pl.ANY)
 
 
 def on_device(hidden_in, grad_out, route_ids, route_probs, w_gate, w_up, w_down):
@@ -292,6 +365,11 @@
     packed8 = pieces * PACKED
     gate_weight, up_weight, down_weight = w_gate[0], w_up[0], w_down[0]
     ids, probs = route_ids.T, route_probs.T
+
+    def in_hbm(array):
+        return pltpu.with_memory_space_constraint(array, pltpu.HBM)
+
+    hidden_in, grad_out = in_hbm(hidden_in), in_hbm(grad_out)
     far, near = pltpu.HBM, jax.ShapeDtypeStruct
     tie = lax.optimization_barrier
     packet = (rows_of(ROWS8, WIDE), ((packed8, WIDE), BF16), far)
@@ -307,7 +385,7 @@
         ],
         flops=2 * packed8 * WIDE * 256,
         moved=2 * (packed8 * WIDE + TOK * model),
-    )(ids, probs, hidden_in)
+    )(in_hbm(ids), in_hbm(probs), hidden_in)
     (dy_send,) = call(
         spread_dy_kernel,
         sp_count,
@@ -315,102 +393,125 @@
         [packet],
         flops=2 * packed8 * WIDE * 256,
         moved=2 * (packed8 * WIDE + TOK * model),
-    )(left, spare, grad_out)
+    )(in_hbm(left), in_hbm(spare), grad_out)
 
     def exchange(packed):
         pieced = packed.reshape(pieces, PACKED, WIDE)
         moved = lax.all_to_all(pieced, ("sp", "ep"), split_axis=0, concat_axis=0, tiled=True)
         return moved.reshape(packed8, WIDE)
 
+    gate_weight, up_weight, down_weight = map(in_hbm, (gate_weight, up_weight, down_weight))
     x_packed = exchange(x_send)
-    x_packed, dy_send, down_turned = tie((x_packed, dy_send, tie(down_weight.T)))
+    x_packed, dy_send = tie((in_hbm(x_packed), dy_send))
     dy_packed = exchange(dy_send)
     masks = (pltpu.VMEM((SLOTS, ROWS8), BF16), pltpu.VMEM((SLOTS, 3 * ROWS8), BF16))
-    rows_out = (whole(all_rows, QUARTER), ((all_rows, QUARTER), BF16), far)
+    two_weights = (pltpu.VMEM((QUARTER, hidden), BF16),) * 2 + (pltpu.SemaphoreType.DMA((4,)),) * 2
+    down_space = (pltpu.VMEM((hidden, QUARTER), BF16), pltpu.SemaphoreType.DMA((4,)))
+    some_rows, some8 = all_rows // 2, packed8 // 2
     x_rows, gate_up_part = call(
         gate_up_kernel,
-        1,
-        [NEAR, NEAR, NEAR],
-        [rows_out, (whole(all_rows, 2 * hidden), ((all_rows, 2 * hidden), BF16), far)],
-        masks,
+        2,
+        [rows_of(some8, WIDE), ANY, ANY],
+        [
+            (rows_of(some_rows, QUARTER), ((all_rows, QUARTER), BF16), far),
+            (rows_of(some_rows, 2 * hidden), ((all_rows, 2 * hidden), BF16), far),
+        ],
+        two_weights + masks,
         flops=4 * all_rows * QUARTER * hidden,
         moved=2 * (packed8 * WIDE + 2 * QUARTER * hidden + all_rows * (QUARTER + 2 * hidden)),
     )(x_packed, gate_weight, up_weight)
     gate_up = lax.psum_scatter(gate_up_part, "sp", scatter_dimension=0, tiled=True)
-    dy_packed, _ = tie((dy_packed, gate_up_part))
-    dy_rows, back_part, prob_rows = call(
-        back_kernel,
-        1,
-        [NEAR, NEAR],
-        [
-            rows_out,
-            (whole(all_rows, hidden), ((all_rows, hidden), BF16), far),
-            (whole(all_rows, 128), ((all_rows, 128), BF16), far),
-        ],
-        masks,
-        flops=32 * 2 * all_rows * QUARTER * hidden,
-        moved=2 * (packed8 * WIDE + QUARTER * hidden + all_rows * (QUARTER + hidden)),
-    )(dy_packed, down_turned)
-    back_part, gate_up = tie((back_part, gate_up))
-    back = lax.psum_scatter(back_part, "sp", scatter_dimension=0, tiled=True)
     own = lax.axis_index("sp").astype(jnp.int32)
     own_rows = all_rows // sp_count
     half = own_rows // 2
-    prob_own = lax.dynamic_slice_in_dim(prob_rows, own * own_rows, own_rows, axis=0)
+    places = (own + jnp.array([0, sp_count - 1, 1, 2], jnp.int32)) % sp_count
+    upward = [(i, (i + 1) % sp_count) for i in range(sp_count)]
+    downward = [(i, (i - 1) % sp_count) for i in range(sp_count)]
+
+    def both_ways(up, down):
+        return lax.ppermute(up, "sp", upward), lax.ppermute(down, "sp", downward)
+
+    dy_packed, _ = tie((dy_packed, gate_up_part))
+    piece = ((half, hidden), BF16)
+    block = ((own_rows, hidden), BF16)
+    dy_rows, far_first, far_second, prob_own = call(
+        back_far_kernel,
+        1,
+        [whole(packed8, WIDE), ANY],
+        [
+            (whole(all_rows, QUARTER), ((all_rows, QUARTER), BF16), far),
+            (whole(*piece[0]), piece, far),
+            (whole(*piece[0]), piece, far),
+            (whole(own_rows, 128), ((own_rows, 128), BF16), far),
+        ],
+        down_space + masks,
+        flops=32 * 2 * all_rows * QUARTER * hidden,
+        moved=2 * (packed8 * WIDE + QUARTER * hidden + all_rows * QUARTER),
+        prefetch=1,
+    )(places, dy_packed, down_weight)
+    far_first, far_second = both_ways(far_first, far_second)
+    back_own, back_below, back_above = call(
+        back_near_kernel,
+        1,
+        [whole(all_rows, QUARTER), ANY],
+        [(whole(*block[0]), block, far)] * 3,
+        down_space,
+        flops=2 * 3 * own_rows * QUARTER * hidden,
+        moved=2 * (QUARTER * hidden + all_rows * QUARTER + 3 * own_rows * hidden),
+        prefetch=1,
+    )(places, in_hbm(dy_rows), down_weight)
+    back_below, back_above = call(
+        join_kernel,
+        1,
+        [whole(*block[0])] * 2 + [whole(*piece[0])] * 2,
+        [(whole(*block[0]), block, far)] * 2,
+        moved=2 * 5 * own_rows * hidden,
+    )(in_hbm(back_below), in_hbm(back_above), far_first, far_second)
+    left_part, right_part = both_ways(back_above, back_below)
     first, second, weighted_own, slot_own = call(
         activate_kernel,
         1,
-        [NEAR, NEAR, NEAR],
+        [whole(own_rows, 2 * hidden)] + [whole(*block[0])] * 3 + [whole(own_rows, 128)],
         [
             (whole(half, 2 * hidden), ((half, 2 * hidden), BF16), far),
             (whole(half, 2 * hidden), ((half, 2 * hidden), BF16), far),
             (whole(own_rows, hidden), ((own_rows, hidden), BF16), far),
-            (whole(own_rows, 128), ((own_rows, 128), BF16), near),
+            (whole(own_rows, 128), ((own_rows, 128), BF16), far),
         ],
         flops=20 * own_rows * hidden,
         moved=12 * own_rows * hidden,
-    )(gate_up, back, prob_own)
-    upward = [(i, (i + 1) % sp_count) for i in range(sp_count)]
-    downward = [(i, (i - 1) % sp_count) for i in range(sp_count)]
-    below_first = lax.ppermute(first, "sp", upward)
-    above_second = lax.ppermute(second, "sp", downward)
-    below_second = lax.ppermute(second, "sp", upward)
-    above_first = lax.ppermute(first, "sp", downward)
-    landing = (
-        pl.BlockSpec((ROWS8, WIDE), lambda i, at: (at[0], 0)),
-        ((packed8, WIDE), BF16),
-        far,
-    )
-    row_cost = dict(
-        flops=4 * own_rows * QUARTER * hidden,
-        moved=2 * (ROWS8 * WIDE + 2 * QUARTER * hidden + own_rows * 2 * hidden),
-        prefetch=1,
-    )
-    (back_send,) = call(
-        row_grad_own_kernel, 1, [NEAR, NEAR, NEAR, NEAR, NEAR], [landing], **row_cost
-    )(own.reshape(1), first, second, gate_weight, up_weight, slot_own)
-
-    def row_grad(at, halves, back_send):
+    )(in_hbm(gate_up), in_hbm(back_own), left_part, right_part, in_hbm(prob_own))
+    below_first, above_second = both_ways(first, second)
+    below_second, above_first = both_ways(second, first)
+
+    def row_grad(shift, grads, extra, own_block=False):
+        count = len(grads)
+        blocks = count // 2
+        landing = pl.BlockSpec((ROWS8, WIDE), lambda i, at: (at[shift + i], 0))
         return call(
-            row_grad_kernel,
-            1,
-            [NEAR, NEAR, NEAR, NEAR, pl.BlockSpec(memory_space=pl.ANY)],
-            [landing],
-            aliases={5: 0},
-            **row_cost,
-        )(at.reshape(1), *halves, gate_weight, up_weight, back_send)[0]
-
+            functools.partial(row_grad_kernel, blocks, own_block),
+            blocks,
+            [whole(half, 2 * hidden)] * count
+            + [ANY, ANY, whole(own_rows, 128) if own_block else ANY],
+            [(landing, ((packed8, WIDE), BF16), far)],
+            (pltpu.VMEM((blocks * SLOTS, QUARTER), BF16), *two_weights),
+            aliases={} if own_block else {count + 3: 0},
+            flops=4 * blocks * own_rows * QUARTER * hidden,
+            moved=2 * (2 * QUARTER * hidden + blocks * (ROWS8 * WIDE + own_rows * 2 * hidden)),
+            prefetch=1,
+        )(places, *grads, gate_weight, up_weight, extra)[0]
+
+    own_halves = (in_hbm(first), in_hbm(second))
+    back_send = row_grad(0, own_halves, in_hbm(slot_own), own_block=True)
     below_first, above_second, back_send = tie((below_first, above_second, back_send))
-    across_first = lax.ppermute(below_first, "sp", upward)
-    across_second = lax.ppermute(above_second, "sp", downward)
-    below, above, across = ((own + n) % sp_count for n in (sp_count - 1, 1, 2))
-    back_send = row_grad(below, (below_first, below_second), back_send)
-    back_send = row_grad(above, (above_first, above_second), back_send)
+    across_first, across_second = both_ways(below_first, above_second)
+    back_send = row_grad(1, (below_first, below_second, above_first, above_second), back_send)
     across_first, across_second, back_send = tie((across_first, across_second, back_send))
-    weighted_own, _, _ = tie((weighted_own, across_first, across_second))
+    weighted_own, _, _ = tie((weighted_own, below_second, above_first))
     weighted = lax.all_gather(weighted_own, "sp", axis=0, tiled=True)
-    back_send = row_grad(across, (across_first, across_second), back_send)
+    back_send = row_grad(3, (across_first, across_second), back_send)
     back_packed = exchange(back_send)
+    below, above, across = (places[j] for j in (1, 2, 3))
     pieces_of = (
         (own, 0, first),
         (own, half, second),
@@ -446,7 +547,7 @@
         (pltpu.VMEM((ROWS8, 128), F32),),
         flops=2 * packed8 * WIDE * TOK * 2,
         moved=2 * (packed8 * WIDE + TOK * model),
-    )(ids, left, combine, back_packed)
+    )(in_hbm(ids), in_hbm(left), in_hbm(combine), back_packed)
     return (
         grad_in,
         grad_gate_weight[None],

time: 266 us -> 236 us (0.89)
  local copies, waits for them, and re-layouts: 35 us -> 4.91 us
  waiting for transfers between devices: 110 us -> 85.9 us
  Pallas kernels: 51.3 us -> 69.3 us
  starting transfers between devices: 36.8 us -> 42.2 us
    reduce_scatter x1 -> x0, waiting for transfers between devices: 26.7 us -> none  [on_device(): back = lax.psum_scatter(back_part, 'sp', scatter_dimension=0, tiled=True)]
    all_to_all x3, waiting for transfers between devices: 53 us -> 77.5 us  [exchange(): lax.all_to_all(pieced, ('sp', 'ep'), split_axis=0, concat_axis=0, tiled=T...]
    all_gather x1, waiting for transfers between devices: 19.7 us -> 0.01 us  [on_device(): weighted = lax.all_gather(weighted_own, 'sp', axis=0, tiled=True)]
    unnamed x47 -> x26, local copies, waits for them, and re-layouts: 22.3 us -> 3.59 us
    pallas_call x7 -> x8, Pallas kernels: 41.7 us -> 55.4 us  [the longest x3 25.6 us: row_grad(): call(functools.partial(row_grad_kernel, blocks, own_block), blocks, [whol...]
    dynamic_update_slice x8, local copies, waits for them, and re-layouts: 11.6 us -> 0.29 us  [on_device(): lax.dynamic_update_slice_in_dim(grads_all, grads, at * own_rows + shift,...]
    reduce_scatter x1, waiting for transfers between devices: 7.95 us -> 0.01 us  [on_device(): lax.psum_scatter(gate_up_part, 'sp', scatter_dimension=0, tiled=True)]
    ppermute x6 -> x10, waiting for transfers between devices: 2.51 us -> 8.3 us  [both_ways(): return (lax.ppermute(up, 'sp', upward), lax.ppermute(down, 'sp', downward))]
  transfers between devices with their start and end apart: 12 -> 15, of which waited for: 6 -> 5; matrix products, arithmetic and copies ran while one was open for 14% -> 7% of each run, Pallas kernels for 14% -> 24%
where the time goes in v3:
time: 236 us; the launch traced here: 235 us
  waiting for transfers between devices  85.9 us (36%)
  Pallas kernels  69.3 us (29%)
  starting transfers between devices  42.2 us (18%)
  between operations  16.4 us (7%)
  matrix products  15.6 us (7%)
  local copies, waits for them, and re-layouts  4.91 us (2%)
    all_to_all x3, waiting for transfers between devices, exchange(): lax.all_to_all(pieced, ('sp', 'ep'), split_axis=0, concat_axis=0, tiled=T...  77.5 us
    all_to_all x3, starting transfers between devices, exchange(): lax.all_to_all(pieced, ('sp', 'ep'), split_axis=0, concat_axis=0, tiled=T...  28.6 us
    pallas_call x3, Pallas kernels, row_grad(): call(functools.partial(row_grad_kernel, blocks, own_block), blocks, [whol...  25.6 us
    dot_general x3, matrix products, over_rows(): lax.dot_general(a, b, contract_rows, preferred_element_type=F32)  15.6 us
    ppermute x10, starting transfers between devices, both_ways(): return (lax.ppermute(up, 'sp', upward), lax.ppermute(down, 'sp', downward))  13.5 us
    pallas_call x1, Pallas kernels, on_device(): call(gate_up_kernel, 2, [rows_of(some8, WIDE), ANY, ANY], [(rows_of(some_...  12.4 us
    ppermute x10, waiting for transfers between devices, both_ways(): return (lax.ppermute(up, 'sp', upward), lax.ppermute(down, 'sp', downward))  8.3 us
    pallas_call x1, Pallas kernels, on_device(): call(back_near_kernel, 1, [whole(all_rows, QUARTER), ANY], [(whole(*block...  7.51 us
  transfers between devices with their start and end apart: 15, of which 5 were waited for; matrix products, arithmetic and copies ran while one was open for 7% of the time, Pallas kernels for 24%

profile of v3, /device:TPU:1, one launch (start us, length us, event | category | flops | bytes accessed | tf_op | source)
XLA Modules:
  0.0 234.8 jit_solution(15684258980603093783)
XLA Ops:
  7.2 5.0 %shard_map.119 = (bf16[1024,1280]{1,0:T(8,128)(2,1)}, bf16[3,256,256]{2,1,0:T(8,128)(2,1)}, bf16[4,128,256]{2,1,0:T(8,128)(2,1)}, bf16[256,128]{1,0:T(8,128)(2,1)}) custom-call(s32[8,128]{1,0:T(8,128)} %bitcast.40, f32[8,128]{1,0:T(8,128)} %bitcast.44, bf16[128,6656]{1,0:T(8,128)(2,1)} %x_ref.2), custom_call_target="tpu_custom_call" | custom-call | flops 671088640 | bytes 4325376 | tf_op jit(solution)/shard_map/pallas_call | solution.py:376
  12.2 11.5 %all-to-all-start = ((bf16[128,8,1280]{2,1,0:T(8,128)(2,1)}), bf16[128,8,1280]{2,1,0:T(8,128)(2,1)S(1)}, u32[]{:S(2)}, u32[]{:S(2)}) async-start(bf16[128,8,1280]{2,1,0:T(8,128)(2,1)} %bitcast.39), calls=%async_computation | async-start | bytes 5242880 | tf_op jit(solution)/shard_map/all_to_all | solution.py:400
  23.7 4.6 %shard_map.120 = bf16[1024,1280]{1,0:T(8,128)(2,1)} custom-call(bf16[3,256,256]{2,1,0:T(8,128)(2,1)} %get-tuple-element.37.left_ref, bf16[256,128]{1,0:T(8,128)(2,1)} %get-tuple-element.40.spare_ref, bf16[128,6656]{1,0:T(8,128)(2,1)} %x_ref.3), custom_call_target="tpu_custom_call" | custom-call | flops 671088640 | bytes 4325376 | tf_op jit(solution)/shard_map/pallas_call | solution.py:389
  28.3 31.5 %all-to-all-done = bf16[128,8,1280]{2,1,0:T(8,128)(2,1)S(1)} async-done(((bf16[128,8,1280]{2,1,0:T(8,128)(2,1)}), bf16[128,8,1280]{2,1,0:T(8,128)(2,1)S(1)}, u32[]{:S(2)}, u32[]{:S(2)}) %all-to-all-start) | async-done | bytes 2621472 | tf_op jit(solution)/shard_map/all_to_all | solution.py:400
  59.8 1.5 copy-done.8
  61.3 4.5 %all-to-all-start.1 = ((bf16[128,8,1280]{2,1,0:T(8,128)(2,1)}), bf16[128,8,1280]{2,1,0:T(8,128)(2,1)S(1)}, u32[]{:S(2)}, u32[]{:S(2)}) async-start(bf16[128,8,1280]{2,1,0:T(8,128)(2,1)} %bitcast.37), calls=%async_computation.2 | async-start | bytes 5242880 | tf_op jit(solution)/shard_map/all_to_all | solution.py:400
  65.9 12.4 %shard_map.121 = (bf16[768,1664]{1,0:T(8,128)(2,1)}, bf16[768,2048]{1,0:T(8,128)(2,1)}) custom-call(bf16[1024,1280]{1,0:T(8,128)(2,1)} %bitcast.38, bf16[1664,1024]{1,0:T(8,128)(2,1)} %bitcast.29, bf16[1664,1024]{1,0:T(8,128)(2,1)} %bitcast.33), custom_call_target="tpu_custom_call" | custom-call | flops 5234491392 | bytes 15138816 | tf_op jit(solution)/shard_map/pallas_call | solution.py:411
  78.4 28.4 %all-to-all-done.1 = bf16[128,8,1280]{2,1,0:T(8,128)(2,1)S(1)} async-done(((bf16[128,8,1280]{2,1,0:T(8,128)(2,1)}), bf16[128,8,1280]{2,1,0:T(8,128)(2,1)S(1)}, u32[]{:S(2)}, u32[]{:S(2)}) %all-to-all-start.1) | async-done | bytes 2621472 | tf_op jit(solution)/shard_map/all_to_all | solution.py:400
  106.8 4.8 %shard_map.122 = (bf16[768,1664]{1,0:T(8,128)(2,1)}, bf16[96,1024]{1,0:T(8,128)(2,1)}, bf16[96,1024]{1,0:T(8,128)(2,1)}, bf16[192,128]{1,0:T(8,128)(2,1)}) custom-call(s32[4]{0:T(128)S(1)} %and_select_fusion.at_ref, bf16[1024,1280]{1,0:T(8,128)(2,1)S(1)} %bitcast.27, bf16[1024,1664]{1,0:T(8,128)(2,1)} %bitcast.42), custom_call_target="tpu_custom_call" | custom-call | flops 83751862272 | bytes 8585216 | tf_op jit(solution)/shard_map/pallas_call | solution.py:437
  112.0 2.3 collective-permute-start.1
  114.3 7.5 %shard_map.123 = (bf16[192,1024]{1,0:T(8,128)(2,1)}, bf16[192,1024]{1,0:T(8,128)(2,1)}, bf16[192,1024]{1,0:T(8,128)(2,1)}) custom-call(s32[4]{0:T(128)S(1)} %and_select_fusion.at_ref, bf16[768,1664]{1,0:T(8,128)(2,1)} %get-tuple-element.45.rows_ref, bf16[1024,1664]{1,0:T(8,128)(2,1)} %bitcast.43), custom_call_target="tpu_custom_call" | custom-call | flops 1962934272 | bytes 7143424 | tf_op jit(solution)/shard_map/pallas_call | solution.py:453
  121.9 1.8 collective-permute-done.first_ref
  123.6 2.1 shard_map.124
  126.0 2.5 %collective-permute-start.3 = (bf16[192,1024]{1,0:T(8,128)(2,1)}, bf16[192,1024]{1,0:T(8,128)(2,1)S(1)}, u32[]{:S(2)}, u32[]{:S(2)}) collective-permute-start(bf16[192,1024]{1,0:T(8,128)(2,1)} %get-tuple-element.52), channel_id=1, source_target_pairs={{0,3},{1,0},{2,1},{3,2},{4,7},{5,4},{6,5},{7,6},{8,11},{9,8},{10,9... | collective-permute-start | bytes 1179656 | tf_op jit(solution)/shard_map/ppermute | solution.py:432
  128.5 6.5 %collective-permute-done.2.left_ref = bf16[192,1024]{1,0:T(8,128)(2,1)S(1)} collective-permute-done((bf16[192,1024]{1,0:T(8,128)(2,1)}, bf16[192,1024]{1,0:T(8,128)(2,1)S(1)}, u32[]{:S(2)}, u32[]{:S(2)}) %collective-permute-start.2) | collective-permute-done | bytes 393248 | tf_op jit(solution)/shard_map/ppermute | solution.py:432
  135.0 3.0 %shard_map.125 = (bf16[96,2048]{1,0:T(8,128)(2,1)}, bf16[96,2048]{1,0:T(8,128)(2,1)}, bf16[192,1024]{1,0:T(8,128)(2,1)}, bf16[192,128]{1,0:T(8,128)(2,1)}) custom-call(bf16[192,2048]{1,0:T(8,128)(2,1)} %reduce-scatter.2.cloned.1.call-done.gate_up_ref, bf16[192,1024]{1,0:T(8,128)(2,1)} %get-tuple-element.46.own_ref, ...), custom_call_target="tpu_custom_call" | custom-call | flops 3932160 | bytes 2359296 | tf_op jit(solution)/shard_map/pallas_call | solution.py:471
  137.9 0.6 collective-permute-start.4
  138.5 2.1 collective-permute-start.5
  140.6 2.7 %collective-permute-start.9 = (bf16[96,2048]{1,0:T(8,128)(2,1)}, bf16[96,2048]{1,0:T(8,128)(2,1)S(1)}, u32[]{:S(2)}, u32[]{:S(2)}) collective-permute-start(bf16[96,2048]{1,0:T(8,128)(2,1)} %get-tuple-element.54.refs_0_), channel_id=1, source_target_pairs={{0,3},{1,0},{2,1},{3,2},{4,7},{5,4},{6,5},{7,6},{8,11},{9,8},{10,9... | collective-permute-start | bytes 1179656 | tf_op jit(solution)/shard_map/ppermute | solution.py:432
  143.3 8.8 %shard_map.126.refs_6_ = bf16[1024,1280]{1,0:T(8,128)(2,1)} custom-call(s32[4]{0:T(128)S(1)} %and_select_fusion.at_ref, bf16[96,2048]{1,0:T(8,128)(2,1)} %get-tuple-element.54.refs_0_, bf16[96,2048]{1,0:T(8,128)(2,1)} %get-tuple-element.55.refs_1_, bf16[1664,1024]{1,0:T(8,128)(2,1)} %bitcast.30, bf16[1664,1024]{1,0:T(8,128)(2,1)} %bitcast.34, ...), custom_call_target="tpu_custom_call" | custom-call | flops 1308622848 | bytes 8257536 | tf_op jit(solution)/shard_map/pallas_call | solution.py:491
  152.2 2.7 %collective-permute-start.7 = (bf16[96,2048]{1,0:T(8,128)(2,1)S(1)}, bf16[96,2048]{1,0:T(8,128)(2,1)S(1)}, u32[]{:S(2)}, u32[]{:S(2)}) collective-permute-start(bf16[96,2048]{1,0:T(8,128)(2,1)S(1)} %collective-permute-done.5.refs_3_), channel_id=1, source_target_pairs={{0,3},{1,0},{2,1},{3,2},{4,7},{5,4},{6,5},{7,6},{8,11},{9,8},{10,9... | collective-permute-start | bytes 1179656 | tf_op jit(solution)/shard_map/ppermute | solution.py:432
  154.9 0.6 fusion.6
  157.6 9.3 %shard_map.127.refs_4_ = bf16[1024,1280]{1,0:T(8,128)(2,1)} custom-call(s32[4]{0:T(128)S(1)} %and_select_fusion.at_ref, bf16[96,2048]{1,0:T(8,128)(2,1)S(1)} %collective-permute-done.4.refs_0_, bf16[96,2048]{1,0:T(8,128)(2,1)S(1)} %collective-permute-done.8.refs_1_, ...), custom_call_target="tpu_custom_call", output_to_operand_aliasing={{}: (7, {})} | custom-call | flops 2617245696 | bytes 9699328 | tf_op jit(solution)/shard_map/pallas_call | solution.py:491
  166.9 7.6 %shard_map.128 = bf16[1024,1280]{1,0:T(8,128)(2,1)} custom-call(s32[4]{0:T(128)S(1)} %and_select_fusion.at_ref, bf16[96,2048]{1,0:T(8,128)(2,1)S(1)} %collective-permute-done.6.refs_0_, bf16[96,2048]{1,0:T(8,128)(2,1)S(1)} %collective-permute-done.7.refs_1_, bf16[1664,1024]{1,0:T(8,128)(2,1)} %bitcast.32, ...), custom_call_target="tpu_custom_call", output_to_operand_aliasing={{}: (5, {})} | custom-call | flops 1308622848 | bytes 8257536 | tf_op jit(solution)/shard_map/pallas_call | solution.py:491
  174.5 12.6 %all-to-all-start.2 = ((bf16[128,8,1280]{2,1,0:T(8,128)(2,1)}), bf16[128,8,1280]{2,1,0:T(8,128)(2,1)S(1)}, u32[]{:S(2)}, u32[]{:S(2)}) async-start(bf16[128,8,1280]{2,1,0:T(8,128)(2,1)} %bitcast.28), calls=%async_computation.3 | async-start | bytes 5242880 | tf_op jit(solution)/shard_map/all_to_all | solution.py:400
  188.9 1.1 copy-done.12
  190.0 4.3 %fusion = bf16[1,1664,1024]{2,1,0:T(8,128)(2,1)} fusion(bf16[768,1664]{1,0:T(8,128)(2,1)S(1)} %copy-done.12, bf16[768,2048]{1,0:T(8,128)(2,1)S(1)} %constant_dynamic-update-slice_fusion), kind=kOutput, calls=%fused_computation.3 | convolution fusion | flops 2618949632 | bytes 7536640 | tf_op jit(solution)/shard_map/dot_general | solution.py:534
  194.3 4.3 %fusion.1 = bf16[1,1664,1024]{2,1,0:T(8,128)(2,1)} fusion(bf16[768,1664]{1,0:T(8,128)(2,1)S(1)} %copy-done.12, bf16[768,2048]{1,0:T(8,128)(2,1)S(1)} %constant_dynamic-update-slice_fusion), kind=kOutput, calls=%fused_computation.4 | convolution fusion | flops 2618949632 | bytes 7536640 | tf_op jit(solution)/shard_map/dot_general | solution.py:534
  198.6 7.0 %fusion.2 = bf16[1,1024,1664]{2,1,0:T(8,128)(2,1)} fusion(bf16[768,1024]{1,0:T(8,128)(2,1)} %all-gather.2.cloned.1.call-done, bf16[768,1664]{1,0:T(8,128)(2,1)} %get-tuple-element.45.rows_ref), kind=kOutput, calls=%fused_computation.5 | convolution fusion | flops 2618949632 | bytes 7536640 | tf_op jit(solution)/shard_map/dot_general | solution.py:534
  205.6 17.6 %all-to-all-done.2 = bf16[128,8,1280]{2,1,0:T(8,128)(2,1)S(1)} async-done(((bf16[128,8,1280]{2,1,0:T(8,128)(2,1)}), bf16[128,8,1280]{2,1,0:T(8,128)(2,1)S(1)}, u32[]{:S(2)}, u32[]{:S(2)}) %all-to-all-start.2) | async-done | bytes 2621472 | tf_op jit(solution)/shard_map/all_to_all | solution.py:400
  223.2 4.2 %shard_map.129 = (bf16[128,6656]{1,0:T(8,128)(2,1)}, f32[8,128]{1,0:T(8,128)S(1)}) custom-call(s32[8,128]{1,0:T(8,128)} %bitcast.41, bf16[3,256,256]{2,1,0:T(8,128)(2,1)} %get-tuple-element.37.left_ref, bf16[4,128,256]{2,1,0:T(8,128)(2,1)} %get-tuple-element.38.combine_ref, bf16[1024,1280]{1,0:T(8,128)(2,1)S(1)} %bitcast.26), custom_call_target="tpu_custom_call" | custom-call | flops 671088640 | bytes 4325376 | tf_op jit(solution)/shard_map/pallas_call | solution.py:539
  227.4 0.6 convert_bitcast_fusion
  (52 shorter events, 2.5 us)
Async XLA Ops:
  12.2 47.6 %all-to-all-start = ((bf16[128,8,1280]{2,1,0:T(8,128)(2,1)}), bf16[128,8,1280]{2,1,0:T(8,128)(2,1)S(1)}, u32[]{:S(2)}, u32[]{:S(2)}) async-start(bf16[128,8,1280]{2,1,0:T(8,128)(2,1)} %bitcast.39), calls=%async_computation | async-start | bytes 5242880 | tf_op jit(solution)/shard_map/all_to_all | solution.py:400
  28.3 37.5 %copy-start.11 = (s32[4]{0:T(128)S(1)}, s32[4]{0:T(128)}, u32[]{:S(2)}) copy-start(s32[4]{0:T(128)} %constant.39.clone) | copy-start | bytes 52
  59.8 1.5 copy-start.8
  61.3 45.5 %all-to-all-start.1 = ((bf16[128,8,1280]{2,1,0:T(8,128)(2,1)}), bf16[128,8,1280]{2,1,0:T(8,128)(2,1)S(1)}, u32[]{:S(2)}, u32[]{:S(2)}) async-start(bf16[128,8,1280]{2,1,0:T(8,128)(2,1)} %bitcast.37), calls=%async_computation.2 | async-start | bytes 5242880 | tf_op jit(solution)/shard_map/all_to_all | solution.py:400
  65.8 69.1 %reduce-scatter.2.cloned.1.call-start = ((), (), s32[]{:S(2)}) async-start(), calls=%async_computation.4 | async-start | bytes 3932160 | tf_op jit(solution)/shard_map/reduce_scatter | solution.py:423
  78.3 120.2 %all-gather.2.cloned.1.call-start = ((), (), s32[]{:S(2)}) async-start(), calls=%async_computation.5 | async-start | bytes 1966080 | tf_op jit(solution)/shard_map/all_gather | solution.py:511
  111.6 12.0 %collective-permute-start = (bf16[96,1024]{1,0:T(8,128)(2,1)}, bf16[96,1024]{1,0:T(8,128)(2,1)S(1)}, u32[]{:S(2)}, u32[]{:S(2)}) collective-permute-start(bf16[96,1024]{1,0:T(8,128)(2,1)} %get-tuple-element.49), channel_id=1, source_target_pairs={{0,1},{1,2},{2,3},{3,0},{4,5},{5,6},{6,7},{7,4},{8,9},{9,10},{10,1... | collective-permute-start | bytes 589832 | tf_op jit(solution)/shard_map/ppermute | solution.py:432
  112.0 11.6 %collective-permute-start.1 = (bf16[96,1024]{1,0:T(8,128)(2,1)}, bf16[96,1024]{1,0:T(8,128)(2,1)S(1)}, u32[]{:S(2)}, u32[]{:S(2)}) collective-permute-start(bf16[96,1024]{1,0:T(8,128)(2,1)} %get-tuple-element.50), channel_id=1, source_target_pairs={{0,3},{1,0},{2,1},{3,2},{4,7},{5,4},{6,5},{7,6},{8,11},{9,8},{10,9... | collective-permute-start | bytes 589832 | tf_op jit(solution)/shard_map/ppermute | solution.py:432
  125.8 9.2 %collective-permute-start.2 = (bf16[192,1024]{1,0:T(8,128)(2,1)}, bf16[192,1024]{1,0:T(8,128)(2,1)S(1)}, u32[]{:S(2)}, u32[]{:S(2)}) collective-permute-start(bf16[192,1024]{1,0:T(8,128)(2,1)} %get-tuple-element.51), channel_id=1, source_target_pairs={{0,1},{1,2},{2,3},{3,0},{4,5},{5,6},{6,7},{7,4},{8,9},{9,10},{10,1... | collective-permute-start | bytes 1179656 | tf_op jit(solution)/shard_map/ppermute | solution.py:432
  126.0 9.0 %collective-permute-start.3 = (bf16[192,1024]{1,0:T(8,128)(2,1)}, bf16[192,1024]{1,0:T(8,128)(2,1)S(1)}, u32[]{:S(2)}, u32[]{:S(2)}) collective-permute-start(bf16[192,1024]{1,0:T(8,128)(2,1)} %get-tuple-element.52), channel_id=1, source_target_pairs={{0,3},{1,0},{2,1},{3,2},{4,7},{5,4},{6,5},{7,6},{8,11},{9,8},{10,9... | collective-permute-start | bytes 1179656 | tf_op jit(solution)/shard_map/ppermute | solution.py:432
  137.9 14.1 %collective-permute-start.4 = (bf16[96,2048]{1,0:T(8,128)(2,1)}, bf16[96,2048]{1,0:T(8,128)(2,1)S(1)}, u32[]{:S(2)}, u32[]{:S(2)}) collective-permute-start(bf16[96,2048]{1,0:T(8,128)(2,1)} %get-tuple-element.54.refs_0_), channel_id=1, source_target_pairs={{0,1},{1,2},{2,3},{3,0},{4,5},{5,6},{6,7},{7,4},{8,9},{9,10},{10,1... | collective-permute-start | bytes 1179656 | tf_op jit(solution)/shard_map/ppermute | solution.py:432
  138.5 13.6 %collective-permute-start.5 = (bf16[96,2048]{1,0:T(8,128)(2,1)}, bf16[96,2048]{1,0:T(8,128)(2,1)S(1)}, u32[]{:S(2)}, u32[]{:S(2)}) collective-permute-start(bf16[96,2048]{1,0:T(8,128)(2,1)} %get-tuple-element.55.refs_1_), channel_id=1, source_target_pairs={{0,3},{1,0},{2,1},{3,2},{4,7},{5,4},{6,5},{7,6},{8,11},{9,8},{10,9... | collective-permute-start | bytes 1179656 | tf_op jit(solution)/shard_map/ppermute | solution.py:432
  140.6 16.9 %collective-permute-start.8 = (bf16[96,2048]{1,0:T(8,128)(2,1)}, bf16[96,2048]{1,0:T(8,128)(2,1)S(1)}, u32[]{:S(2)}, u32[]{:S(2)}) collective-permute-start(bf16[96,2048]{1,0:T(8,128)(2,1)} %get-tuple-element.55.refs_1_), channel_id=1, source_target_pairs={{0,1},{1,2},{2,3},{3,0},{4,5},{5,6},{6,7},{7,4},{8,9},{9,10},{10,1... | collective-permute-start | bytes 1179656 | tf_op jit(solution)/shard_map/ppermute | solution.py:432
  140.6 16.9 %collective-permute-start.9 = (bf16[96,2048]{1,0:T(8,128)(2,1)}, bf16[96,2048]{1,0:T(8,128)(2,1)S(1)}, u32[]{:S(2)}, u32[]{:S(2)}) collective-permute-start(bf16[96,2048]{1,0:T(8,128)(2,1)} %get-tuple-element.54.refs_0_), channel_id=1, source_target_pairs={{0,3},{1,0},{2,1},{3,2},{4,7},{5,4},{6,5},{7,6},{8,11},{9,8},{10,9... | collective-permute-start | bytes 1179656 | tf_op jit(solution)/shard_map/ppermute | solution.py:432
  152.1 14.8 %copy-start.2 = (bf16[96,2048]{1,0:T(8,128)(2,1)}, bf16[96,2048]{1,0:T(8,128)(2,1)S(1)}, u32[]{:S(2)}) copy-start(bf16[96,2048]{1,0:T(8,128)(2,1)S(1)} %collective-permute-done.4.refs_0_) | copy-start | bytes 1179652
  152.1 14.8 %copy-start = (bf16[96,2048]{1,0:T(8,128)(2,1)}, bf16[96,2048]{1,0:T(8,128)(2,1)S(1)}, u32[]{:S(2)}) copy-start(bf16[96,2048]{1,0:T(8,128)(2,1)S(1)} %collective-permute-done.5.refs_3_) | copy-start | bytes 1179652
  152.1 14.8 %collective-permute-start.6 = (bf16[96,2048]{1,0:T(8,128)(2,1)S(1)}, bf16[96,2048]{1,0:T(8,128)(2,1)S(1)}, u32[]{:S(2)}, u32[]{:S(2)}) collective-permute-start(bf16[96,2048]{1,0:T(8,128)(2,1)S(1)} %collective-permute-done.4.refs_0_), channel_id=1, source_target_pairs={{0,1},{1,2},{2,3},{3,0},{4,5},{5,6},{6,7},{7,4},{8,9},{9,10},{10,1... | collective-permute-start | bytes 1179656 | tf_op jit(solution)/shard_map/ppermute | solution.py:432
  152.2 14.7 %collective-permute-start.7 = (bf16[96,2048]{1,0:T(8,128)(2,1)S(1)}, bf16[96,2048]{1,0:T(8,128)(2,1)S(1)}, u32[]{:S(2)}, u32[]{:S(2)}) collective-permute-start(bf16[96,2048]{1,0:T(8,128)(2,1)S(1)} %collective-permute-done.5.refs_3_), channel_id=1, source_target_pairs={{0,3},{1,0},{2,1},{3,2},{4,7},{5,4},{6,5},{7,6},{8,11},{9,8},{10,9... | collective-permute-start | bytes 1179656 | tf_op jit(solution)/shard_map/ppermute | solution.py:432
  157.5 9.4 %copy-start.4 = (bf16[96,2048]{1,0:T(8,128)(2,1)}, bf16[96,2048]{1,0:T(8,128)(2,1)S(1)}, u32[]{:S(2)}) copy-start(bf16[96,2048]{1,0:T(8,128)(2,1)S(1)} %collective-permute-done.8.refs_1_) | copy-start | bytes 1179652
  157.5 9.3 %copy-start.6 = (bf16[96,2048]{1,0:T(8,128)(2,1)}, bf16[96,2048]{1,0:T(8,128)(2,1)S(1)}, u32[]{:S(2)}) copy-start(bf16[96,2048]{1,0:T(8,128)(2,1)S(1)} %collective-permute-done.9.refs_2_) | copy-start | bytes 1179652
  174.5 48.7 %all-to-all-start.2 = ((bf16[128,8,1280]{2,1,0:T(8,128)(2,1)}), bf16[128,8,1280]{2,1,0:T(8,128)(2,1)S(1)}, u32[]{:S(2)}, u32[]{:S(2)}) async-start(bf16[128,8,1280]{2,1,0:T(8,128)(2,1)} %bitcast.28), calls=%async_computation.3 | async-start | bytes 5242880 | tf_op jit(solution)/shard_map/all_to_all | solution.py:400
  187.1 1.0 copy-start.10
  187.2 1.1 copy-start.9
  187.2 1.2 copy-start.3
  187.2 1.3 copy-start.5
  187.2 1.4 copy-start.7
  187.2 1.5 copy-start.1
  188.1 1.9 copy-start.12
Sparse Core Ops, SparseCore 0:
  78.5 49.3 reduce-scatter.1
  157.7 30.5 all-gather.1

commit v4 on v3

--- a/solution.py
+++ b/solution.py
@@ -18,6 +18,7 @@
 BLOCK = 32
 SLOTS = BLOCK * CAP
 ROWS8 = BLOCK * PACKED
+RING = 4
 MIB = 1 << 20
 BF16 = jnp.bfloat16
 F32 = jnp.float32
@@ -140,23 +141,59 @@
         copy.wait()
 
 
+def ring_place(n):
+    return jnp.bitwise_and(lax.axis_index("sp").astype(jnp.int32) + n, RING - 1)
+
+
+def span(at, rows):
+    return pl.ds(pl.multiple_of(at * rows, rows), rows)
+
+
 def gate_up_kernel(
-    packed_ref, gate_hbm, up_hbm, rows_ref, parts_ref, gate_ref, up_ref, gate_sem, up_sem, *masks
+    packed_hbm,
+    gate_hbm,
+    up_hbm,
+    rows_ref,
+    parts_ref,
+    packed_ref,
+    packed_sem,
+    gate_ref,
+    up_ref,
+    gate_sem,
+    up_sem,
+    *masks,
 ):
-    first = pl.program_id(0) == 0
+    step = pl.program_id(0)
     weights = ((gate_hbm, gate_ref, gate_sem), (up_hbm, up_ref, up_sem))
-
-    @pl.when(first)
+    rows8 = packed_ref.shape[0] // 2
+    pieces = [
+        pltpu.make_async_copy(
+            packed_hbm.at[pl.ds(j * rows8, rows8)],
+            packed_ref.at[pl.ds(j * rows8, rows8)],
+            packed_sem.at[j],
+        )
+        for j in range(2)
+    ]
+
+    @pl.when(step == 0)
     def _():
+        pieces[0].start()
         for weight in weights:
             start(shares(*weight))
+        pieces[1].start()
         unpack_masks(*masks)
 
-    unpack_all(packed_ref, rows_ref, *masks)
+    for j in range(2):
+
+        @pl.when(step == j)
+        def _(j=j):
+            pieces[j].wait()
+
+    unpack_all(packed_ref.at[span(step, rows8)], rows_ref, *masks)
     hidden = gate_ref.shape[1]
     for j, weight in enumerate(weights):
 
-        @pl.when(first)
+        @pl.when(step == 0)
         def _(weight=weight):
             finish(shares(*weight))
 
@@ -164,41 +201,50 @@
         parts_ref[:, cols] = product(rows_ref[...], weight[1][...]).astype(BF16)
 
 
-def block_of(rows_ref, at, count=SLOTS):
-    return rows_ref[pl.ds(pl.multiple_of(at * SLOTS, SLOTS), count), :]
-
-
-def back_far_kernel(
-    at_ref, packed_ref, down_hbm, rows_ref, first_ref, second_ref, prob_ref, down_ref, sem, *masks
-):
+def back_parts(rows_ref, down_ref, copies, outs):
+    width = down_ref.shape[0] // len(copies)
+    for j, copy in enumerate(copies):
+        copy.wait()
+        cols = pl.ds(j * width, width)
+        part = product_t(rows_ref[...], down_ref[cols, :]).astype(BF16)
+        for row, out_ref in outs:
+            out_ref[:, cols] = part[row : row + out_ref.shape[0]]
+
+
+def back_block_kernel(turns, packed_hbm, down_hbm, *refs):
+    outs, rest = refs[:2], refs[2:]
+    packed_ref, packed_sem, rows_ref, down_ref, sem, *masks = rest
+    pieces = [
+        pltpu.make_async_copy(
+            packed_hbm.at[span(ring_place(n), ROWS8)],
+            packed_ref.at[pl.ds(j * ROWS8, ROWS8)],
+            packed_sem.at[j],
+        )
+        for j, n in enumerate(turns)
+    ]
+    copies = shares(down_hbm, down_ref, sem)
+    start(pieces)
+    start(copies)
+    unpack_masks(*masks)
+    finish(pieces)
+    unpack_all(packed_ref, rows_ref, *masks)
+    back_parts(rows_ref, down_ref, copies, ((0, outs[0]), (outs[0].shape[0], outs[1])))
+
+
+def back_own_kernel(packed_ref, down_hbm, rows_ref, own_ref, prob_ref, down_ref, sem, *masks):
     copies = shares(down_hbm, down_ref, sem)
     start(copies)
     unpack_masks(*masks)
     unpack_all(packed_ref, rows_ref, *masks)
-    finish(copies)
-    part = product_t(block_of(rows_ref, at_ref[3]), down_ref[...]).astype(BF16)
-    half = first_ref.shape[0]
-    first_ref[...] = part[:half]
-    second_ref[...] = part[half:]
+    own = ring_place(0)
+    back_parts(rows_ref.at[span(own, SLOTS)], down_ref, copies, ((0, own_ref),))
     r = iota((SLOTS, ROWS8), 0)
     c = iota((SLOTS, ROWS8), 1)
     pick = one_hot((r // CAP == c // PACKED) & (c % PACKED == CAP)).astype(BF16)
     mine = iota((SLOTS, 128), 0) % CAP == iota((SLOTS, 128), 1)
-    own8 = pl.ds(pl.multiple_of(at_ref[0] * ROWS8, ROWS8), ROWS8)
-    probs = product(pick, packed_ref[own8, 3 * TAIL :])
+    probs = product(pick, packed_ref[span(own, ROWS8), 3 * TAIL :])
     prob = jnp.sum(jnp.where(mine, probs, 0.0), axis=1, keepdims=True)
     prob_ref[...] = jnp.broadcast_to(prob, (SLOTS, 128)).astype(BF16)
-
-
-def back_near_kernel(at_ref, rows_ref, down_hbm, own_ref, below_ref, above_ref, down_ref, sem):
-    copies = shares(down_hbm, down_ref, sem)
-    start(copies)
-    finish(copies)
-    blocks = [block_of(rows_ref, at_ref[j]) for j in range(3)]
-    part = product_t(jnp.concatenate(blocks, axis=0), down_ref[...]).astype(BF16)
-    own_ref[...] = part[:SLOTS]
-    below_ref[...] = part[SLOTS : 2 * SLOTS]
-    above_ref[...] = part[2 * SLOTS :]
 
 
 def join_kernel(below_ref, above_ref, first_ref, second_ref, below_out, above_out):
@@ -237,51 +283,84 @@
         slot_ref[at, :] = jnp.where(mine, slot, 0.0).astype(BF16)
 
 
-def pack(rows, out_ref):
+def pack_group(g, rows_ref, out_ref, spare=None):
     r = iota((ROWS8, SLOTS), 0)
     c = iota((ROWS8, SLOTS), 1)
     same = r // PACKED == c // CAP
     place = r % PACKED
     slot = c % CAP
     main = one_hot(same & (slot == place)).astype(BF16)
-    rest = rows[:, WIDE:]
-    for g in range(3):
+    if g < 3:
+        cols = pl.ds(g * TAIL, TAIL)
         tail = one_hot(same & (place >= CAP) & (slot == (place - CAP) * 3 + g)).astype(BF16)
         left = jnp.concatenate([main, tail], axis=1)
-        right = jnp.concatenate([rows[:, g * TAIL : (g + 1) * TAIL], rest], axis=0)
-        out_ref[:, g * TAIL : (g + 1) * TAIL] = product(left, right).astype(BF16)
-    return product(main, rows[:, 3 * TAIL : WIDE])
-
-
-def row_grad_kernel(blocks, own, at_ref, *refs):
-    grads_refs, rest = refs[:-9], refs[-9:]
-    gate_hbm, up_hbm, extra_ref, out_ref, rows_ref, gate_ref, up_ref, gate_sem, up_sem = rest
+        right = jnp.concatenate([rows_ref[:, cols], rows_ref[:, WIDE:]], axis=0)
+        out_ref[:, cols] = product(left, right).astype(BF16)
+        return
+    last = product(main, rows_ref[:, 3 * TAIL : WIDE])
+    if spare is not None:
+        lift = one_hot(same & (place == CAP)).astype(BF16)
+        last = last + product(lift, spare)
+    out_ref[:, 3 * TAIL :] = last.astype(BF16)
+
+
+COLUMN_RUNS = ((WIDE, QUARTER, ()), (0, 2 * TAIL, (0, 1)), (2 * TAIL, WIDE, (2, 3)))
+
+
+def row_grad_kernel(turns, own, *refs):
+    halves = 2 * len(turns)
+    halves_hbm, rest = refs[:halves], refs[halves:]
+    gate_hbm, up_hbm, extra_ref, out_hbm, grads_ref, rows_ref, packed_ref, gate_ref, up_ref = rest[:9]
+    grads_sem, gate_sem, up_sem, out_sem = rest[9:]
     hidden = gate_ref.shape[1]
-    step = pl.program_id(0)
-
-    @pl.when(step == 0)
-    def _():
-        gate_copies = shares(gate_hbm, gate_ref, gate_sem)
-        up_copies = shares(up_hbm, up_ref, up_sem)
-        start(gate_copies)
-        start(up_copies)
-        grads = jnp.concatenate([r[...] for r in grads_refs], axis=0)
-        finish(gate_copies)
-        rows = product_t(grads[:, :hidden], gate_ref[...])
-        finish(up_copies)
-        rows_ref[...] = (rows + product_t(grads[:, hidden:], up_ref[...])).astype(BF16)
-
-    for j in range(blocks):
-
-        @pl.when(step == j)
-        def _(j=j):
-            spare = pack(rows_ref[j * SLOTS : (j + 1) * SLOTS, :], out_ref)
-            if own:
-                r = iota((ROWS8, SLOTS), 0)
-                c = iota((ROWS8, SLOTS), 1)
-                lift = one_hot((r // PACKED == c // CAP) & (r % PACKED == CAP)).astype(BF16)
-                spare = spare + product(lift, extra_ref[...])
-            out_ref[:, 3 * TAIL :] = spare.astype(BF16)
+    half = SLOTS // 2
+    grads = [
+        pltpu.make_async_copy(h, grads_ref.at[pl.ds(i * half, half)], grads_sem.at[i])
+        for i, h in enumerate(halves_hbm)
+    ]
+    start(grads)
+    pairs = []
+    for i, (low, high, _) in enumerate(COLUMN_RUNS):
+        run = pl.ds(low, high - low)
+        pair = (
+            pltpu.make_async_copy(gate_hbm.at[run], gate_ref.at[run], gate_sem.at[i]),
+            pltpu.make_async_copy(up_hbm.at[run], up_ref.at[run], up_sem.at[i]),
+        )
+        start(pair)
+        pairs.append(pair)
+    finish(grads)
+    spare = extra_ref[...] if own else None
+    sent = []
+    for (low, high, groups), pair in zip(COLUMN_RUNS, pairs):
+        finish(pair)
+        run = pl.ds(low, high - low)
+        rows = product_t(grads_ref[:, :hidden], gate_ref[run, :])
+        rows = rows + product_t(grads_ref[:, hidden:], up_ref[run, :])
+        rows_ref[:, run] = rows.astype(BF16)
+        for j, n in enumerate(turns):
+            there = packed_ref.at[pl.ds(j * ROWS8, ROWS8)]
+            for g in groups:
+                pack_group(g, rows_ref.at[pl.ds(j * SLOTS, SLOTS)], there, spare)
+            if groups:
+                copy = pltpu.make_async_copy(
+                    there.at[:, run],
+                    out_hbm.at[span(ring_place(n), ROWS8), run],
+                    out_sem.at[len(sent)],
+                )
+                copy.start()
+                sent.append(copy)
+    finish(sent)
+
+
+def assemble_kernel(*refs):
+    halves_hbm, out_ref, sem = refs[:8], refs[8], refs[9]
+    half = SLOTS // 2
+    copies = []
+    for i, h in enumerate(halves_hbm):
+        row = pl.multiple_of(ring_place((0, RING - 1, 1, 2)[i // 2]) * SLOTS + i % 2 * half, half)
+        copies.append(pltpu.make_async_copy(h, out_ref.at[pl.ds(row, half)], sem.at[i]))
+    start(copies)
+    finish(copies)
 
 
 def combine_kernel(ids_ref, left_ref, combine_ref, packed_ref, out_ref, probs_ref, slot_ref):
@@ -314,19 +393,18 @@
         gather = one_hot(iota((EXPERTS, ROWS8), 1) // PACKED == iota((EXPERTS, ROWS8), 0))
         table = product(gather.astype(BF16), value)
         expert = iota((EXPERTS, TOK), 0)
-        for k in range(TOP):
-            hit = ids_ref[k : k + 1, :] == expert
-            found = jnp.sum(jnp.where(hit, table, 0.0), axis=0, keepdims=True)
-            probs_ref[k : k + 1, :] = found
-
-
-def call(
-    kernel, grid, ins, outs, scratch=(), flops=0, moved=0, prefetch=0, aliases=None, limit=24
-):
+        found = [
+            jnp.sum(jnp.where(ids_ref[k : k + 1, :] == expert, table, 0.0), axis=0, keepdims=True)
+            for k in range(TOP)
+        ]
+        probs_ref[...] = jnp.concatenate(found, axis=0).astype(BF16)
+
+
+def call(kernel, grid, ins, outs, scratch=(), flops=0, moved=0, aliases=None):
     return pl.pallas_call(
         kernel,
         grid_spec=pltpu.PrefetchScalarGridSpec(
-            num_scalar_prefetch=prefetch,
+            num_scalar_prefetch=0,
             grid=(grid,),
             in_specs=ins,
             out_specs=[s for s, _, _ in outs],
@@ -334,7 +412,7 @@
         ),
         out_shape=[place(shape, kind) for _, (shape, kind), place in outs],
         compiler_params=pltpu.CompilerParams(
-            dimension_semantics=("arbitrary",), vmem_limit_bytes=limit * MIB
+            dimension_semantics=("arbitrary",), vmem_limit_bytes=24 * MIB
         ),
         input_output_aliases=aliases or {},
         cost_estimate=pl.CostEstimate(flops=flops, bytes_accessed=moved, transcendentals=0),
@@ -407,24 +485,22 @@
     masks = (pltpu.VMEM((SLOTS, ROWS8), BF16), pltpu.VMEM((SLOTS, 3 * ROWS8), BF16))
     two_weights = (pltpu.VMEM((QUARTER, hidden), BF16),) * 2 + (pltpu.SemaphoreType.DMA((4,)),) * 2
     down_space = (pltpu.VMEM((hidden, QUARTER), BF16), pltpu.SemaphoreType.DMA((4,)))
-    some_rows, some8 = all_rows // 2, packed8 // 2
+    some_rows = all_rows // 2
     x_rows, gate_up_part = call(
         gate_up_kernel,
         2,
-        [rows_of(some8, WIDE), ANY, ANY],
+        [ANY, ANY, ANY],
         [
             (rows_of(some_rows, QUARTER), ((all_rows, QUARTER), BF16), far),
             (rows_of(some_rows, 2 * hidden), ((all_rows, 2 * hidden), BF16), far),
         ],
-        two_weights + masks,
+        (pltpu.VMEM((packed8, WIDE), BF16), pltpu.SemaphoreType.DMA((2,)), *two_weights, *masks),
         flops=4 * all_rows * QUARTER * hidden,
         moved=2 * (packed8 * WIDE + 2 * QUARTER * hidden + all_rows * (QUARTER + 2 * hidden)),
     )(x_packed, gate_weight, up_weight)
     gate_up = lax.psum_scatter(gate_up_part, "sp", scatter_dimension=0, tiled=True)
-    own = lax.axis_index("sp").astype(jnp.int32)
     own_rows = all_rows // sp_count
     half = own_rows // 2
-    places = (own + jnp.array([0, sp_count - 1, 1, 2], jnp.int32)) % sp_count
     upward = [(i, (i + 1) % sp_count) for i in range(sp_count)]
     downward = [(i, (i - 1) % sp_count) for i in range(sp_count)]
 
@@ -434,40 +510,57 @@
     dy_packed, _ = tie((dy_packed, gate_up_part))
     piece = ((half, hidden), BF16)
     block = ((own_rows, hidden), BF16)
-    dy_rows, far_first, far_second, prob_own = call(
-        back_far_kernel,
+
+    def back_space(turns):
+        return (
+            pltpu.VMEM((turns * ROWS8, WIDE), BF16),
+            pltpu.SemaphoreType.DMA((turns,)),
+            pltpu.VMEM((turns * SLOTS, QUARTER), BF16),
+            *down_space,
+            *masks,
+        )
+
+    far_first, far_second = call(
+        functools.partial(back_block_kernel, (2,)),
+        1,
+        [ANY, ANY],
+        [(whole(*piece[0]), piece, near)] * 2,
+        back_space(1),
+        flops=32 * 2 * all_rows * QUARTER * hidden,
+        moved=2 * (packed8 * WIDE + QUARTER * hidden + all_rows * QUARTER),
+    )(dy_packed, down_weight)
+    far_first, far_second = both_ways(far_first, far_second)
+    back_below, back_above = call(
+        functools.partial(back_block_kernel, (sp_count - 1, 1)),
+        1,
+        [ANY, ANY],
+        [(whole(*block[0]), block, near)] * 2,
+        back_space(2),
+        flops=2 * 2 * own_rows * QUARTER * hidden,
+        moved=2 * (QUARTER * hidden + 2 * ROWS8 * WIDE + 2 * own_rows * hidden),
+    )(dy_packed, down_weight)
+    back_below, back_above = call(
+        join_kernel,
+        1,
+        [whole(*block[0])] * 2 + [whole(*piece[0])] * 2,
+        [(whole(*block[0]), block, near)] * 2,
+        moved=2 * 5 * own_rows * hidden,
+    )(back_below, back_above, far_first, far_second)
+    left_part, right_part = both_ways(back_above, back_below)
+    dy_late, _ = tie((dy_packed, back_above))
+    dy_rows, back_own, prob_own = call(
+        back_own_kernel,
         1,
         [whole(packed8, WIDE), ANY],
         [
             (whole(all_rows, QUARTER), ((all_rows, QUARTER), BF16), far),
-            (whole(*piece[0]), piece, far),
-            (whole(*piece[0]), piece, far),
+            (whole(*block[0]), block, far),
             (whole(own_rows, 128), ((own_rows, 128), BF16), far),
         ],
-        down_space + masks,
-        flops=32 * 2 * all_rows * QUARTER * hidden,
-        moved=2 * (packed8 * WIDE + QUARTER * hidden + all_rows * QUARTER),
-        prefetch=1,
-    )(places, dy_packed, down_weight)
-    far_first, far_second = both_ways(far_first, far_second)
-    back_own, back_below, back_above = call(
-        back_near_kernel,
-        1,
-        [whole(all_rows, QUARTER), ANY],
-        [(whole(*block[0]), block, far)] * 3,
-        down_space,
-        flops=2 * 3 * own_rows * QUARTER * hidden,
-        moved=2 * (QUARTER * hidden + all_rows * QUARTER + 3 * own_rows * hidden),
-        prefetch=1,
-    )(places, in_hbm(dy_rows), down_weight)
-    back_below, back_above = call(
-        join_kernel,
-        1,
-        [whole(*block[0])] * 2 + [whole(*piece[0])] * 2,
-        [(whole(*block[0]), block, far)] * 2,
-        moved=2 * 5 * own_rows * hidden,
-    )(in_hbm(back_below), in_hbm(back_above), far_first, far_second)
-    left_part, right_part = both_ways(back_above, back_below)
+        (*down_space, *masks),
+        flops=2 * own_rows * QUARTER * hidden,
+        moved=2 * (QUARTER * hidden + packed8 * WIDE + all_rows * QUARTER + own_rows * hidden),
+    )(dy_late, down_weight)
     first, second, weighted_own, slot_own = call(
         activate_kernel,
         1,
@@ -484,50 +577,50 @@
     below_first, above_second = both_ways(first, second)
     below_second, above_first = both_ways(second, first)
 
-    def row_grad(shift, grads, extra, own_block=False):
+    def row_grad(turns, grads, extra, own_block=False):
         count = len(grads)
-        blocks = count // 2
-        landing = pl.BlockSpec((ROWS8, WIDE), lambda i, at: (at[shift + i], 0))
+        blocks = len(turns)
+        dma = pltpu.SemaphoreType.DMA
         return call(
-            functools.partial(row_grad_kernel, blocks, own_block),
-            blocks,
-            [whole(half, 2 * hidden)] * count
-            + [ANY, ANY, whole(own_rows, 128) if own_block else ANY],
-            [(landing, ((packed8, WIDE), BF16), far)],
-            (pltpu.VMEM((blocks * SLOTS, QUARTER), BF16), *two_weights),
-            aliases={} if own_block else {count + 3: 0},
+            functools.partial(row_grad_kernel, turns, own_block),
+            1,
+            [ANY] * (count + 2) + [whole(own_rows, 128) if own_block else ANY],
+            [(ANY, ((packed8, WIDE), BF16), far)],
+            (
+                pltpu.VMEM((blocks * SLOTS, 2 * hidden), BF16),
+                pltpu.VMEM((blocks * SLOTS, QUARTER), BF16),
+                pltpu.VMEM((blocks * ROWS8, WIDE), BF16),
+                pltpu.VMEM((QUARTER, hidden), BF16),
+                pltpu.VMEM((QUARTER, hidden), BF16),
+                dma((count,)),
+                dma((3,)),
+                dma((3,)),
+                dma((2 * blocks,)),
+            ),
+            aliases={} if own_block else {count + 2: 0},
             flops=4 * blocks * own_rows * QUARTER * hidden,
             moved=2 * (2 * QUARTER * hidden + blocks * (ROWS8 * WIDE + own_rows * 2 * hidden)),
-            prefetch=1,
-        )(places, *grads, gate_weight, up_weight, extra)[0]
+        )(*grads, gate_weight, up_weight, extra)[0]
 
     own_halves = (in_hbm(first), in_hbm(second))
-    back_send = row_grad(0, own_halves, in_hbm(slot_own), own_block=True)
+    back_send = row_grad((0,), own_halves, in_hbm(slot_own), own_block=True)
     below_first, above_second, back_send = tie((below_first, above_second, back_send))
     across_first, across_second = both_ways(below_first, above_second)
-    back_send = row_grad(1, (below_first, below_second, above_first, above_second), back_send)
+    near_halves = (below_first, below_second, above_first, above_second)
+    back_send = row_grad((sp_count - 1, 1), near_halves, back_send)
     across_first, across_second, back_send = tie((across_first, across_second, back_send))
     weighted_own, _, _ = tie((weighted_own, below_second, above_first))
     weighted = lax.all_gather(weighted_own, "sp", axis=0, tiled=True)
-    back_send = row_grad(3, (across_first, across_second), back_send)
+    back_send = row_grad((2,), (across_first, across_second), back_send)
     back_packed = exchange(back_send)
-    below, above, across = (places[j] for j in (1, 2, 3))
-    pieces_of = (
-        (own, 0, first),
-        (own, half, second),
-        (below, 0, below_first),
-        (below, half, below_second),
-        (above, 0, above_first),
-        (above, half, above_second),
-        (across, 0, across_first),
-        (across, half, across_second),
-    )
-    grads_all = jnp.zeros((all_rows, 2 * hidden), BF16)
-    grads_all, _ = tie((grads_all, back_send))
-    for at, shift, grads in pieces_of:
-        grads_all = lax.dynamic_update_slice_in_dim(
-            grads_all, grads, at * own_rows + shift, axis=0
-        )
+    (grads_all,) = call(
+        assemble_kernel,
+        1,
+        [ANY] * 8,
+        [(whole(all_rows, 2 * hidden), ((all_rows, 2 * hidden), BF16), near)],
+        (pltpu.SemaphoreType.DMA((8,)),),
+        moved=2 * 2 * all_rows * 2 * hidden,
+    )(*tie((*own_halves, *near_halves, across_first, across_second, back_send))[:8])
     contract_rows = (((0,), (0,)), ((), ()))
 
     def over_rows(a, b):
@@ -542,18 +635,18 @@
         [whole(TOP, TOK), whole(3, ROWS8, ROWS8), whole(4, TOK, ROWS8), rows_of(ROWS8, WIDE)],
         [
             (cols_of(TOK, QUARTER), ((TOK, model), BF16), near),
-            (whole(TOP, TOK), ((TOP, TOK), F32), near),
+            (whole(TOP, TOK), ((TOP, TOK), BF16), near),
         ],
         (pltpu.VMEM((ROWS8, 128), F32),),
         flops=2 * packed8 * WIDE * TOK * 2,
         moved=2 * (packed8 * WIDE + TOK * model),
-    )(in_hbm(ids), in_hbm(left), in_hbm(combine), back_packed)
+    )(ids, left, combine, back_packed)
     return (
         grad_in,
         grad_gate_weight[None],
         grad_up_weight[None],
         grad_down_weight[None],
-        grad_probs.astype(BF16).T,
+        grad_probs.T,
     )
 
 

time: 236 us -> 231 us (0.979)
  Pallas kernels: 69.3 us -> 64.9 us
  waiting for transfers between devices: 85.9 us -> 89.2 us
    ppermute x10, waiting for transfers between devices: 8.3 us -> 12.7 us  [both_ways(): return (lax.ppermute(up, 'sp', upward), lax.ppermute(down, 'sp', downward))]
    unnamed x26, local copies, waits for them, and re-layouts: 3.59 us -> 6.1 us
    pallas_call x6 -> x8, Pallas kernels: 50.3 us -> 49.1 us  [the longest x3 22.3 us: row_grad(): call(functools.partial(row_grad_kernel, turns, own_block), 1, [ANY] * (co...]
  transfers between devices with their start and end apart: 15 -> 15, of which waited for: 5 -> 9; matrix products, arithmetic and copies ran while one was open for 7% -> 7% of each run, Pallas kernels for 24% -> 23%
where the time goes in v4:
time: 231 us
  waiting for transfers between devices  89.2 us (39%)
  Pallas kernels  64.9 us (28%)
  starting transfers between devices  40.7 us (18%)
  matrix products  15.6 us (7%)
  between operations  14.2 us (6%)
  local copies, waits for them, and re-layouts  6.1 us (3%)
    all_to_all x3, waiting for transfers between devices, exchange(): lax.all_to_all(pieced, ('sp', 'ep'), split_axis=0, concat_axis=0, tiled=T...  76.4 us
    all_to_all x3, starting transfers between devices, exchange(): lax.all_to_all(pieced, ('sp', 'ep'), split_axis=0, concat_axis=0, tiled=T...  28.7 us
    pallas_call x3, Pallas kernels, row_grad(): call(functools.partial(row_grad_kernel, turns, own_block), 1, [ANY] * (co...  22.3 us
    dot_general x3, matrix products, over_rows(): lax.dot_general(a, b, contract_rows, preferred_element_type=F32)  15.6 us
    ppermute x10, waiting for transfers between devices, both_ways(): return (lax.ppermute(up, 'sp', upward), lax.ppermute(down, 'sp', downward))  12.7 us
    ppermute x10, starting transfers between devices, both_ways(): return (lax.ppermute(up, 'sp', upward), lax.ppermute(down, 'sp', downward))  11.8 us
    pallas_call x1, Pallas kernels, on_device(): call(gate_up_kernel, 2, [ANY, ANY, ANY], [(rows_of(some_rows, QUARTER), (...  11.4 us
    unnamed x26, local copies, waits for them, and re-layouts  6.1 us
  transfers between devices with their start and end apart: 15, of which 9 were waited for; matrix products, arithmetic and copies ran while one was open for 7% of the time, Pallas kernels for 23%

profile of v4, /device:TPU:1, one launch (start us, length us, event | category | flops | bytes accessed | tf_op | source)
XLA Modules:
  0.0 230.6 jit_solution(10898656425206719943)
XLA Ops:
  7.2 5.0 %shard_map.110 = (bf16[1024,1280]{1,0:T(8,128)(2,1)}, bf16[3,256,256]{2,1,0:T(8,128)(2,1)}, bf16[4,128,256]{2,1,0:T(8,128)(2,1)}, bf16[256,128]{1,0:T(8,128)(2,1)}) custom-call(s32[8,128]{1,0:T(8,128)} %bitcast.26, f32[8,128]{1,0:T(8,128)} %bitcast.43, bf16[128,6656]{1,0:T(8,128)(2,1)} %x_ref.2), custom_call_target="tpu_custom_call" | custom-call | flops 671088640 | bytes 4325376 | tf_op jit(solution)/shard_map/pallas_call | solution.py:454
  12.2 11.5 %all-to-all-start = ((bf16[128,8,1280]{2,1,0:T(8,128)(2,1)}), bf16[128,8,1280]{2,1,0:T(8,128)(2,1)S(1)}, u32[]{:S(2)}, u32[]{:S(2)}) async-start(bf16[128,8,1280]{2,1,0:T(8,128)(2,1)} %bitcast.42), calls=%async_computation | async-start | bytes 5242880 | tf_op jit(solution)/shard_map/all_to_all | solution.py:478
  23.7 4.6 %shard_map.111 = bf16[1024,1280]{1,0:T(8,128)(2,1)} custom-call(bf16[3,256,256]{2,1,0:T(8,128)(2,1)} %get-tuple-element.45.left_ref, bf16[256,128]{1,0:T(8,128)(2,1)} %get-tuple-element.48.spare_ref, bf16[128,6656]{1,0:T(8,128)(2,1)} %x_ref.3), custom_call_target="tpu_custom_call" | custom-call | flops 671088640 | bytes 4325376 | tf_op jit(solution)/shard_map/pallas_call | solution.py:467
  28.3 31.5 %all-to-all-done = bf16[128,8,1280]{2,1,0:T(8,128)(2,1)S(1)} async-done(((bf16[128,8,1280]{2,1,0:T(8,128)(2,1)}), bf16[128,8,1280]{2,1,0:T(8,128)(2,1)S(1)}, u32[]{:S(2)}, u32[]{:S(2)}) %all-to-all-start) | async-done | bytes 2621472 | tf_op jit(solution)/shard_map/all_to_all | solution.py:478
  59.8 1.5 copy-done.11
  61.3 4.5 %all-to-all-start.1 = ((bf16[128,8,1280]{2,1,0:T(8,128)(2,1)}), bf16[128,8,1280]{2,1,0:T(8,128)(2,1)S(1)}, u32[]{:S(2)}, u32[]{:S(2)}) async-start(bf16[128,8,1280]{2,1,0:T(8,128)(2,1)} %bitcast.40), calls=%async_computation.2 | async-start | bytes 5242880 | tf_op jit(solution)/shard_map/all_to_all | solution.py:478
  65.9 11.4 %shard_map.112 = (bf16[768,1664]{1,0:T(8,128)(2,1)}, bf16[768,2048]{1,0:T(8,128)(2,1)}) custom-call(bf16[1024,1280]{1,0:T(8,128)(2,1)} %bitcast.41, bf16[1664,1024]{1,0:T(8,128)(2,1)} %bitcast.29, bf16[1664,1024]{1,0:T(8,128)(2,1)} %bitcast.33), custom_call_target="tpu_custom_call" | custom-call | flops 5234491392 | bytes 15138816 | tf_op jit(solution)/shard_map/pallas_call | solution.py:489
  77.4 30.4 %all-to-all-done.1 = bf16[128,8,1280]{2,1,0:T(8,128)(2,1)S(1)} async-done(((bf16[128,8,1280]{2,1,0:T(8,128)(2,1)}), bf16[128,8,1280]{2,1,0:T(8,128)(2,1)S(1)}, u32[]{:S(2)}, u32[]{:S(2)}) %all-to-all-start.1) | async-done | bytes 2621472 | tf_op jit(solution)/shard_map/all_to_all | solution.py:478
  107.8 3.9 %shard_map.114 = (bf16[96,1024]{1,0:T(8,128)(2,1)S(1)}, bf16[96,1024]{1,0:T(8,128)(2,1)S(1)}) custom-call(bf16[1024,1280]{1,0:T(8,128)(2,1)S(1)} %bitcast.22, bf16[1024,1664]{1,0:T(8,128)(2,1)} %bitcast.37), custom_call_target="tpu_custom_call" | custom-call | flops 83751862272 | bytes 8585216 | tf_op jit(solution)/shard_map/pallas_call | solution.py:523
  112.1 2.4 %collective-permute-start.1 = (bf16[96,1024]{1,0:T(8,128)(2,1)S(1)}, bf16[96,1024]{1,0:T(8,128)(2,1)S(1)}, u32[]{:S(2)}, u32[]{:S(2)}) collective-permute-start(bf16[96,1024]{1,0:T(8,128)(2,1)S(1)} %get-tuple-element.56), channel_id=1, source_target_pairs={{0,3},{1,0},{2,1},{3,2},{4,7},{5,4},{6,5},{7,6},{8,11},{9,8},{10,9... | collective-permute-start | bytes 589832 | tf_op jit(solution)/shard_map/ppermute | solution.py:508
  114.5 5.2 %shard_map.113 = (bf16[192,1024]{1,0:T(8,128)(2,1)S(1)}, bf16[192,1024]{1,0:T(8,128)(2,1)S(1)}) custom-call(bf16[1024,1280]{1,0:T(8,128)(2,1)S(1)} %bitcast.23, bf16[1024,1664]{1,0:T(8,128)(2,1)} %bitcast.38), custom_call_target="tpu_custom_call" | custom-call | flops 1308622848 | bytes 5505024 | tf_op jit(solution)/shard_map/pallas_call | solution.py:533
  119.7 3.9 %collective-permute-done.first_ref = bf16[96,1024]{1,0:T(8,128)(2,1)S(1)} collective-permute-done((bf16[96,1024]{1,0:T(8,128)(2,1)S(1)}, bf16[96,1024]{1,0:T(8,128)(2,1)S(1)}, u32[]{:S(2)}, u32[]{:S(2)}) %collective-permute-start) | collective-permute-done | bytes 196640 | tf_op jit(solution)/shard_map/ppermute | solution.py:508
  123.7 2.2 collective-permute-start.3
  125.9 4.9 %shard_map.116 = (bf16[768,1664]{1,0:T(8,128)(2,1)}, bf16[192,1024]{1,0:T(8,128)(2,1)}, bf16[192,128]{1,0:T(8,128)(2,1)}) custom-call(bf16[1024,1280]{1,0:T(8,128)(2,1)S(1)} %bitcast.24, bf16[1024,1664]{1,0:T(8,128)(2,1)} %bitcast.39), custom_call_target="tpu_custom_call" | custom-call | flops 654311424 | bytes 8978432 | tf_op jit(solution)/shard_map/pallas_call | solution.py:551
  130.8 2.2 collective-permute-done.3.right_ref
  132.9 3.1 %collective-permute-done.2.left_ref = bf16[192,1024]{1,0:T(8,128)(2,1)S(1)} collective-permute-done((bf16[192,1024]{1,0:T(8,128)(2,1)S(1)}, bf16[192,1024]{1,0:T(8,128)(2,1)S(1)}, u32[]{:S(2)}, u32[]{:S(2)}) %collective-permute-start.2) | collective-permute-done | bytes 393248 | tf_op jit(solution)/shard_map/ppermute | solution.py:508
  136.1 2.9 %shard_map.117 = (bf16[96,2048]{1,0:T(8,128)(2,1)}, bf16[96,2048]{1,0:T(8,128)(2,1)}, bf16[192,1024]{1,0:T(8,128)(2,1)}, bf16[192,128]{1,0:T(8,128)(2,1)}) custom-call(bf16[192,2048]{1,0:T(8,128)(2,1)} %reduce-scatter.2.cloned.1.call-done.gate_up_ref, bf16[192,1024]{1,0:T(8,128)(2,1)} %get-tuple-element.59.own_ref, ...), custom_call_target="tpu_custom_call" | custom-call | flops 3932160 | bytes 2359296 | tf_op jit(solution)/shard_map/pallas_call | solution.py:564
  139.0 2.7 %collective-permute-start.5 = (bf16[96,2048]{1,0:T(8,128)(2,1)}, bf16[96,2048]{1,0:T(8,128)(2,1)S(1)}, u32[]{:S(2)}, u32[]{:S(2)}) collective-permute-start(bf16[96,2048]{1,0:T(8,128)(2,1)} %get-tuple-element.74.refs_1_), channel_id=1, source_target_pairs={{0,3},{1,0},{2,1},{3,2},{4,7},{5,4},{6,5},{7,6},{8,11},{9,8},{10,9... | collective-permute-start | bytes 1179656 | tf_op jit(solution)/shard_map/ppermute | solution.py:508
  141.7 1.4 collective-permute-start.8
  143.1 7.8 %shard_map.118.refs_6_ = bf16[1024,1280]{1,0:T(8,128)(2,1)} custom-call(bf16[96,2048]{1,0:T(8,128)(2,1)} %get-tuple-element.73.refs_0_, bf16[96,2048]{1,0:T(8,128)(2,1)} %get-tuple-element.74.refs_1_, bf16[1664,1024]{1,0:T(8,128)(2,1)} %bitcast.30, bf16[1664,1024]{1,0:T(8,128)(2,1)} %bitcast.34, bf16[192,128]{1,0:T(8,128)(2,1)} %get-tuple-element.64.refs_4_), custom_call_target="tpu_custom_call" | custom-call | flops 1308622848 | bytes 8257536 | tf_op jit(solution)/shard_map/pallas_call | solution.py:584
  151.1 2.7 %collective-permute-start.7 = (bf16[96,2048]{1,0:T(8,128)(2,1)S(1)}, bf16[96,2048]{1,0:T(8,128)(2,1)S(1)}, u32[]{:S(2)}, u32[]{:S(2)}) collective-permute-start(bf16[96,2048]{1,0:T(8,128)(2,1)S(1)} %collective-permute-done.5.refs_3_.refs_5_), channel_id=1, source_target_pairs={{0,3},{1,0},{2,1},{3,2},{4,7},{5,4},{6,5},{7,6},{8,11},{9,8},{10,9... | collective-permute-start | bytes 1179656 | tf_op jit(solution)/shard_map/ppermute | solution.py:508
  153.8 2.2 collective-permute-done.9.refs_2_.refs_4_
  156.9 8.0 %shard_map.119.refs_4_ = bf16[1024,1280]{1,0:T(8,128)(2,1)} custom-call(bf16[96,2048]{1,0:T(8,128)(2,1)S(1)} %collective-permute-done.4.refs_0_.refs_2_, bf16[96,2048]{1,0:T(8,128)(2,1)S(1)} %collective-permute-done.8.refs_1_.refs_3_, bf16[96,2048]{1,0:T(8,128)(2,1)S(1)} %collective-permute-done.9.refs_2_.refs_4_, ...), custom_call_target="tpu_custom_call", output_to_operand_aliasing={{}: (6, {})} | custom-call | flops 2617245696 | bytes 9699328 | tf_op jit(solution)/shard_map/pallas_call | solution.py:584
  165.3 6.5 %shard_map.120 = bf16[1024,1280]{1,0:T(8,128)(2,1)} custom-call(bf16[96,2048]{1,0:T(8,128)(2,1)S(1)} %collective-permute-done.6.refs_0_.refs_6_, bf16[96,2048]{1,0:T(8,128)(2,1)S(1)} %collective-permute-done.7.refs_1_.refs_7_, bf16[1664,1024]{1,0:T(8,128)(2,1)} %bitcast.32, bf16[1664,1024]{1,0:T(8,128)(2,1)} %bitcast.36, ...), custom_call_target="tpu_custom_call", output_to_operand_aliasing={{}: (4, {})} | custom-call | flops 1308622848 | bytes 8257536 | tf_op jit(solution)/shard_map/pallas_call | solution.py:584
  171.8 12.7 %all-to-all-start.2 = ((bf16[128,8,1280]{2,1,0:T(8,128)(2,1)}), bf16[128,8,1280]{2,1,0:T(8,128)(2,1)S(1)}, u32[]{:S(2)}, u32[]{:S(2)}) async-start(bf16[128,8,1280]{2,1,0:T(8,128)(2,1)} %bitcast.28), calls=%async_computation.3 | async-start | bytes 5242880 | tf_op jit(solution)/shard_map/all_to_all | solution.py:478
  186.6 1.0 copy-done.6
  188.6 1.3 shard_map.122
  190.5 4.2 %fusion.1 = bf16[1,1664,1024]{2,1,0:T(8,128)(2,1)} fusion(bf16[768,1664]{1,0:T(8,128)(2,1)S(1)} %copy-done.12, bf16[768,2048]{1,0:T(8,128)(2,1)S(1)} %shard_map.122), kind=kOutput, calls=%fused_computation.4 | convolution fusion | flops 2618949632 | bytes 7536640 | tf_op jit(solution)/shard_map/dot_general | solution.py:627
  194.8 4.2 %fusion = bf16[1,1664,1024]{2,1,0:T(8,128)(2,1)} fusion(bf16[768,1664]{1,0:T(8,128)(2,1)S(1)} %copy-done.12, bf16[768,2048]{1,0:T(8,128)(2,1)S(1)} %shard_map.122), kind=kOutput, calls=%fused_computation.3 | convolution fusion | flops 2618949632 | bytes 7536640 | tf_op jit(solution)/shard_map/dot_general | solution.py:627
  199.0 7.1 %fusion.2 = bf16[1,1024,1664]{2,1,0:T(8,128)(2,1)} fusion(bf16[768,1024]{1,0:T(8,128)(2,1)} %all-gather.2.cloned.1.call-done, bf16[768,1664]{1,0:T(8,128)(2,1)} %get-tuple-element.83), kind=kOutput, calls=%fused_computation.5 | convolution fusion | flops 2618949632 | bytes 7536640 | tf_op jit(solution)/shard_map/dot_general | solution.py:627
  206.1 14.5 %all-to-all-done.2 = bf16[128,8,1280]{2,1,0:T(8,128)(2,1)S(1)} async-done(((bf16[128,8,1280]{2,1,0:T(8,128)(2,1)}), bf16[128,8,1280]{2,1,0:T(8,128)(2,1)S(1)}, u32[]{:S(2)}, u32[]{:S(2)}) %all-to-all-start.2) | async-done | bytes 2621472 | tf_op jit(solution)/shard_map/all_to_all | solution.py:478
  220.7 3.1 %shard_map.121 = (bf16[128,6656]{1,0:T(8,128)(2,1)}, bf16[8,128]{1,0:T(8,128)(2,1)}) custom-call(s32[8,128]{1,0:T(8,128)S(1)} %bitcast.27, bf16[3,256,256]{2,1,0:T(8,128)(2,1)S(1)} %copy-done, bf16[4,128,256]{2,1,0:T(8,128)(2,1)S(1)} %copy-done.9, bf16[1024,1280]{1,0:T(8,128)(2,1)S(1)} %bitcast.25), custom_call_target="tpu_custom_call" | custom-call | flops 671088640 | bytes 4325376 | tf_op jit(solution)/shard_map/pallas_call | solution.py:632
  (42 shorter events, 5.6 us)
Async XLA Ops:
  12.2 47.6 %all-to-all-start = ((bf16[128,8,1280]{2,1,0:T(8,128)(2,1)}), bf16[128,8,1280]{2,1,0:T(8,128)(2,1)S(1)}, u32[]{:S(2)}, u32[]{:S(2)}) async-start(bf16[128,8,1280]{2,1,0:T(8,128)(2,1)} %bitcast.42), calls=%async_computation | async-start | bytes 5242880 | tf_op jit(solution)/shard_map/all_to_all | solution.py:478
  59.8 1.5 copy-start.11
  61.3 46.5 %all-to-all-start.1 = ((bf16[128,8,1280]{2,1,0:T(8,128)(2,1)}), bf16[128,8,1280]{2,1,0:T(8,128)(2,1)S(1)}, u32[]{:S(2)}, u32[]{:S(2)}) async-start(bf16[128,8,1280]{2,1,0:T(8,128)(2,1)} %bitcast.40), calls=%async_computation.2 | async-start | bytes 5242880 | tf_op jit(solution)/shard_map/all_to_all | solution.py:478
  65.8 70.3 %reduce-scatter.2.cloned.1.call-start = ((), (), s32[]{:S(2)}) async-start(), calls=%async_computation.4 | async-start | bytes 3932160 | tf_op jit(solution)/shard_map/reduce_scatter | solution.py:501
  77.3 121.7 %all-gather.2.cloned.1.call-start = ((), (), s32[]{:S(2)}) async-start(), calls=%async_computation.5 | async-start | bytes 1966080 | tf_op jit(solution)/shard_map/all_gather | solution.py:613
  111.7 11.8 %collective-permute-start = (bf16[96,1024]{1,0:T(8,128)(2,1)S(1)}, bf16[96,1024]{1,0:T(8,128)(2,1)S(1)}, u32[]{:S(2)}, u32[]{:S(2)}) collective-permute-start(bf16[96,1024]{1,0:T(8,128)(2,1)S(1)} %get-tuple-element.55), channel_id=1, source_target_pairs={{0,1},{1,2},{2,3},{3,0},{4,5},{5,6},{6,7},{7,4},{8,9},{9,10},{10,1... | collective-permute-start | bytes 589832 | tf_op jit(solution)/shard_map/ppermute | solution.py:508
  112.1 11.4 %collective-permute-start.1 = (bf16[96,1024]{1,0:T(8,128)(2,1)S(1)}, bf16[96,1024]{1,0:T(8,128)(2,1)S(1)}, u32[]{:S(2)}, u32[]{:S(2)}) collective-permute-start(bf16[96,1024]{1,0:T(8,128)(2,1)S(1)} %get-tuple-element.56), channel_id=1, source_target_pairs={{0,3},{1,0},{2,1},{3,2},{4,7},{5,4},{6,5},{7,6},{8,11},{9,8},{10,9... | collective-permute-start | bytes 589832 | tf_op jit(solution)/shard_map/ppermute | solution.py:508
  123.7 9.3 %collective-permute-start.3 = (bf16[192,1024]{1,0:T(8,128)(2,1)S(1)}, bf16[192,1024]{1,0:T(8,128)(2,1)S(1)}, u32[]{:S(2)}, u32[]{:S(2)}) collective-permute-start(bf16[192,1024]{1,0:T(8,128)(2,1)S(1)} %get-tuple-element.60), channel_id=1, source_target_pairs={{0,3},{1,0},{2,1},{3,2},{4,7},{5,4},{6,5},{7,6},{8,11},{9,8},{10,9... | collective-permute-start | bytes 1179656 | tf_op jit(solution)/shard_map/ppermute | solution.py:508
  125.9 10.2 %collective-permute-start.2 = (bf16[192,1024]{1,0:T(8,128)(2,1)S(1)}, bf16[192,1024]{1,0:T(8,128)(2,1)S(1)}, u32[]{:S(2)}, u32[]{:S(2)}) collective-permute-start(bf16[192,1024]{1,0:T(8,128)(2,1)S(1)} %get-tuple-element.57), channel_id=1, source_target_pairs={{0,1},{1,2},{2,3},{3,0},{4,5},{5,6},{6,7},{7,4},{8,9},{9,10},{10,1... | collective-permute-start | bytes 1179656 | tf_op jit(solution)/shard_map/ppermute | solution.py:508
  139.0 12.0 %collective-permute-start.4 = (bf16[96,2048]{1,0:T(8,128)(2,1)}, bf16[96,2048]{1,0:T(8,128)(2,1)S(1)}, u32[]{:S(2)}, u32[]{:S(2)}) collective-permute-start(bf16[96,2048]{1,0:T(8,128)(2,1)} %get-tuple-element.73.refs_0_), channel_id=1, source_target_pairs={{0,1},{1,2},{2,3},{3,0},{4,5},{5,6},{6,7},{7,4},{8,9},{9,10},{10,1... | collective-permute-start | bytes 1179656 | tf_op jit(solution)/shard_map/ppermute | solution.py:508
  139.0 12.0 %collective-permute-start.5 = (bf16[96,2048]{1,0:T(8,128)(2,1)}, bf16[96,2048]{1,0:T(8,128)(2,1)S(1)}, u32[]{:S(2)}, u32[]{:S(2)}) collective-permute-start(bf16[96,2048]{1,0:T(8,128)(2,1)} %get-tuple-element.74.refs_1_), channel_id=1, source_target_pairs={{0,3},{1,0},{2,1},{3,2},{4,7},{5,4},{6,5},{7,6},{8,11},{9,8},{10,9... | collective-permute-start | bytes 1179656 | tf_op jit(solution)/shard_map/ppermute | solution.py:508
  141.7 14.3 %collective-permute-start.9 = (bf16[96,2048]{1,0:T(8,128)(2,1)}, bf16[96,2048]{1,0:T(8,128)(2,1)S(1)}, u32[]{:S(2)}, u32[]{:S(2)}) collective-permute-start(bf16[96,2048]{1,0:T(8,128)(2,1)} %get-tuple-element.73.refs_0_), channel_id=1, source_target_pairs={{0,3},{1,0},{2,1},{3,2},{4,7},{5,4},{6,5},{7,6},{8,11},{9,8},{10,9... | collective-permute-start | bytes 1179656 | tf_op jit(solution)/shard_map/ppermute | solution.py:508
  141.7 15.2 %collective-permute-start.8 = (bf16[96,2048]{1,0:T(8,128)(2,1)}, bf16[96,2048]{1,0:T(8,128)(2,1)S(1)}, u32[]{:S(2)}, u32[]{:S(2)}) collective-permute-start(bf16[96,2048]{1,0:T(8,128)(2,1)} %get-tuple-element.74.refs_1_), channel_id=1, source_target_pairs={{0,1},{1,2},{2,3},{3,0},{4,5},{5,6},{6,7},{7,4},{8,9},{9,10},{10,1... | collective-permute-start | bytes 1179656 | tf_op jit(solution)/shard_map/ppermute | solution.py:508
  151.0 13.9 %copy-start.1 = (bf16[96,2048]{1,0:T(8,128)(2,1)}, bf16[96,2048]{1,0:T(8,128)(2,1)S(1)}, u32[]{:S(2)}) copy-start(bf16[96,2048]{1,0:T(8,128)(2,1)S(1)} %collective-permute-done.4.refs_0_.refs_2_) | copy-start | bytes 1179652
  151.0 13.9 %copy-start.3 = (bf16[96,2048]{1,0:T(8,128)(2,1)}, bf16[96,2048]{1,0:T(8,128)(2,1)S(1)}, u32[]{:S(2)}) copy-start(bf16[96,2048]{1,0:T(8,128)(2,1)S(1)} %collective-permute-done.5.refs_3_.refs_5_) | copy-start | bytes 1179652
  151.0 14.3 %collective-permute-start.6 = (bf16[96,2048]{1,0:T(8,128)(2,1)S(1)}, bf16[96,2048]{1,0:T(8,128)(2,1)S(1)}, u32[]{:S(2)}, u32[]{:S(2)}) collective-permute-start(bf16[96,2048]{1,0:T(8,128)(2,1)S(1)} %collective-permute-done.4.refs_0_.refs_2_), channel_id=1, source_target_pairs={{0,1},{1,2},{2,3},{3,0},{4,5},{5,6},{6,7},{7,4},{8,9},{9,10},{10,1... | collective-permute-start | bytes 1179656 | tf_op jit(solution)/shard_map/ppermute | solution.py:508
  151.1 14.2 %collective-permute-start.7 = (bf16[96,2048]{1,0:T(8,128)(2,1)S(1)}, bf16[96,2048]{1,0:T(8,128)(2,1)S(1)}, u32[]{:S(2)}, u32[]{:S(2)}) collective-permute-start(bf16[96,2048]{1,0:T(8,128)(2,1)S(1)} %collective-permute-done.5.refs_3_.refs_5_), channel_id=1, source_target_pairs={{0,3},{1,0},{2,1},{3,2},{4,7},{5,4},{6,5},{7,6},{8,11},{9,8},{10,9... | collective-permute-start | bytes 1179656 | tf_op jit(solution)/shard_map/ppermute | solution.py:508
  156.0 8.9 %copy-start.5 = (bf16[96,2048]{1,0:T(8,128)(2,1)}, bf16[96,2048]{1,0:T(8,128)(2,1)S(1)}, u32[]{:S(2)}) copy-start(bf16[96,2048]{1,0:T(8,128)(2,1)S(1)} %collective-permute-done.9.refs_2_.refs_4_) | copy-start | bytes 1179652
  156.9 8.0 %copy-start.7 = (bf16[96,2048]{1,0:T(8,128)(2,1)}, bf16[96,2048]{1,0:T(8,128)(2,1)S(1)}, u32[]{:S(2)}) copy-start(bf16[96,2048]{1,0:T(8,128)(2,1)S(1)} %collective-permute-done.8.refs_1_.refs_3_) | copy-start | bytes 1179652
  171.8 48.8 %all-to-all-start.2 = ((bf16[128,8,1280]{2,1,0:T(8,128)(2,1)}), bf16[128,8,1280]{2,1,0:T(8,128)(2,1)S(1)}, u32[]{:S(2)}, u32[]{:S(2)}) async-start(bf16[128,8,1280]{2,1,0:T(8,128)(2,1)} %bitcast.28), calls=%async_computation.3 | async-start | bytes 5242880 | tf_op jit(solution)/shard_map/all_to_all | solution.py:478
  184.6 1.0 copy-start.2
  185.6 1.0 copy-start.4
  186.6 1.0 copy-start.6
  187.6 1.0 copy-start.8
  188.6 2.0 copy-start.12
  199.0 21.6 %copy-start = (bf16[3,256,256]{2,1,0:T(8,128)(2,1)S(1)}, bf16[3,256,256]{2,1,0:T(8,128)(2,1)}, u32[]{:S(2)}) copy-start(bf16[3,256,256]{2,1,0:T(8,128)(2,1)} %get-tuple-element.45.left_ref) | copy-start | bytes 1179652
  199.0 21.6 %copy-start.9 = (bf16[4,128,256]{2,1,0:T(8,128)(2,1)S(1)}, bf16[4,128,256]{2,1,0:T(8,128)(2,1)}, u32[]{:S(2)}) copy-start(bf16[4,128,256]{2,1,0:T(8,128)(2,1)} %get-tuple-element.46.combine_ref) | copy-start | bytes 786436
  199.0 21.6 %copy-start.10 = (s32[128,8]{0,1:T(8,128)S(1)}, s32[128,8]{0,1:T(8,128)}, u32[]{:S(2)}) copy-start(s32[128,8]{0,1:T(8,128)} %param.9) | copy-start | bytes 12292
Sparse Core Ops, SparseCore 0:
  77.5 50.3 reduce-scatter.1
  157.1 31.2 all-gather.1

commit v5 on v4

--- a/solution.py
+++ b/solution.py
@@ -40,29 +40,39 @@
     return jnp.where(mask, 1.0, 0.0)
 
 
-def tables(ids, probs, left_ref, combine_ref, spare_ref):
+def ranked(ids, probs=None):
     expert = iota((EXPERTS, TOK), 0)
     member = jnp.zeros((EXPERTS, TOK), F32)
     weight = jnp.zeros((EXPERTS, TOK), F32)
     for k in range(TOP):
         hit = ids[k : k + 1, :] == expert
         member = member + jnp.where(hit, 1.0, 0.0)
-        weight = weight + jnp.where(hit, probs[k : k + 1, :], 0.0)
+        if probs is not None:
+            weight = weight + jnp.where(hit, probs[k : k + 1, :], 0.0)
     member = member.astype(BF16)
     before = one_hot(iota((TOK, TOK), 0) < iota((TOK, TOK), 1)).astype(BF16)
-    rank = product(member, before).astype(BF16)
+    rank = jnp.where(member > 0.5, product(member, before), -1.0).astype(BF16)
     widen = one_hot(iota((ROWS8, EXPERTS), 0) // PACKED == iota((ROWS8, EXPERTS), 1)).astype(BF16)
-    member8 = product(widen, member)
-    rank8 = jnp.where(member8 > 0.5, product(widen, rank), -1.0)
-    weight8 = product(widen, weight.astype(BF16))
-    place = iota((ROWS8, TOK), 0) % PACKED
+    rank8 = product(widen, rank)
+    weight8 = None if probs is None else product(widen, weight.astype(BF16))
+    return iota((ROWS8, TOK), 0) % PACKED, rank8, weight8
+
+
+def tables(ids, left_ref):
+    place, rank8, _ = ranked(ids)
     own = one_hot((rank8 == place.astype(F32)) & (place < CAP))
-    combine_ref[0] = own.T.astype(BF16)
     for g in range(3):
         goal = (place - CAP) * 3 + g
         tail = one_hot((rank8 == goal.astype(F32)) & (place >= CAP))
-        combine_ref[g + 1] = tail.T.astype(BF16)
         left_ref[g] = jnp.concatenate([own, tail], axis=1).astype(BF16)
+
+
+def late_tables(ids, probs, left_ref, combine_ref, spare_ref):
+    _, _, weight8 = ranked(ids, probs)
+    own = left_ref[0, :, :TOK].astype(F32)
+    combine_ref[0] = own.T.astype(BF16)
+    for g in range(3):
+        combine_ref[g + 1] = left_ref[g, :, TOK:].astype(F32).T.astype(BF16)
     prob = jnp.sum(own * weight8, axis=1, keepdims=True)
     row = iota((ROWS8, 128), 0)
     diagonal = jnp.where(row % PACKED == iota((ROWS8, 128), 1), prob, 0.0).astype(BF16)
@@ -81,15 +91,19 @@
     return product(left_ref[0][:, :TOK], x_ref[:, 3 * TAIL : WIDE])
 
 
-def spread_x_kernel(ids_ref, probs_ref, x_ref, out_ref, left_ref, combine_ref, spare_ref):
+def spread_x_kernel(ids_ref, x_ref, out_ref, left_ref):
     @pl.when(pl.program_id(0) == 0)
     def _():
-        tables(ids_ref[...], probs_ref[...], left_ref, combine_ref, spare_ref)
+        tables(ids_ref[...], left_ref)
 
     out_ref[:, 3 * TAIL :] = spread(left_ref, x_ref, out_ref).astype(BF16)
 
 
-def spread_dy_kernel(left_ref, spare_ref, x_ref, out_ref):
+def spread_dy_kernel(ids_ref, probs_ref, left_ref, x_ref, out_ref, combine_ref, spare_ref):
+    @pl.when(pl.program_id(0) == 0)
+    def _():
+        late_tables(ids_ref[...], probs_ref[...], left_ref, combine_ref, spare_ref)
+
     last = spread(left_ref, x_ref, out_ref)
     out_ref[:, 3 * TAIL :] = last.astype(BF16) + spare_ref[...]
 
@@ -363,41 +377,39 @@
     finish(copies)
 
 
-def combine_kernel(ids_ref, left_ref, combine_ref, packed_ref, out_ref, probs_ref, slot_ref):
-    step = pl.program_id(0)
-    packed = packed_ref[...]
-    out_ref[:, :WIDE] = product(combine_ref[0], packed).astype(BF16)
+def combine_kernel(ids_ref, left_ref, combine_ref, packed_ref, out_hbm, probs_ref, out_ref, sem):
     tails = jnp.concatenate([combine_ref[g + 1] for g in range(3)], axis=1)
-    out_ref[:, WIDE:] = product(tails, stacked(packed)).astype(BF16)
-    spare = packed[:, 3 * TAIL :].astype(F32)
-
-    @pl.when(step == 0)
-    def _():
-        slot_ref[...] = spare
-
-    @pl.when(step > 0)
-    def _():
-        slot_ref[...] += spare
-
-    @pl.when(step == pl.num_programs(0) - 1)
-    def _():
-        row = iota((ROWS8, 128), 0)
-        slots = jnp.where(row % PACKED == CAP, slot_ref[...], 0.0).astype(BF16)
-        r = iota((ROWS8, ROWS8), 0)
-        c = iota((ROWS8, ROWS8), 1)
-        group = one_hot(r // PACKED == c // PACKED).astype(BF16)
-        wide = product(group, slots)
-        mine = iota((ROWS8, 128), 1) == row % PACKED
-        column = jnp.sum(jnp.where(mine, wide, 0.0), axis=1, keepdims=True)
-        value = (left_ref[0, :, :TOK].astype(F32) * column).astype(BF16)
-        gather = one_hot(iota((EXPERTS, ROWS8), 1) // PACKED == iota((EXPERTS, ROWS8), 0))
-        table = product(gather.astype(BF16), value)
-        expert = iota((EXPERTS, TOK), 0)
-        found = [
-            jnp.sum(jnp.where(ids_ref[k : k + 1, :] == expert, table, 0.0), axis=0, keepdims=True)
-            for k in range(TOP)
-        ]
-        probs_ref[...] = jnp.concatenate(found, axis=0).astype(BF16)
+    spare = jnp.zeros((ROWS8, 128), F32)
+    sent = []
+    for q in range(packed_ref.shape[0] // ROWS8):
+        rows = pl.ds(q * ROWS8, ROWS8)
+        cols = pl.ds(q * QUARTER, QUARTER)
+        low = q * QUARTER
+        out_ref[:, low : low + WIDE] = product(combine_ref[0], packed_ref[rows, :]).astype(BF16)
+        rest = product(tails, stacked(packed_ref[rows, :])).astype(BF16)
+        out_ref[:, low + WIDE : low + QUARTER] = rest
+        copy = pltpu.make_async_copy(out_ref.at[:, cols], out_hbm.at[:, cols], sem.at[q])
+        copy.start()
+        sent.append(copy)
+        spare = spare + packed_ref[rows, 3 * TAIL :].astype(F32)
+    row = iota((ROWS8, 128), 0)
+    slots = jnp.where(row % PACKED == CAP, spare, 0.0).astype(BF16)
+    r = iota((ROWS8, ROWS8), 0)
+    c = iota((ROWS8, ROWS8), 1)
+    group = one_hot(r // PACKED == c // PACKED).astype(BF16)
+    wide = product(group, slots)
+    mine = iota((ROWS8, 128), 1) == row % PACKED
+    column = jnp.sum(jnp.where(mine, wide, 0.0), axis=1, keepdims=True)
+    value = (left_ref[0, :, :TOK].astype(F32) * column).astype(BF16)
+    gather = one_hot(iota((EXPERTS, ROWS8), 1) // PACKED == iota((EXPERTS, ROWS8), 0))
+    table = product(gather.astype(BF16), value)
+    expert = iota((EXPERTS, TOK), 0)
+    found = [
+        jnp.sum(jnp.where(ids_ref[k : k + 1, :] == expert, table, 0.0), axis=0, keepdims=True)
+        for k in range(TOP)
+    ]
+    probs_ref[...] = jnp.concatenate(found, axis=0).astype(BF16)
+    finish(sent)
 
 
 def call(kernel, grid, ins, outs, scratch=(), flops=0, moved=0, aliases=None):
@@ -432,6 +444,7 @@
 
 
 ANY = pl.BlockSpec(memory_space=pl.ANY)
+NEAR = pl.BlockSpec(memory_space=pltpu.VMEM)
 
 
 def on_device(hidden_in, grad_out, route_ids, route_probs, w_gate, w_up, w_down):
@@ -451,27 +464,23 @@
     far, near = pltpu.HBM, jax.ShapeDtypeStruct
     tie = lax.optimization_barrier
     packet = (rows_of(ROWS8, WIDE), ((packed8, WIDE), BF16), far)
-    x_send, left, combine, spare = call(
+    x_send, left = call(
         spread_x_kernel,
         sp_count,
-        [whole(TOP, TOK), whole(TOP, TOK), cols_of(TOK, QUARTER)],
-        [
-            packet,
-            (whole(3, ROWS8, ROWS8), ((3, ROWS8, ROWS8), BF16), far),
-            (whole(4, TOK, ROWS8), ((4, TOK, ROWS8), BF16), far),
-            (whole(ROWS8, 128), ((ROWS8, 128), BF16), far),
-        ],
+        [whole(TOP, TOK), cols_of(TOK, QUARTER)],
+        [packet, (whole(3, ROWS8, ROWS8), ((3, ROWS8, ROWS8), BF16), far)],
         flops=2 * packed8 * WIDE * 256,
         moved=2 * (packed8 * WIDE + TOK * model),
-    )(in_hbm(ids), in_hbm(probs), hidden_in)
-    (dy_send,) = call(
+    )(in_hbm(ids), hidden_in)
+    dy_send, combine = call(
         spread_dy_kernel,
         sp_count,
-        [whole(3, ROWS8, ROWS8), whole(ROWS8, 128), cols_of(TOK, QUARTER)],
-        [packet],
+        [whole(TOP, TOK), whole(TOP, TOK), whole(3, ROWS8, ROWS8), cols_of(TOK, QUARTER)],
+        [packet, (whole(4, TOK, ROWS8), ((4, TOK, ROWS8), BF16), far)],
+        (pltpu.VMEM((ROWS8, 128), BF16),),
         flops=2 * packed8 * WIDE * 256,
         moved=2 * (packed8 * WIDE + TOK * model),
-    )(in_hbm(left), in_hbm(spare), grad_out)
+    )(in_hbm(ids), in_hbm(probs), in_hbm(left), grad_out)
 
     def exchange(packed):
         pieced = packed.reshape(pieces, PACKED, WIDE)
@@ -631,13 +640,13 @@
     grad_down_weight = over_rows(weighted, dy_rows)
     grad_in, grad_probs = call(
         combine_kernel,
-        sp_count,
-        [whole(TOP, TOK), whole(3, ROWS8, ROWS8), whole(4, TOK, ROWS8), rows_of(ROWS8, WIDE)],
+        1,
+        [NEAR, NEAR, NEAR, NEAR],
         [
-            (cols_of(TOK, QUARTER), ((TOK, model), BF16), near),
+            (ANY, ((TOK, model), BF16), far),
             (whole(TOP, TOK), ((TOP, TOK), BF16), near),
         ],
-        (pltpu.VMEM((ROWS8, 128), F32),),
+        (pltpu.VMEM((TOK, model), BF16), pltpu.SemaphoreType.DMA((sp_count,))),
         flops=2 * packed8 * WIDE * TOK * 2,
         moved=2 * (packed8 * WIDE + TOK * model),
     )(ids, left, combine, back_packed)

time: 231 us -> 230 us (level)
  transfers between devices with their start and end apart: 15 -> 15, of which waited for: 9 -> 9; matrix products, arithmetic and copies ran while one was open for 7% -> 7% of each run, Pallas kernels for 23% -> 24%
where the time goes in v5:
time: 230 us
  waiting for transfers between devices  88.7 us (39%)
  Pallas kernels  64.3 us (28%)
  starting transfers between devices  40.7 us (18%)
  matrix products  15.6 us (7%)
  between operations  14.3 us (6%)
  local copies, waits for them, and re-layouts  6.1 us (3%)
    all_to_all x3, waiting for transfers between devices, exchange(): lax.all_to_all(pieced, ('sp', 'ep'), split_axis=0, concat_axis=0, tiled=T...  76 us
    all_to_all x3, starting transfers between devices, exchange(): lax.all_to_all(pieced, ('sp', 'ep'), split_axis=0, concat_axis=0, tiled=T...  28.8 us
    pallas_call x3, Pallas kernels, row_grad(): call(functools.partial(row_grad_kernel, turns, own_block), 1, [ANY] * (co...  22.4 us
    dot_general x3, matrix products, over_rows(): lax.dot_general(a, b, contract_rows, preferred_element_type=F32)  15.6 us
    ppermute x10, waiting for transfers between devices, both_ways(): return (lax.ppermute(up, 'sp', upward), lax.ppermute(down, 'sp', downward))  12.6 us
    ppermute x10, starting transfers between devices, both_ways(): return (lax.ppermute(up, 'sp', upward), lax.ppermute(down, 'sp', downward))  11.8 us
    pallas_call x1, Pallas kernels, on_device(): call(gate_up_kernel, 2, [ANY, ANY, ANY], [(rows_of(some_rows, QUARTER), (...  11.4 us
    unnamed x26, local copies, waits for them, and re-layouts  6.1 us
  transfers between devices with their start and end apart: 15, of which 9 were waited for; matrix products, arithmetic and copies ran while one was open for 7% of the time, Pallas kernels for 24%

profile of v5, /device:TPU:1, one launch (start us, length us, event | category | flops | bytes accessed | tf_op | source)
XLA Modules:
  0.0 229.7 jit_solution(10153730626643617579)
XLA Ops:
  7.2 4.8 %shard_map.110 = (bf16[1024,1280]{1,0:T(8,128)(2,1)}, bf16[3,256,256]{2,1,0:T(8,128)(2,1)}) custom-call(s32[8,128]{1,0:T(8,128)} %bitcast.26, bf16[128,6656]{1,0:T(8,128)(2,1)} %x_ref.2), custom_call_target="tpu_custom_call" | custom-call | flops 671088640 | bytes 4325376 | tf_op jit(solution)/shard_map/pallas_call | solution.py:467
  12.0 11.5 %all-to-all-start = ((bf16[128,8,1280]{2,1,0:T(8,128)(2,1)}), bf16[128,8,1280]{2,1,0:T(8,128)(2,1)S(1)}, u32[]{:S(2)}, u32[]{:S(2)}) async-start(bf16[128,8,1280]{2,1,0:T(8,128)(2,1)} %bitcast.43), calls=%async_computation | async-start | bytes 5242880 | tf_op jit(solution)/shard_map/all_to_all | solution.py:487
  23.5 5.1 %shard_map.111 = (bf16[1024,1280]{1,0:T(8,128)(2,1)}, bf16[4,128,256]{2,1,0:T(8,128)(2,1)}) custom-call(s32[8,128]{1,0:T(8,128)} %bitcast.27, f32[8,128]{1,0:T(8,128)} %bitcast.44, bf16[3,256,256]{2,1,0:T(8,128)(2,1)} %get-tuple-element.45.left_ref, bf16[128,6656]{1,0:T(8,128)(2,1)} %x_ref.3), custom_call_target="tpu_custom_call" | custom-call | flops 671088640 | bytes 4325376 | tf_op jit(solution)/shard_map/pallas_call | solution.py:475
  28.5 31.0 %all-to-all-done = bf16[128,8,1280]{2,1,0:T(8,128)(2,1)S(1)} async-done(((bf16[128,8,1280]{2,1,0:T(8,128)(2,1)}), bf16[128,8,1280]{2,1,0:T(8,128)(2,1)S(1)}, u32[]{:S(2)}, u32[]{:S(2)}) %all-to-all-start) | async-done | bytes 2621472 | tf_op jit(solution)/shard_map/all_to_all | solution.py:487
  59.6 1.5 copy-done.11
  61.1 4.5 %all-to-all-start.1 = ((bf16[128,8,1280]{2,1,0:T(8,128)(2,1)}), bf16[128,8,1280]{2,1,0:T(8,128)(2,1)S(1)}, u32[]{:S(2)}, u32[]{:S(2)}) async-start(bf16[128,8,1280]{2,1,0:T(8,128)(2,1)} %bitcast.41), calls=%async_computation.2 | async-start | bytes 5242880 | tf_op jit(solution)/shard_map/all_to_all | solution.py:487
  65.6 11.4 %shard_map.112 = (bf16[768,1664]{1,0:T(8,128)(2,1)}, bf16[768,2048]{1,0:T(8,128)(2,1)}) custom-call(bf16[1024,1280]{1,0:T(8,128)(2,1)} %bitcast.42, bf16[1664,1024]{1,0:T(8,128)(2,1)} %bitcast.30, bf16[1664,1024]{1,0:T(8,128)(2,1)} %bitcast.34), custom_call_target="tpu_custom_call" | custom-call | flops 5234491392 | bytes 15138816 | tf_op jit(solution)/shard_map/pallas_call | solution.py:498
  77.1 30.4 %all-to-all-done.1 = bf16[128,8,1280]{2,1,0:T(8,128)(2,1)S(1)} async-done(((bf16[128,8,1280]{2,1,0:T(8,128)(2,1)}), bf16[128,8,1280]{2,1,0:T(8,128)(2,1)S(1)}, u32[]{:S(2)}, u32[]{:S(2)}) %all-to-all-start.1) | async-done | bytes 2621472 | tf_op jit(solution)/shard_map/all_to_all | solution.py:487
  107.5 3.9 %shard_map.114 = (bf16[96,1024]{1,0:T(8,128)(2,1)S(1)}, bf16[96,1024]{1,0:T(8,128)(2,1)S(1)}) custom-call(bf16[1024,1280]{1,0:T(8,128)(2,1)S(1)} %bitcast.22, bf16[1024,1664]{1,0:T(8,128)(2,1)} %bitcast.38), custom_call_target="tpu_custom_call" | custom-call | flops 83751862272 | bytes 8585216 | tf_op jit(solution)/shard_map/pallas_call | solution.py:532
  111.9 2.4 %collective-permute-start.1 = (bf16[96,1024]{1,0:T(8,128)(2,1)S(1)}, bf16[96,1024]{1,0:T(8,128)(2,1)S(1)}, u32[]{:S(2)}, u32[]{:S(2)}) collective-permute-start(bf16[96,1024]{1,0:T(8,128)(2,1)S(1)} %get-tuple-element.56), channel_id=1, source_target_pairs={{0,3},{1,0},{2,1},{3,2},{4,7},{5,4},{6,5},{7,6},{8,11},{9,8},{10,9... | collective-permute-start | bytes 589832 | tf_op jit(solution)/shard_map/ppermute | solution.py:517
  114.2 5.2 %shard_map.113 = (bf16[192,1024]{1,0:T(8,128)(2,1)S(1)}, bf16[192,1024]{1,0:T(8,128)(2,1)S(1)}) custom-call(bf16[1024,1280]{1,0:T(8,128)(2,1)S(1)} %bitcast.23, bf16[1024,1664]{1,0:T(8,128)(2,1)} %bitcast.39), custom_call_target="tpu_custom_call" | custom-call | flops 1308622848 | bytes 5505024 | tf_op jit(solution)/shard_map/pallas_call | solution.py:542
  119.4 3.9 %collective-permute-done.first_ref = bf16[96,1024]{1,0:T(8,128)(2,1)S(1)} collective-permute-done((bf16[96,1024]{1,0:T(8,128)(2,1)S(1)}, bf16[96,1024]{1,0:T(8,128)(2,1)S(1)}, u32[]{:S(2)}, u32[]{:S(2)}) %collective-permute-start) | collective-permute-done | bytes 196640 | tf_op jit(solution)/shard_map/ppermute | solution.py:517
  123.4 2.2 collective-permute-start.3
  125.6 4.9 %shard_map.116 = (bf16[768,1664]{1,0:T(8,128)(2,1)}, bf16[192,1024]{1,0:T(8,128)(2,1)}, bf16[192,128]{1,0:T(8,128)(2,1)}) custom-call(bf16[1024,1280]{1,0:T(8,128)(2,1)S(1)} %bitcast.24, bf16[1024,1664]{1,0:T(8,128)(2,1)} %bitcast.40), custom_call_target="tpu_custom_call" | custom-call | flops 654311424 | bytes 8978432 | tf_op jit(solution)/shard_map/pallas_call | solution.py:560
  130.5 2.2 collective-permute-done.3.right_ref
  132.7 3.1 %collective-permute-done.2.left_ref = bf16[192,1024]{1,0:T(8,128)(2,1)S(1)} collective-permute-done((bf16[192,1024]{1,0:T(8,128)(2,1)S(1)}, bf16[192,1024]{1,0:T(8,128)(2,1)S(1)}, u32[]{:S(2)}, u32[]{:S(2)}) %collective-permute-start.2) | collective-permute-done | bytes 393248 | tf_op jit(solution)/shard_map/ppermute | solution.py:517
  135.8 2.9 %shard_map.117 = (bf16[96,2048]{1,0:T(8,128)(2,1)}, bf16[96,2048]{1,0:T(8,128)(2,1)}, bf16[192,1024]{1,0:T(8,128)(2,1)}, bf16[192,128]{1,0:T(8,128)(2,1)}) custom-call(bf16[192,2048]{1,0:T(8,128)(2,1)} %reduce-scatter.2.cloned.1.call-done.gate_up_ref, bf16[192,1024]{1,0:T(8,128)(2,1)} %get-tuple-element.59.own_ref, ...), custom_call_target="tpu_custom_call" | custom-call | flops 3932160 | bytes 2359296 | tf_op jit(solution)/shard_map/pallas_call | solution.py:573
  138.7 2.7 %collective-permute-start.5 = (bf16[96,2048]{1,0:T(8,128)(2,1)}, bf16[96,2048]{1,0:T(8,128)(2,1)S(1)}, u32[]{:S(2)}, u32[]{:S(2)}) collective-permute-start(bf16[96,2048]{1,0:T(8,128)(2,1)} %get-tuple-element.74.refs_1_), channel_id=1, source_target_pairs={{0,3},{1,0},{2,1},{3,2},{4,7},{5,4},{6,5},{7,6},{8,11},{9,8},{10,9... | collective-permute-start | bytes 1179656 | tf_op jit(solution)/shard_map/ppermute | solution.py:517
  141.5 1.4 collective-permute-start.8
  142.9 7.9 %shard_map.118.refs_6_ = bf16[1024,1280]{1,0:T(8,128)(2,1)} custom-call(bf16[96,2048]{1,0:T(8,128)(2,1)} %get-tuple-element.73.refs_0_, bf16[96,2048]{1,0:T(8,128)(2,1)} %get-tuple-element.74.refs_1_, bf16[1664,1024]{1,0:T(8,128)(2,1)} %bitcast.31, bf16[1664,1024]{1,0:T(8,128)(2,1)} %bitcast.35, bf16[192,128]{1,0:T(8,128)(2,1)} %get-tuple-element.64.refs_4_), custom_call_target="tpu_custom_call" | custom-call | flops 1308622848 | bytes 8257536 | tf_op jit(solution)/shard_map/pallas_call | solution.py:593
  150.9 2.7 %collective-permute-start.7 = (bf16[96,2048]{1,0:T(8,128)(2,1)S(1)}, bf16[96,2048]{1,0:T(8,128)(2,1)S(1)}, u32[]{:S(2)}, u32[]{:S(2)}) collective-permute-start(bf16[96,2048]{1,0:T(8,128)(2,1)S(1)} %collective-permute-done.5.refs_3_.refs_5_), channel_id=1, source_target_pairs={{0,3},{1,0},{2,1},{3,2},{4,7},{5,4},{6,5},{7,6},{8,11},{9,8},{10,9... | collective-permute-start | bytes 1179656 | tf_op jit(solution)/shard_map/ppermute | solution.py:517
  153.6 2.2 collective-permute-done.9.refs_2_.refs_4_
  156.7 8.0 %shard_map.119.refs_4_ = bf16[1024,1280]{1,0:T(8,128)(2,1)} custom-call(bf16[96,2048]{1,0:T(8,128)(2,1)S(1)} %collective-permute-done.4.refs_0_.refs_2_, bf16[96,2048]{1,0:T(8,128)(2,1)S(1)} %collective-permute-done.8.refs_1_.refs_3_, bf16[96,2048]{1,0:T(8,128)(2,1)S(1)} %collective-permute-done.9.refs_2_.refs_4_, ...), custom_call_target="tpu_custom_call", output_to_operand_aliasing={{}: (6, {})} | custom-call | flops 2617245696 | bytes 9699328 | tf_op jit(solution)/shard_map/pallas_call | solution.py:593
  165.1 6.5 %shard_map.120 = bf16[1024,1280]{1,0:T(8,128)(2,1)} custom-call(bf16[96,2048]{1,0:T(8,128)(2,1)S(1)} %collective-permute-done.6.refs_0_.refs_6_, bf16[96,2048]{1,0:T(8,128)(2,1)S(1)} %collective-permute-done.7.refs_1_.refs_7_, bf16[1664,1024]{1,0:T(8,128)(2,1)} %bitcast.33, bf16[1664,1024]{1,0:T(8,128)(2,1)} %bitcast.37, ...), custom_call_target="tpu_custom_call", output_to_operand_aliasing={{}: (4, {})} | custom-call | flops 1308622848 | bytes 8257536 | tf_op jit(solution)/shard_map/pallas_call | solution.py:593
  171.6 12.8 %all-to-all-start.2 = ((bf16[128,8,1280]{2,1,0:T(8,128)(2,1)}), bf16[128,8,1280]{2,1,0:T(8,128)(2,1)S(1)}, u32[]{:S(2)}, u32[]{:S(2)}) async-start(bf16[128,8,1280]{2,1,0:T(8,128)(2,1)} %bitcast.29), calls=%async_computation.3 | async-start | bytes 5242880 | tf_op jit(solution)/shard_map/all_to_all | solution.py:487
  185.4 1.0 copy-done.3
  188.4 1.3 shard_map.122
  190.4 4.2 %fusion.1 = bf16[1,1664,1024]{2,1,0:T(8,128)(2,1)} fusion(bf16[768,1664]{1,0:T(8,128)(2,1)S(1)} %copy-done.12, bf16[768,2048]{1,0:T(8,128)(2,1)S(1)} %shard_map.122), kind=kOutput, calls=%fused_computation.4 | convolution fusion | flops 2618949632 | bytes 7536640 | tf_op jit(solution)/shard_map/dot_general | solution.py:636
  194.6 4.3 %fusion = bf16[1,1664,1024]{2,1,0:T(8,128)(2,1)} fusion(bf16[768,1664]{1,0:T(8,128)(2,1)S(1)} %copy-done.12, bf16[768,2048]{1,0:T(8,128)(2,1)S(1)} %shard_map.122), kind=kOutput, calls=%fused_computation.3 | convolution fusion | flops 2618949632 | bytes 7536640 | tf_op jit(solution)/shard_map/dot_general | solution.py:636
  198.9 7.1 %fusion.2 = bf16[1,1024,1664]{2,1,0:T(8,128)(2,1)} fusion(bf16[768,1024]{1,0:T(8,128)(2,1)} %all-gather.2.cloned.1.call-done, bf16[768,1664]{1,0:T(8,128)(2,1)} %get-tuple-element.83), kind=kOutput, calls=%fused_computation.5 | convolution fusion | flops 2618949632 | bytes 7536640 | tf_op jit(solution)/shard_map/dot_general | solution.py:636
  206.0 14.5 %all-to-all-done.2 = bf16[128,8,1280]{2,1,0:T(8,128)(2,1)S(1)} async-done(((bf16[128,8,1280]{2,1,0:T(8,128)(2,1)}), bf16[128,8,1280]{2,1,0:T(8,128)(2,1)S(1)}, u32[]{:S(2)}, u32[]{:S(2)}) %all-to-all-start.2) | async-done | bytes 2621472 | tf_op jit(solution)/shard_map/all_to_all | solution.py:487
  220.5 2.3 %shard_map.121 = (bf16[128,6656]{1,0:T(8,128)(2,1)}, bf16[8,128]{1,0:T(8,128)(2,1)}) custom-call(s32[8,128]{1,0:T(8,128)S(1)} %bitcast.28, bf16[3,256,256]{2,1,0:T(8,128)(2,1)S(1)} %copy-done.8, bf16[4,128,256]{2,1,0:T(8,128)(2,1)S(1)} %copy-done.9, bf16[1024,1280]{1,0:T(8,128)(2,1)S(1)} %bitcast.25), custom_call_target="tpu_custom_call" | custom-call | flops 671088640 | bytes 4325376 | tf_op jit(solution)/shard_map/pallas_call | solution.py:641
  (42 shorter events, 5.6 us)
Async XLA Ops:
  12.0 47.6 %all-to-all-start = ((bf16[128,8,1280]{2,1,0:T(8,128)(2,1)}), bf16[128,8,1280]{2,1,0:T(8,128)(2,1)S(1)}, u32[]{:S(2)}, u32[]{:S(2)}) async-start(bf16[128,8,1280]{2,1,0:T(8,128)(2,1)} %bitcast.43), calls=%async_computation | async-start | bytes 5242880 | tf_op jit(solution)/shard_map/all_to_all | solution.py:487
  59.6 1.5 copy-start.11
  61.1 46.5 %all-to-all-start.1 = ((bf16[128,8,1280]{2,1,0:T(8,128)(2,1)}), bf16[128,8,1280]{2,1,0:T(8,128)(2,1)S(1)}, u32[]{:S(2)}, u32[]{:S(2)}) async-start(bf16[128,8,1280]{2,1,0:T(8,128)(2,1)} %bitcast.41), calls=%async_computation.2 | async-start | bytes 5242880 | tf_op jit(solution)/shard_map/all_to_all | solution.py:487
  65.6 70.3 %reduce-scatter.2.cloned.1.call-start = ((), (), s32[]{:S(2)}) async-start(), calls=%async_computation.4 | async-start | bytes 3932160 | tf_op jit(solution)/shard_map/reduce_scatter | solution.py:510
  77.1 121.8 %all-gather.2.cloned.1.call-start = ((), (), s32[]{:S(2)}) async-start(), calls=%async_computation.5 | async-start | bytes 1966080 | tf_op jit(solution)/shard_map/all_gather | solution.py:622
  111.5 11.8 %collective-permute-start = (bf16[96,1024]{1,0:T(8,128)(2,1)S(1)}, bf16[96,1024]{1,0:T(8,128)(2,1)S(1)}, u32[]{:S(2)}, u32[]{:S(2)}) collective-permute-start(bf16[96,1024]{1,0:T(8,128)(2,1)S(1)} %get-tuple-element.55), channel_id=1, source_target_pairs={{0,1},{1,2},{2,3},{3,0},{4,5},{5,6},{6,7},{7,4},{8,9},{9,10},{10,1... | collective-permute-start | bytes 589832 | tf_op jit(solution)/shard_map/ppermute | solution.py:517
  111.9 11.4 %collective-permute-start.1 = (bf16[96,1024]{1,0:T(8,128)(2,1)S(1)}, bf16[96,1024]{1,0:T(8,128)(2,1)S(1)}, u32[]{:S(2)}, u32[]{:S(2)}) collective-permute-start(bf16[96,1024]{1,0:T(8,128)(2,1)S(1)} %get-tuple-element.56), channel_id=1, source_target_pairs={{0,3},{1,0},{2,1},{3,2},{4,7},{5,4},{6,5},{7,6},{8,11},{9,8},{10,9... | collective-permute-start | bytes 589832 | tf_op jit(solution)/shard_map/ppermute | solution.py:517
  123.4 9.3 %collective-permute-start.3 = (bf16[192,1024]{1,0:T(8,128)(2,1)S(1)}, bf16[192,1024]{1,0:T(8,128)(2,1)S(1)}, u32[]{:S(2)}, u32[]{:S(2)}) collective-permute-start(bf16[192,1024]{1,0:T(8,128)(2,1)S(1)} %get-tuple-element.60), channel_id=1, source_target_pairs={{0,3},{1,0},{2,1},{3,2},{4,7},{5,4},{6,5},{7,6},{8,11},{9,8},{10,9... | collective-permute-start | bytes 1179656 | tf_op jit(solution)/shard_map/ppermute | solution.py:517
  125.6 10.2 %collective-permute-start.2 = (bf16[192,1024]{1,0:T(8,128)(2,1)S(1)}, bf16[192,1024]{1,0:T(8,128)(2,1)S(1)}, u32[]{:S(2)}, u32[]{:S(2)}) collective-permute-start(bf16[192,1024]{1,0:T(8,128)(2,1)S(1)} %get-tuple-element.57), channel_id=1, source_target_pairs={{0,1},{1,2},{2,3},{3,0},{4,5},{5,6},{6,7},{7,4},{8,9},{9,10},{10,1... | collective-permute-start | bytes 1179656 | tf_op jit(solution)/shard_map/ppermute | solution.py:517
  138.7 12.0 %collective-permute-start.4 = (bf16[96,2048]{1,0:T(8,128)(2,1)}, bf16[96,2048]{1,0:T(8,128)(2,1)S(1)}, u32[]{:S(2)}, u32[]{:S(2)}) collective-permute-start(bf16[96,2048]{1,0:T(8,128)(2,1)} %get-tuple-element.73.refs_0_), channel_id=1, source_target_pairs={{0,1},{1,2},{2,3},{3,0},{4,5},{5,6},{6,7},{7,4},{8,9},{9,10},{10,1... | collective-permute-start | bytes 1179656 | tf_op jit(solution)/shard_map/ppermute | solution.py:517
  138.7 12.0 %collective-permute-start.5 = (bf16[96,2048]{1,0:T(8,128)(2,1)}, bf16[96,2048]{1,0:T(8,128)(2,1)S(1)}, u32[]{:S(2)}, u32[]{:S(2)}) collective-permute-start(bf16[96,2048]{1,0:T(8,128)(2,1)} %get-tuple-element.74.refs_1_), channel_id=1, source_target_pairs={{0,3},{1,0},{2,1},{3,2},{4,7},{5,4},{6,5},{7,6},{8,11},{9,8},{10,9... | collective-permute-start | bytes 1179656 | tf_op jit(solution)/shard_map/ppermute | solution.py:517
  141.4 14.3 %collective-permute-start.9 = (bf16[96,2048]{1,0:T(8,128)(2,1)}, bf16[96,2048]{1,0:T(8,128)(2,1)S(1)}, u32[]{:S(2)}, u32[]{:S(2)}) collective-permute-start(bf16[96,2048]{1,0:T(8,128)(2,1)} %get-tuple-element.73.refs_0_), channel_id=1, source_target_pairs={{0,3},{1,0},{2,1},{3,2},{4,7},{5,4},{6,5},{7,6},{8,11},{9,8},{10,9... | collective-permute-start | bytes 1179656 | tf_op jit(solution)/shard_map/ppermute | solution.py:517
  141.5 15.2 %collective-permute-start.8 = (bf16[96,2048]{1,0:T(8,128)(2,1)}, bf16[96,2048]{1,0:T(8,128)(2,1)S(1)}, u32[]{:S(2)}, u32[]{:S(2)}) collective-permute-start(bf16[96,2048]{1,0:T(8,128)(2,1)} %get-tuple-element.74.refs_1_), channel_id=1, source_target_pairs={{0,1},{1,2},{2,3},{3,0},{4,5},{5,6},{6,7},{7,4},{8,9},{9,10},{10,1... | collective-permute-start | bytes 1179656 | tf_op jit(solution)/shard_map/ppermute | solution.py:517
  150.8 13.9 %copy-start = (bf16[96,2048]{1,0:T(8,128)(2,1)}, bf16[96,2048]{1,0:T(8,128)(2,1)S(1)}, u32[]{:S(2)}) copy-start(bf16[96,2048]{1,0:T(8,128)(2,1)S(1)} %collective-permute-done.4.refs_0_.refs_2_) | copy-start | bytes 1179652
  150.8 13.9 %copy-start.2 = (bf16[96,2048]{1,0:T(8,128)(2,1)}, bf16[96,2048]{1,0:T(8,128)(2,1)S(1)}, u32[]{:S(2)}) copy-start(bf16[96,2048]{1,0:T(8,128)(2,1)S(1)} %collective-permute-done.5.refs_3_.refs_5_) | copy-start | bytes 1179652
  150.8 14.3 %collective-permute-start.6 = (bf16[96,2048]{1,0:T(8,128)(2,1)S(1)}, bf16[96,2048]{1,0:T(8,128)(2,1)S(1)}, u32[]{:S(2)}, u32[]{:S(2)}) collective-permute-start(bf16[96,2048]{1,0:T(8,128)(2,1)S(1)} %collective-permute-done.4.refs_0_.refs_2_), channel_id=1, source_target_pairs={{0,1},{1,2},{2,3},{3,0},{4,5},{5,6},{6,7},{7,4},{8,9},{9,10},{10,1... | collective-permute-start | bytes 1179656 | tf_op jit(solution)/shard_map/ppermute | solution.py:517
  150.9 14.2 %collective-permute-start.7 = (bf16[96,2048]{1,0:T(8,128)(2,1)S(1)}, bf16[96,2048]{1,0:T(8,128)(2,1)S(1)}, u32[]{:S(2)}, u32[]{:S(2)}) collective-permute-start(bf16[96,2048]{1,0:T(8,128)(2,1)S(1)} %collective-permute-done.5.refs_3_.refs_5_), channel_id=1, source_target_pairs={{0,3},{1,0},{2,1},{3,2},{4,7},{5,4},{6,5},{7,6},{8,11},{9,8},{10,9... | collective-permute-start | bytes 1179656 | tf_op jit(solution)/shard_map/ppermute | solution.py:517
  155.7 9.0 %copy-start.4 = (bf16[96,2048]{1,0:T(8,128)(2,1)}, bf16[96,2048]{1,0:T(8,128)(2,1)S(1)}, u32[]{:S(2)}) copy-start(bf16[96,2048]{1,0:T(8,128)(2,1)S(1)} %collective-permute-done.9.refs_2_.refs_4_) | copy-start | bytes 1179652
  156.6 8.1 %copy-start.6 = (bf16[96,2048]{1,0:T(8,128)(2,1)}, bf16[96,2048]{1,0:T(8,128)(2,1)S(1)}, u32[]{:S(2)}) copy-start(bf16[96,2048]{1,0:T(8,128)(2,1)S(1)} %collective-permute-done.8.refs_1_.refs_3_) | copy-start | bytes 1179652
  171.6 48.9 %all-to-all-start.2 = ((bf16[128,8,1280]{2,1,0:T(8,128)(2,1)}), bf16[128,8,1280]{2,1,0:T(8,128)(2,1)S(1)}, u32[]{:S(2)}, u32[]{:S(2)}) async-start(bf16[128,8,1280]{2,1,0:T(8,128)(2,1)} %bitcast.29), calls=%async_computation.3 | async-start | bytes 5242880 | tf_op jit(solution)/shard_map/all_to_all | solution.py:487
  184.4 1.0 copy-start.1
  185.4 1.0 copy-start.3
  186.4 1.0 copy-start.5
  187.4 1.0 copy-start.7
  188.4 2.0 copy-start.12
  198.9 21.6 %copy-start.8 = (bf16[3,256,256]{2,1,0:T(8,128)(2,1)S(1)}, bf16[3,256,256]{2,1,0:T(8,128)(2,1)}, u32[]{:S(2)}) copy-start(bf16[3,256,256]{2,1,0:T(8,128)(2,1)} %get-tuple-element.45.left_ref) | copy-start | bytes 1179652
  198.9 21.6 %copy-start.9 = (bf16[4,128,256]{2,1,0:T(8,128)(2,1)S(1)}, bf16[4,128,256]{2,1,0:T(8,128)(2,1)}, u32[]{:S(2)}) copy-start(bf16[4,128,256]{2,1,0:T(8,128)(2,1)} %get-tuple-element.46.combine_ref) | copy-start | bytes 786436
  198.9 21.6 %copy-start.10 = (s32[128,8]{0,1:T(8,128)S(1)}, s32[128,8]{0,1:T(8,128)}, u32[]{:S(2)}) copy-start(s32[128,8]{0,1:T(8,128)} %param.9) | copy-start | bytes 12292
Sparse Core Ops, SparseCore 0:
  77.2 50.3 reduce-scatter.1
  156.8 31.1 all-gather.1

commit v6 on v5

--- a/solution.py
+++ b/solution.py
@@ -321,7 +321,7 @@
 COLUMN_RUNS = ((WIDE, QUARTER, ()), (0, 2 * TAIL, (0, 1)), (2 * TAIL, WIDE, (2, 3)))
 
 
-def row_grad_kernel(turns, own, *refs):
+def row_grad_kernel(turns, own, held, *refs):
     halves = 2 * len(turns)
     halves_hbm, rest = refs[:halves], refs[halves:]
     gate_hbm, up_hbm, extra_ref, out_hbm, grads_ref, rows_ref, packed_ref, gate_ref, up_ref = rest[:9]
@@ -336,13 +336,13 @@
     pairs = []
     for i, (low, high, _) in enumerate(COLUMN_RUNS):
         run = pl.ds(low, high - low)
-        pair = (
-            pltpu.make_async_copy(gate_hbm.at[run], gate_ref.at[run], gate_sem.at[i]),
-            pltpu.make_async_copy(up_hbm.at[run], up_ref.at[run], up_sem.at[i]),
-        )
+        pair = [pltpu.make_async_copy(gate_hbm.at[run], gate_ref.at[run], gate_sem.at[i])]
+        if not held:
+            pair.append(pltpu.make_async_copy(up_hbm.at[run], up_ref.at[run], up_sem.at[i]))
         start(pair)
         pairs.append(pair)
     finish(grads)
+    up_ref = up_hbm if held else up_ref
     spare = extra_ref[...] if own else None
     sent = []
     for (low, high, groups), pair in zip(COLUMN_RUNS, pairs):
@@ -586,14 +586,15 @@
     below_first, above_second = both_ways(first, second)
     below_second, above_first = both_ways(second, first)
 
-    def row_grad(turns, grads, extra, own_block=False):
+    def row_grad(turns, grads, extra, own_block=False, held=False):
         count = len(grads)
         blocks = len(turns)
         dma = pltpu.SemaphoreType.DMA
         return call(
-            functools.partial(row_grad_kernel, turns, own_block),
+            functools.partial(row_grad_kernel, turns, own_block, held),
             1,
-            [ANY] * (count + 2) + [whole(own_rows, 128) if own_block else ANY],
+            [ANY] * (count + 1)
+            + [NEAR if held else ANY, whole(own_rows, 128) if own_block else ANY],
             [(ANY, ((packed8, WIDE), BF16), far)],
             (
                 pltpu.VMEM((blocks * SLOTS, 2 * hidden), BF16),
@@ -609,7 +610,7 @@
             aliases={} if own_block else {count + 2: 0},
             flops=4 * blocks * own_rows * QUARTER * hidden,
             moved=2 * (2 * QUARTER * hidden + blocks * (ROWS8 * WIDE + own_rows * 2 * hidden)),
-        )(*grads, gate_weight, up_weight, extra)[0]
+        )(*grads, gate_weight, w_up[0] if held else up_weight, extra)[0]
 
     own_halves = (in_hbm(first), in_hbm(second))
     back_send = row_grad((0,), own_halves, in_hbm(slot_own), own_block=True)
@@ -620,7 +621,7 @@
     across_first, across_second, back_send = tie((across_first, across_second, back_send))
     weighted_own, _, _ = tie((weighted_own, below_second, above_first))
     weighted = lax.all_gather(weighted_own, "sp", axis=0, tiled=True)
-    back_send = row_grad((2,), (across_first, across_second), back_send)
+    back_send = row_grad((2,), (across_first, across_second), back_send, held=True)
     back_packed = exchange(back_send)
     (grads_all,) = call(
         assemble_kernel,

time: 230 us -> 230 us (level)
    unnamed x26 -> x28, local copies, waits for them, and re-layouts: 6.1 us -> 6.11 us
  transfers between devices with their start and end apart: 15 -> 15, of which waited for: 9 -> 8; matrix products, arithmetic and copies ran while one was open for 7% -> 7% of each run, Pallas kernels for 24% -> 24%
where the time goes in v6:
time: 230 us
  waiting for transfers between devices  88.3 us (38%)
  Pallas kernels  64.3 us (28%)
  starting transfers between devices  40.9 us (18%)
  matrix products  15.6 us (7%)
  between operations  14.3 us (6%)
  local copies, waits for them, and re-layouts  6.11 us (3%)
    all_to_all x3, waiting for transfers between devices, exchange(): lax.all_to_all(pieced, ('sp', 'ep'), split_axis=0, concat_axis=0, tiled=T...  76 us
    all_to_all x3, starting transfers between devices, exchange(): lax.all_to_all(pieced, ('sp', 'ep'), split_axis=0, concat_axis=0, tiled=T...  29 us
    pallas_call x3, Pallas kernels, row_grad(): call(functools.partial(row_grad_kernel, turns, own_block, held), 1, [ANY]...  22.4 us
    dot_general x3, matrix products, over_rows(): lax.dot_general(a, b, contract_rows, preferred_element_type=F32)  15.6 us
    ppermute x10, waiting for transfers between devices, both_ways(): return (lax.ppermute(up, 'sp', upward), lax.ppermute(down, 'sp', downward))  12.3 us
    ppermute x10, starting transfers between devices, both_ways(): return (lax.ppermute(up, 'sp', upward), lax.ppermute(down, 'sp', downward))  11.8 us
    pallas_call x1, Pallas kernels, on_device(): call(gate_up_kernel, 2, [ANY, ANY, ANY], [(rows_of(some_rows, QUARTER), (...  11.4 us
    unnamed x28, local copies, waits for them, and re-layouts  6.11 us
  transfers between devices with their start and end apart: 15, of which 8 were waited for; matrix products, arithmetic and copies ran while one was open for 7% of the time, Pallas kernels for 24%

profile of v6, /device:TPU:1, one launch (start us, length us, event | category | flops | bytes accessed | tf_op | source)
XLA Modules:
  0.0 229.6 jit_solution(17872469077782857273)
XLA Ops:
  7.2 4.8 %shard_map.110 = (bf16[1024,1280]{1,0:T(8,128)(2,1)}, bf16[3,256,256]{2,1,0:T(8,128)(2,1)}) custom-call(s32[8,128]{1,0:T(8,128)} %bitcast.30, bf16[128,6656]{1,0:T(8,128)(2,1)} %x_ref.2), custom_call_target="tpu_custom_call" | custom-call | flops 671088640 | bytes 4325376 | tf_op jit(solution)/shard_map/pallas_call | solution.py:467
  12.0 11.5 %all-to-all-start = ((bf16[128,8,1280]{2,1,0:T(8,128)(2,1)}), bf16[128,8,1280]{2,1,0:T(8,128)(2,1)S(1)}, u32[]{:S(2)}, u32[]{:S(2)}) async-start(bf16[128,8,1280]{2,1,0:T(8,128)(2,1)} %bitcast.43), calls=%async_computation | async-start | bytes 5242880 | tf_op jit(solution)/shard_map/all_to_all | solution.py:487
  23.5 5.1 %shard_map.111 = (bf16[1024,1280]{1,0:T(8,128)(2,1)}, bf16[4,128,256]{2,1,0:T(8,128)(2,1)}) custom-call(s32[8,128]{1,0:T(8,128)} %bitcast.31, f32[8,128]{1,0:T(8,128)} %bitcast.44, bf16[3,256,256]{2,1,0:T(8,128)(2,1)} %get-tuple-element.45.left_ref, bf16[128,6656]{1,0:T(8,128)(2,1)} %x_ref.3), custom_call_target="tpu_custom_call" | custom-call | flops 671088640 | bytes 4325376 | tf_op jit(solution)/shard_map/pallas_call | solution.py:475
  28.5 31.0 %all-to-all-done = bf16[128,8,1280]{2,1,0:T(8,128)(2,1)S(1)} async-done(((bf16[128,8,1280]{2,1,0:T(8,128)(2,1)}), bf16[128,8,1280]{2,1,0:T(8,128)(2,1)S(1)}, u32[]{:S(2)}, u32[]{:S(2)}) %all-to-all-start) | async-done | bytes 2621472 | tf_op jit(solution)/shard_map/all_to_all | solution.py:487
  59.6 1.5 copy-done.12
  61.1 4.5 %all-to-all-start.1 = ((bf16[128,8,1280]{2,1,0:T(8,128)(2,1)}), bf16[128,8,1280]{2,1,0:T(8,128)(2,1)S(1)}, u32[]{:S(2)}, u32[]{:S(2)}) async-start(bf16[128,8,1280]{2,1,0:T(8,128)(2,1)} %bitcast.41), calls=%async_computation.2 | async-start | bytes 5242880 | tf_op jit(solution)/shard_map/all_to_all | solution.py:487
  65.6 11.4 %shard_map.112 = (bf16[768,1664]{1,0:T(8,128)(2,1)}, bf16[768,2048]{1,0:T(8,128)(2,1)}) custom-call(bf16[1024,1280]{1,0:T(8,128)(2,1)} %bitcast.42, bf16[1664,1024]{1,0:T(8,128)(2,1)} %bitcast.34, bf16[1664,1024]{1,0:T(8,128)(2,1)} %bitcast.22), custom_call_target="tpu_custom_call" | custom-call | flops 5234491392 | bytes 15138816 | tf_op jit(solution)/shard_map/pallas_call | solution.py:498
  77.1 30.4 %all-to-all-done.1 = bf16[128,8,1280]{2,1,0:T(8,128)(2,1)S(1)} async-done(((bf16[128,8,1280]{2,1,0:T(8,128)(2,1)}), bf16[128,8,1280]{2,1,0:T(8,128)(2,1)S(1)}, u32[]{:S(2)}, u32[]{:S(2)}) %all-to-all-start.1) | async-done | bytes 2621472 | tf_op jit(solution)/shard_map/all_to_all | solution.py:487
  107.5 3.9 %shard_map.114 = (bf16[96,1024]{1,0:T(8,128)(2,1)S(1)}, bf16[96,1024]{1,0:T(8,128)(2,1)S(1)}) custom-call(bf16[1024,1280]{1,0:T(8,128)(2,1)S(1)} %bitcast.26, bf16[1024,1664]{1,0:T(8,128)(2,1)} %bitcast.38), custom_call_target="tpu_custom_call" | custom-call | flops 83751862272 | bytes 8585216 | tf_op jit(solution)/shard_map/pallas_call | solution.py:532
  111.9 2.4 %collective-permute-start.1 = (bf16[96,1024]{1,0:T(8,128)(2,1)S(1)}, bf16[96,1024]{1,0:T(8,128)(2,1)S(1)}, u32[]{:S(2)}, u32[]{:S(2)}) collective-permute-start(bf16[96,1024]{1,0:T(8,128)(2,1)S(1)} %get-tuple-element.56), channel_id=1, source_target_pairs={{0,3},{1,0},{2,1},{3,2},{4,7},{5,4},{6,5},{7,6},{8,11},{9,8},{10,9... | collective-permute-start | bytes 589832 | tf_op jit(solution)/shard_map/ppermute | solution.py:517
  114.2 5.2 %shard_map.113 = (bf16[192,1024]{1,0:T(8,128)(2,1)S(1)}, bf16[192,1024]{1,0:T(8,128)(2,1)S(1)}) custom-call(bf16[1024,1280]{1,0:T(8,128)(2,1)S(1)} %bitcast.27, bf16[1024,1664]{1,0:T(8,128)(2,1)} %bitcast.39), custom_call_target="tpu_custom_call" | custom-call | flops 1308622848 | bytes 5505024 | tf_op jit(solution)/shard_map/pallas_call | solution.py:542
  119.4 3.9 %collective-permute-done.first_ref = bf16[96,1024]{1,0:T(8,128)(2,1)S(1)} collective-permute-done((bf16[96,1024]{1,0:T(8,128)(2,1)S(1)}, bf16[96,1024]{1,0:T(8,128)(2,1)S(1)}, u32[]{:S(2)}, u32[]{:S(2)}) %collective-permute-start) | collective-permute-done | bytes 196640 | tf_op jit(solution)/shard_map/ppermute | solution.py:517
  123.4 2.2 collective-permute-start.3
  125.6 4.9 %shard_map.116 = (bf16[768,1664]{1,0:T(8,128)(2,1)}, bf16[192,1024]{1,0:T(8,128)(2,1)}, bf16[192,128]{1,0:T(8,128)(2,1)}) custom-call(bf16[1024,1280]{1,0:T(8,128)(2,1)S(1)} %bitcast.28, bf16[1024,1664]{1,0:T(8,128)(2,1)} %bitcast.40), custom_call_target="tpu_custom_call" | custom-call | flops 654311424 | bytes 8978432 | tf_op jit(solution)/shard_map/pallas_call | solution.py:560
  130.5 2.2 collective-permute-done.3.right_ref
  132.7 3.1 %collective-permute-done.2.left_ref = bf16[192,1024]{1,0:T(8,128)(2,1)S(1)} collective-permute-done((bf16[192,1024]{1,0:T(8,128)(2,1)S(1)}, bf16[192,1024]{1,0:T(8,128)(2,1)S(1)}, u32[]{:S(2)}, u32[]{:S(2)}) %collective-permute-start.2) | collective-permute-done | bytes 393248 | tf_op jit(solution)/shard_map/ppermute | solution.py:517
  135.8 2.9 %shard_map.117 = (bf16[96,2048]{1,0:T(8,128)(2,1)}, bf16[96,2048]{1,0:T(8,128)(2,1)}, bf16[192,1024]{1,0:T(8,128)(2,1)}, bf16[192,128]{1,0:T(8,128)(2,1)}) custom-call(bf16[192,2048]{1,0:T(8,128)(2,1)} %reduce-scatter.2.cloned.1.call-done.gate_up_ref, bf16[192,1024]{1,0:T(8,128)(2,1)} %get-tuple-element.59.own_ref, ...), custom_call_target="tpu_custom_call" | custom-call | flops 3932160 | bytes 2359296 | tf_op jit(solution)/shard_map/pallas_call | solution.py:573
  138.8 2.7 %collective-permute-start.5 = (bf16[96,2048]{1,0:T(8,128)(2,1)}, bf16[96,2048]{1,0:T(8,128)(2,1)S(1)}, u32[]{:S(2)}, u32[]{:S(2)}) collective-permute-start(bf16[96,2048]{1,0:T(8,128)(2,1)} %get-tuple-element.74.refs_1_), channel_id=1, source_target_pairs={{0,3},{1,0},{2,1},{3,2},{4,7},{5,4},{6,5},{7,6},{8,11},{9,8},{10,9... | collective-permute-start | bytes 1179656 | tf_op jit(solution)/shard_map/ppermute | solution.py:517
  141.5 1.4 collective-permute-start.8
  142.9 7.8 %shard_map.118.refs_6_ = bf16[1024,1280]{1,0:T(8,128)(2,1)} custom-call(bf16[96,2048]{1,0:T(8,128)(2,1)} %get-tuple-element.73.refs_0_, bf16[96,2048]{1,0:T(8,128)(2,1)} %get-tuple-element.74.refs_1_, bf16[1664,1024]{1,0:T(8,128)(2,1)} %bitcast.35, bf16[1664,1024]{1,0:T(8,128)(2,1)} %bitcast.23, bf16[192,128]{1,0:T(8,128)(2,1)} %get-tuple-element.64.refs_4_), custom_call_target="tpu_custom_call" | custom-call | flops 1308622848 | bytes 8257536 | tf_op jit(solution)/shard_map/pallas_call | solution.py:593
  150.9 2.7 %collective-permute-start.7 = (bf16[96,2048]{1,0:T(8,128)(2,1)S(1)}, bf16[96,2048]{1,0:T(8,128)(2,1)S(1)}, u32[]{:S(2)}, u32[]{:S(2)}) collective-permute-start(bf16[96,2048]{1,0:T(8,128)(2,1)S(1)} %collective-permute-done.5.refs_3_.refs_5_), channel_id=1, source_target_pairs={{0,3},{1,0},{2,1},{3,2},{4,7},{5,4},{6,5},{7,6},{8,11},{9,8},{10,9... | collective-permute-start | bytes 1179656 | tf_op jit(solution)/shard_map/ppermute | solution.py:517
  153.5 2.2 collective-permute-done.9.refs_2_.refs_4_
  156.7 8.6 %shard_map.119.refs_4_ = bf16[1024,1280]{1,0:T(8,128)(2,1)} custom-call(bf16[96,2048]{1,0:T(8,128)(2,1)S(1)} %collective-permute-done.4.refs_0_.refs_2_, bf16[96,2048]{1,0:T(8,128)(2,1)S(1)} %collective-permute-done.8.refs_1_.refs_3_, bf16[96,2048]{1,0:T(8,128)(2,1)S(1)} %collective-permute-done.9.refs_2_.refs_4_, ...), custom_call_target="tpu_custom_call", output_to_operand_aliasing={{}: (6, {})} | custom-call | flops 2617245696 | bytes 9699328 | tf_op jit(solution)/shard_map/pallas_call | solution.py:593
  165.3 6.0 %shard_map.120 = bf16[1024,1280]{1,0:T(8,128)(2,1)} custom-call(bf16[96,2048]{1,0:T(8,128)(2,1)S(1)} %collective-permute-done.6.refs_0_.refs_6_, bf16[96,2048]{1,0:T(8,128)(2,1)S(1)} %collective-permute-done.7.refs_1_.refs_7_, bf16[1664,1024]{1,0:T(8,128)(2,1)} %bitcast.37, bf16[1664,1024]{1,0:T(8,128)(2,1)S(1)} %bitcast.25, ...), custom_call_target="tpu_custom_call", output_to_operand_aliasing={{}: (4, {})} | custom-call | flops 1308622848 | bytes 8257536 | tf_op jit(solution)/shard_map/pallas_call | solution.py:593
  171.3 13.0 %all-to-all-start.2 = ((bf16[128,8,1280]{2,1,0:T(8,128)(2,1)}), bf16[128,8,1280]{2,1,0:T(8,128)(2,1)S(1)}, u32[]{:S(2)}, u32[]{:S(2)}) async-start(bf16[128,8,1280]{2,1,0:T(8,128)(2,1)} %bitcast.33), calls=%async_computation.3 | async-start | bytes 5242880 | tf_op jit(solution)/shard_map/all_to_all | solution.py:487
  186.3 1.0 copy-done.6
  188.3 1.3 shard_map.122
  190.3 4.2 %fusion.1 = bf16[1,1664,1024]{2,1,0:T(8,128)(2,1)} fusion(bf16[768,1664]{1,0:T(8,128)(2,1)S(1)} %copy-done.13, bf16[768,2048]{1,0:T(8,128)(2,1)S(1)} %shard_map.122), kind=kOutput, calls=%fused_computation.4 | convolution fusion | flops 2618949632 | bytes 7536640 | tf_op jit(solution)/shard_map/dot_general | solution.py:637
  194.5 4.3 %fusion = bf16[1,1664,1024]{2,1,0:T(8,128)(2,1)} fusion(bf16[768,1664]{1,0:T(8,128)(2,1)S(1)} %copy-done.13, bf16[768,2048]{1,0:T(8,128)(2,1)S(1)} %shard_map.122), kind=kOutput, calls=%fused_computation.3 | convolution fusion | flops 2618949632 | bytes 7536640 | tf_op jit(solution)/shard_map/dot_general | solution.py:637
  198.8 7.1 %fusion.2 = bf16[1,1024,1664]{2,1,0:T(8,128)(2,1)} fusion(bf16[768,1024]{1,0:T(8,128)(2,1)} %all-gather.2.cloned.1.call-done, bf16[768,1664]{1,0:T(8,128)(2,1)} %get-tuple-element.83), kind=kOutput, calls=%fused_computation.5 | convolution fusion | flops 2618949632 | bytes 7536640 | tf_op jit(solution)/shard_map/dot_general | solution.py:637
  205.9 14.5 %all-to-all-done.2 = bf16[128,8,1280]{2,1,0:T(8,128)(2,1)S(1)} async-done(((bf16[128,8,1280]{2,1,0:T(8,128)(2,1)}), bf16[128,8,1280]{2,1,0:T(8,128)(2,1)S(1)}, u32[]{:S(2)}, u32[]{:S(2)}) %all-to-all-start.2) | async-done | bytes 2621472 | tf_op jit(solution)/shard_map/all_to_all | solution.py:487
  220.4 2.3 %shard_map.121 = (bf16[128,6656]{1,0:T(8,128)(2,1)}, bf16[8,128]{1,0:T(8,128)(2,1)}) custom-call(s32[8,128]{1,0:T(8,128)S(1)} %bitcast.32, bf16[3,256,256]{2,1,0:T(8,128)(2,1)S(1)} %copy-done.9, bf16[4,128,256]{2,1,0:T(8,128)(2,1)S(1)} %copy-done.10, bf16[1024,1280]{1,0:T(8,128)(2,1)S(1)} %bitcast.29), custom_call_target="tpu_custom_call" | custom-call | flops 671088640 | bytes 4325376 | tf_op jit(solution)/shard_map/pallas_call | solution.py:642
  (44 shorter events, 5.3 us)
Async XLA Ops:
  12.0 47.6 %all-to-all-start = ((bf16[128,8,1280]{2,1,0:T(8,128)(2,1)}), bf16[128,8,1280]{2,1,0:T(8,128)(2,1)S(1)}, u32[]{:S(2)}, u32[]{:S(2)}) async-start(bf16[128,8,1280]{2,1,0:T(8,128)(2,1)} %bitcast.43), calls=%async_computation | async-start | bytes 5242880 | tf_op jit(solution)/shard_map/all_to_all | solution.py:487
  59.6 1.5 copy-start.12
  61.1 46.5 %all-to-all-start.1 = ((bf16[128,8,1280]{2,1,0:T(8,128)(2,1)}), bf16[128,8,1280]{2,1,0:T(8,128)(2,1)S(1)}, u32[]{:S(2)}, u32[]{:S(2)}) async-start(bf16[128,8,1280]{2,1,0:T(8,128)(2,1)} %bitcast.41), calls=%async_computation.2 | async-start | bytes 5242880 | tf_op jit(solution)/shard_map/all_to_all | solution.py:487
  65.6 70.3 %reduce-scatter.2.cloned.1.call-start = ((), (), s32[]{:S(2)}) async-start(), calls=%async_computation.4 | async-start | bytes 3932160 | tf_op jit(solution)/shard_map/reduce_scatter | solution.py:510
  77.1 121.7 %all-gather.2.cloned.1.call-start = ((), (), s32[]{:S(2)}) async-start(), calls=%async_computation.5 | async-start | bytes 1966080 | tf_op jit(solution)/shard_map/all_gather | solution.py:623
  111.5 11.8 %collective-permute-start = (bf16[96,1024]{1,0:T(8,128)(2,1)S(1)}, bf16[96,1024]{1,0:T(8,128)(2,1)S(1)}, u32[]{:S(2)}, u32[]{:S(2)}) collective-permute-start(bf16[96,1024]{1,0:T(8,128)(2,1)S(1)} %get-tuple-element.55), channel_id=1, source_target_pairs={{0,1},{1,2},{2,3},{3,0},{4,5},{5,6},{6,7},{7,4},{8,9},{9,10},{10,1... | collective-permute-start | bytes 589832 | tf_op jit(solution)/shard_map/ppermute | solution.py:517
  111.9 11.4 %collective-permute-start.1 = (bf16[96,1024]{1,0:T(8,128)(2,1)S(1)}, bf16[96,1024]{1,0:T(8,128)(2,1)S(1)}, u32[]{:S(2)}, u32[]{:S(2)}) collective-permute-start(bf16[96,1024]{1,0:T(8,128)(2,1)S(1)} %get-tuple-element.56), channel_id=1, source_target_pairs={{0,3},{1,0},{2,1},{3,2},{4,7},{5,4},{6,5},{7,6},{8,11},{9,8},{10,9... | collective-permute-start | bytes 589832 | tf_op jit(solution)/shard_map/ppermute | solution.py:517
  123.4 9.3 %collective-permute-start.3 = (bf16[192,1024]{1,0:T(8,128)(2,1)S(1)}, bf16[192,1024]{1,0:T(8,128)(2,1)S(1)}, u32[]{:S(2)}, u32[]{:S(2)}) collective-permute-start(bf16[192,1024]{1,0:T(8,128)(2,1)S(1)} %get-tuple-element.60), channel_id=1, source_target_pairs={{0,3},{1,0},{2,1},{3,2},{4,7},{5,4},{6,5},{7,6},{8,11},{9,8},{10,9... | collective-permute-start | bytes 1179656 | tf_op jit(solution)/shard_map/ppermute | solution.py:517
  125.6 10.2 %collective-permute-start.2 = (bf16[192,1024]{1,0:T(8,128)(2,1)S(1)}, bf16[192,1024]{1,0:T(8,128)(2,1)S(1)}, u32[]{:S(2)}, u32[]{:S(2)}) collective-permute-start(bf16[192,1024]{1,0:T(8,128)(2,1)S(1)} %get-tuple-element.57), channel_id=1, source_target_pairs={{0,1},{1,2},{2,3},{3,0},{4,5},{5,6},{6,7},{7,4},{8,9},{9,10},{10,1... | collective-permute-start | bytes 1179656 | tf_op jit(solution)/shard_map/ppermute | solution.py:517
  138.7 12.0 %collective-permute-start.4 = (bf16[96,2048]{1,0:T(8,128)(2,1)}, bf16[96,2048]{1,0:T(8,128)(2,1)S(1)}, u32[]{:S(2)}, u32[]{:S(2)}) collective-permute-start(bf16[96,2048]{1,0:T(8,128)(2,1)} %get-tuple-element.73.refs_0_), channel_id=1, source_target_pairs={{0,1},{1,2},{2,3},{3,0},{4,5},{5,6},{6,7},{7,4},{8,9},{9,10},{10,1... | collective-permute-start | bytes 1179656 | tf_op jit(solution)/shard_map/ppermute | solution.py:517
  138.8 12.0 %collective-permute-start.5 = (bf16[96,2048]{1,0:T(8,128)(2,1)}, bf16[96,2048]{1,0:T(8,128)(2,1)S(1)}, u32[]{:S(2)}, u32[]{:S(2)}) collective-permute-start(bf16[96,2048]{1,0:T(8,128)(2,1)} %get-tuple-element.74.refs_1_), channel_id=1, source_target_pairs={{0,3},{1,0},{2,1},{3,2},{4,7},{5,4},{6,5},{7,6},{8,11},{9,8},{10,9... | collective-permute-start | bytes 1179656 | tf_op jit(solution)/shard_map/ppermute | solution.py:517
  141.4 14.3 %collective-permute-start.9 = (bf16[96,2048]{1,0:T(8,128)(2,1)}, bf16[96,2048]{1,0:T(8,128)(2,1)S(1)}, u32[]{:S(2)}, u32[]{:S(2)}) collective-permute-start(bf16[96,2048]{1,0:T(8,128)(2,1)} %get-tuple-element.73.refs_0_), channel_id=1, source_target_pairs={{0,3},{1,0},{2,1},{3,2},{4,7},{5,4},{6,5},{7,6},{8,11},{9,8},{10,9... | collective-permute-start | bytes 1179656 | tf_op jit(solution)/shard_map/ppermute | solution.py:517
  141.5 15.2 %collective-permute-start.8 = (bf16[96,2048]{1,0:T(8,128)(2,1)}, bf16[96,2048]{1,0:T(8,128)(2,1)S(1)}, u32[]{:S(2)}, u32[]{:S(2)}) collective-permute-start(bf16[96,2048]{1,0:T(8,128)(2,1)} %get-tuple-element.74.refs_1_), channel_id=1, source_target_pairs={{0,1},{1,2},{2,3},{3,0},{4,5},{5,6},{6,7},{7,4},{8,9},{9,10},{10,1... | collective-permute-start | bytes 1179656 | tf_op jit(solution)/shard_map/ppermute | solution.py:517
  150.8 14.5 %copy-start.1 = (bf16[96,2048]{1,0:T(8,128)(2,1)}, bf16[96,2048]{1,0:T(8,128)(2,1)S(1)}, u32[]{:S(2)}) copy-start(bf16[96,2048]{1,0:T(8,128)(2,1)S(1)} %collective-permute-done.4.refs_0_.refs_2_) | copy-start | bytes 1179652
  150.8 14.5 %copy-start.3 = (bf16[96,2048]{1,0:T(8,128)(2,1)}, bf16[96,2048]{1,0:T(8,128)(2,1)S(1)}, u32[]{:S(2)}) copy-start(bf16[96,2048]{1,0:T(8,128)(2,1)S(1)} %collective-permute-done.5.refs_3_.refs_5_) | copy-start | bytes 1179652
  150.8 14.5 %collective-permute-start.6 = (bf16[96,2048]{1,0:T(8,128)(2,1)S(1)}, bf16[96,2048]{1,0:T(8,128)(2,1)S(1)}, u32[]{:S(2)}, u32[]{:S(2)}) collective-permute-start(bf16[96,2048]{1,0:T(8,128)(2,1)S(1)} %collective-permute-done.4.refs_0_.refs_2_), channel_id=1, source_target_pairs={{0,1},{1,2},{2,3},{3,0},{4,5},{5,6},{6,7},{7,4},{8,9},{9,10},{10,1... | collective-permute-start | bytes 1179656 | tf_op jit(solution)/shard_map/ppermute | solution.py:517
  150.9 14.4 %collective-permute-start.7 = (bf16[96,2048]{1,0:T(8,128)(2,1)S(1)}, bf16[96,2048]{1,0:T(8,128)(2,1)S(1)}, u32[]{:S(2)}, u32[]{:S(2)}) collective-permute-start(bf16[96,2048]{1,0:T(8,128)(2,1)S(1)} %collective-permute-done.5.refs_3_.refs_5_), channel_id=1, source_target_pairs={{0,3},{1,0},{2,1},{3,2},{4,7},{5,4},{6,5},{7,6},{8,11},{9,8},{10,9... | collective-permute-start | bytes 1179656 | tf_op jit(solution)/shard_map/ppermute | solution.py:517
  155.7 9.5 %copy-start.5 = (bf16[96,2048]{1,0:T(8,128)(2,1)}, bf16[96,2048]{1,0:T(8,128)(2,1)S(1)}, u32[]{:S(2)}) copy-start(bf16[96,2048]{1,0:T(8,128)(2,1)S(1)} %collective-permute-done.9.refs_2_.refs_4_) | copy-start | bytes 1179652
  156.7 8.6 %copy-start.7 = (bf16[96,2048]{1,0:T(8,128)(2,1)}, bf16[96,2048]{1,0:T(8,128)(2,1)S(1)}, u32[]{:S(2)}) copy-start(bf16[96,2048]{1,0:T(8,128)(2,1)S(1)} %collective-permute-done.8.refs_1_.refs_3_) | copy-start | bytes 1179652
  156.7 8.6 %copy-start = (bf16[1,1664,1024]{2,1,0:T(8,128)(2,1)S(1)}, bf16[1,1664,1024]{2,1,0:T(8,128)(2,1)}, u32[]{:S(2)}) copy-start(bf16[1,1664,1024]{2,1,0:T(8,128)(2,1)} %param.12) | copy-start | bytes 10223620
  171.3 49.1 %all-to-all-start.2 = ((bf16[128,8,1280]{2,1,0:T(8,128)(2,1)}), bf16[128,8,1280]{2,1,0:T(8,128)(2,1)S(1)}, u32[]{:S(2)}, u32[]{:S(2)}) async-start(bf16[128,8,1280]{2,1,0:T(8,128)(2,1)} %bitcast.33), calls=%async_computation.3 | async-start | bytes 5242880 | tf_op jit(solution)/shard_map/all_to_all | solution.py:487
  184.3 1.0 copy-start.2
  185.3 1.0 copy-start.4
  186.3 1.0 copy-start.6
  187.3 1.0 copy-start.8
  188.3 2.0 copy-start.13
  198.8 21.6 %copy-start.9 = (bf16[3,256,256]{2,1,0:T(8,128)(2,1)S(1)}, bf16[3,256,256]{2,1,0:T(8,128)(2,1)}, u32[]{:S(2)}) copy-start(bf16[3,256,256]{2,1,0:T(8,128)(2,1)} %get-tuple-element.45.left_ref) | copy-start | bytes 1179652
  198.8 21.6 %copy-start.10 = (bf16[4,128,256]{2,1,0:T(8,128)(2,1)S(1)}, bf16[4,128,256]{2,1,0:T(8,128)(2,1)}, u32[]{:S(2)}) copy-start(bf16[4,128,256]{2,1,0:T(8,128)(2,1)} %get-tuple-element.46.combine_ref) | copy-start | bytes 786436
  198.8 21.6 %copy-start.11 = (s32[128,8]{0,1:T(8,128)S(1)}, s32[128,8]{0,1:T(8,128)}, u32[]{:S(2)}) copy-start(s32[128,8]{0,1:T(8,128)} %param.9) | copy-start | bytes 12292
Sparse Core Ops, SparseCore 0:
  77.2 50.3 reduce-scatter.1
  156.8 31.2 all-gather.1
